TPU v7x, 32 devices: a whole 2x2x4 slice. The times are simulated.
32 devices in a mesh: tp: 4 (over y, core), dp: 2 (over x), grp: 4 (over z).
Axes of the slice: x: 2, y: 2, z: 4, core: 2. Of those that a mesh axis runs over, the one named last changes fastest.
Arguments:
- tokens: bfloat16 [16, 1024, 768], P(('dp', 'grp')), may hold values from -6 to 6
- sigma_index: int32 [16], P(('dp', 'grp')), may hold values from 0 to 63
- absorbed: int32 [16, 1024], P(('dp', 'grp')), may hold values 0 or 1
- cotangent: bfloat16 [16, 1024, 768], P(('dp', 'grp')), may hold values from -6 to 6
- time_table: float32 [64, 128], replicated, may hold values from -6 to 6
- in_weight: float32 [768, 7, 768], P('dp', None, 'tp'), may hold values from -0.21875 to 0.21875
- back_weight: float32 [5, 768, 768], P(None, 'tp', 'dp'), may hold values from -1.1547005 to 1.1547005
- ada_weight: float32 [128, 6, 768], P('dp', None, 'tp'), may hold values from -0.25 to 0.25
- small_params: float32 [9, 768], P(None, 'dp'), may hold values from -1.2 to 2.2
- up_bias: float32 [4, 768], P(None, ('tp', 'dp')), may hold values from -3 to 3
- in_first: float32 [4, 768, 7, 768], P('grp', 'dp', None, 'tp'), may hold values from -32 to 32
- back_first: float32 [4, 5, 768, 768], P('grp', None, 'tp', 'dp'), may hold values from -32 to 32
- ada_first: float32 [4, 128, 6, 768], P('grp', 'dp', None, 'tp'), may hold values from -32 to 32
- small_first: float32 [4, 9, 768], P('grp', None, 'dp'), may hold values from -32 to 32
- bias_first: float32 [4, 4, 768], P('grp', None, ('tp', 'dp')), may hold values from -32 to 32
- in_second: float32 [4, 768, 7, 768], P('grp', 'dp', None, 'tp'), may hold values from 1.024 to 16.384
- back_second: float32 [4, 5, 768, 768], P('grp', None, 'tp', 'dp'), may hold values from 1.024 to 16.384
- ada_second: float32 [4, 128, 6, 768], P('grp', 'dp', None, 'tp'), may hold values from 1.024 to 16.384
- small_second: float32 [4, 9, 768], P('grp', None, 'dp'), may hold values from 1.024 to 16.384
- bias_second: float32 [4, 4, 768], P('grp', None, ('tp', 'dp')), may hold values from 1.024 to 16.384
- in_moment: float32 [768, 7, 768], P('dp', None, 'tp'), may hold values from -0.09375 to 0.09375
- back_moment: float32 [5, 768, 768], P(None, 'tp', 'dp'), may hold values from -0.09375 to 0.09375
- ada_moment: float32 [128, 6, 768], P('dp', None, 'tp'), may hold values from -0.09375 to 0.09375
- small_moment: float32 [9, 768], P(None, 'dp'), may hold values from -0.875 to 0.875
- bias_moment: float32 [4, 768], P(None, ('tp', 'dp')), may hold values from -0.875 to 0.875
Outputs:
- block_out: bfloat16 [16, 1024, 768], P(('dp', 'grp'))
- input_grad: float32 [16, 1024, 768], P(('dp', 'grp'))
- in_first_new: float32 [4, 768, 7, 768], P('grp', 'dp', None, 'tp')
- back_first_new: float32 [4, 5, 768, 768], P('grp', None, 'tp', 'dp')
- ada_first_new: float32 [4, 128, 6, 768], P('grp', 'dp', None, 'tp')
- small_first_new: float32 [4, 9, 768], P('grp', None, 'dp')
- bias_first_new: float32 [4, 4, 768], P('grp', None, ('tp', 'dp'))
- in_second_new: float32 [4, 768, 7, 768], P('grp', 'dp', None, 'tp')
- back_second_new: float32 [4, 5, 768, 768], P('grp', None, 'tp', 'dp')
- ada_second_new: float32 [4, 128, 6, 768], P('grp', 'dp', None, 'tp')
- small_second_new: float32 [4, 9, 768], P('grp', None, 'dp')
- bias_second_new: float32 [4, 4, 768], P('grp', None, ('tp', 'dp'))
- in_weight_new: float32 [768, 7, 768], P('dp', None, 'tp')
- back_weight_new: float32 [5, 768, 768], P(None, 'tp', 'dp')
- ada_weight_new: float32 [128, 6, 768], P('dp', None, 'tp')
- small_params_new: float32 [9, 768], P(None, 'dp')
- up_bias_new: float32 [4, 768], P(None, ('tp', 'dp'))
- in_diff: float32 [768, 7, 768], P('dp', None, 'tp')
- back_diff: float32 [5, 768, 768], P(None, 'tp', 'dp')
- ada_diff: float32 [128, 6, 768], P('dp', None, 'tp')
- small_diff: float32 [9, 768], P(None, 'dp')
- bias_diff: float32 [4, 768], P(None, ('tp', 'dp'))
- in_moment_new: float32 [768, 7, 768], P('dp', None, 'tp')
- back_moment_new: float32 [5, 768, 768], P(None, 'tp', 'dp')
- ada_moment_new: float32 [128, 6, 768], P('dp', None, 'tp')
- small_moment_new: float32 [9, 768], P(None, 'dp')
- bias_moment_new: float32 [4, 768], P(None, ('tp', 'dp'))
All inputs are finite; a program needn't handle non-finite values. No bound on the sum of `absorbed` on one device may be relied on, other than what follows from the above.
Results may differ from a plain program's by a relative error of at most 0.018.
Values may be sent and summed in bfloat16 or wider, within the bound.
A program may use at most 192 MiB of HBM per device.

v0:
```python
import jax
import jax.numpy as jnp
from jax import lax
from jax.sharding import PartitionSpec as P

HEAD_DIM = 64
STEP = 10


highest = lax.Precision.HIGHEST
norm_eps = 1e-05
beta_one = 0.9
beta_two = 0.999
adam_eps = 1e-08
decay_rate = 0.1
rate_matrix = 0.03
rate_small = 0.3
outer_mu = 0.9
outer_rate = 0.7


def layer_norm(values, gain_row):
    row_mean = jnp.mean(values, axis=-1, keepdims=True)
    centered = values - row_mean
    variance = jnp.mean(centered * centered, axis=-1, keepdims=True)
    return centered * lax.rsqrt(variance + norm_eps) * gain_row


def modulate(values, gain_row, shift_row, scale_row):
    return layer_norm(values, gain_row) * (1.0 + scale_row) + shift_row


def rotary(values):
    length = values.shape[-3]
    head_size = values.shape[-1]
    half_size = head_size // 2
    frequency = 10000.0 ** (-2.0 * jnp.arange(half_size, dtype=jnp.float32) / head_size)
    angles = jnp.arange(length, dtype=jnp.float32)[:, None] * frequency[None, :]
    cosine = jnp.cos(angles)[:, None, :]
    sine_part = jnp.sin(angles)[:, None, :]
    lower = values[..., :half_size]
    upper = values[..., half_size:]
    return jnp.concatenate(
        [lower * cosine - upper * sine_part, upper * cosine + lower * sine_part], axis=-1
    )


def gelu_tanh(values):
    return (
        0.5
        * values
        * (1.0 + jnp.tanh(0.7978845608028654 * (values + 0.044715 * values * values * values)))
    )


def rotate_pair(query_part, key_part):
    return (rotary(query_part), rotary(key_part))


def adam_step(weight, gradient, first_moment, second_moment, rate, decay):
    first_new = beta_one * first_moment + (1.0 - beta_one) * gradient
    second_new = beta_two * second_moment + (1.0 - beta_two) * gradient * gradient
    first_hat = first_new / (1.0 - beta_one**STEP)
    second_hat = second_new / (1.0 - beta_two**STEP)
    return (
        first_new,
        second_new,
        weight - rate * (first_hat / (jnp.sqrt(second_hat) + adam_eps) + decay * weight),
    )


def on_device(
    tokens,
    sigma_index,
    absorbed,
    cotangent,
    time_table,
    in_weight,
    back_weight,
    ada_weight,
    small_params,
    up_bias,
    in_first,
    back_first,
    ada_first,
    small_first,
    bias_first,
    in_second,
    back_second,
    ada_second,
    small_second,
    bias_second,
    in_moment,
    back_moment,
    ada_moment,
    small_moment,
    bias_moment,
):
    in_matrix, back_matrix, ada_matrix, small_low, bias_low = (
        lax.all_gather(in_weight.astype(jnp.bfloat16), "dp", axis=0, tiled=True),
        lax.all_gather(back_weight.astype(jnp.bfloat16), "dp", axis=2, tiled=True),
        lax.all_gather(ada_weight.astype(jnp.bfloat16), "dp", axis=0, tiled=True),
        lax.all_gather(small_params.astype(jnp.bfloat16), "dp", axis=1, tiled=True),
        lax.all_gather(up_bias.astype(jnp.bfloat16), "dp", axis=1, tiled=True),
    )
    seq_count, length, model_width = tokens.shape
    local_width = in_matrix.shape[2]
    head_count = local_width // HEAD_DIM
    row_block = min(512, length)
    block_count = length // row_block
    head_shape = (seq_count, length, head_count, HEAD_DIM)
    small_rows = small_low.astype(jnp.float32)
    table_ids = jnp.arange(time_table.shape[0], dtype=jnp.int32)
    onehot = (sigma_index[:, None] == table_ids[None, :]).astype(jnp.float32)
    condition = jax.nn.silu(jnp.dot(onehot, time_table, precision=highest))
    cond_low = condition.astype(jnp.bfloat16)
    mod_part = jnp.einsum("sc,cad->sad", cond_low, ada_matrix, preferred_element_type=jnp.float32)
    modulation = lax.all_gather(mod_part, "tp", axis=2, tiled=True) + small_rows[3:9][None]
    token_vals = tokens.astype(jnp.float32)
    hidden_one_f, pull_one = jax.vjp(
        modulate, token_vals, small_rows[0], modulation[:, 0:1], modulation[:, 1:2]
    )
    first_hidden = hidden_one_f.astype(jnp.bfloat16)
    query_key_value_weight = in_matrix[:, 0:3, :]
    projected = jnp.einsum(
        "xgv,vrh->xgrh", first_hidden, query_key_value_weight, preferred_element_type=jnp.float32
    )
    (query_rot, key_rot), pull_rot = jax.vjp(
        rotate_pair, projected[:, :, 0].reshape(head_shape), projected[:, :, 1].reshape(head_shape)
    )
    queries = query_rot.astype(jnp.bfloat16)
    key_rows = key_rot.astype(jnp.bfloat16)
    value_rows = projected[:, :, 2].reshape(head_shape).astype(jnp.bfloat16)

    def forward_block(block_index):
        seq_index = block_index // block_count
        row_start = block_index % block_count * row_block
        query_seq = lax.dynamic_index_in_dim(queries, seq_index, 0, keepdims=False)
        query_rows = lax.dynamic_slice_in_dim(query_seq, row_start, row_block, 0)
        key_seq = lax.dynamic_index_in_dim(key_rows, seq_index, 0, keepdims=False)
        value_seq = lax.dynamic_index_in_dim(value_rows, seq_index, 0, keepdims=False)
        scores = (
            jnp.einsum("rhe,khe->hrk", query_rows, key_seq, preferred_element_type=jnp.float32)
            * 0.125
        )
        row_max = jnp.max(scores, axis=-1, keepdims=True)
        shifted = jnp.exp(scores - row_max)
        row_total = jnp.sum(shifted, axis=-1, keepdims=True)
        attn_probs = (shifted / row_total).astype(jnp.bfloat16)
        mixed_rows = jnp.einsum(
            "hrk,khe->rhe", attn_probs, value_seq, preferred_element_type=jnp.float32
        )
        return (mixed_rows.astype(jnp.bfloat16), row_max[..., 0] + jnp.log(row_total[..., 0]))

    mixed_heads, log_totals = lax.map(
        forward_block, jnp.arange(seq_count * block_count, dtype=jnp.int32)
    )
    mixed_heads = mixed_heads.reshape(seq_count, length, local_width)
    log_totals = log_totals.reshape(seq_count, block_count, head_count, row_block)
    output_weight = back_matrix[0]
    gate_one = modulation[:, 2:3]
    gate_two = modulation[:, 5:6]
    attention_branch = jnp.einsum(
        "wrp,pj->wrj", mixed_heads, output_weight, preferred_element_type=jnp.float32
    )
    attended = lax.psum(attention_branch, "tp")
    after_attn = token_vals + gate_one * attended
    hidden_two_f, pull_two = jax.vjp(
        modulate, after_attn, small_rows[1], modulation[:, 3:4], modulation[:, 4:5]
    )
    second_hidden = hidden_two_f.astype(jnp.bfloat16)
    up_weight = in_matrix[:, 3:7, :].reshape(model_width, 4 * local_width)
    pre_act = jnp.einsum(
        "hjn,np->hjp", second_hidden, up_weight, preferred_element_type=jnp.float32
    ) + bias_low.reshape(4 * local_width).astype(jnp.float32)
    activated_f, pull_act = jax.vjp(gelu_tanh, pre_act)
    activation_values = activated_f.astype(jnp.bfloat16)
    down_weight = back_matrix[1:5].reshape(4 * local_width, model_width)
    feedforward_branch = jnp.einsum(
        "wrp,pj->wrj", activation_values, down_weight, preferred_element_type=jnp.float32
    )
    branch = (
        lax.psum(feedforward_branch.astype(jnp.bfloat16), "tp").astype(jnp.float32) + small_rows[2]
    )
    block_here = (after_attn + gate_two * branch).astype(jnp.bfloat16)
    out_grad = cotangent.astype(jnp.float32) * absorbed.astype(jnp.float32)[:, :, None]
    branch_gradient = (gate_two * out_grad).astype(jnp.bfloat16)
    gate_two_part = jnp.sum(out_grad * branch, axis=1)
    down_bias_grad = jnp.sum(branch_gradient.astype(jnp.float32), axis=(0, 1))
    down_grad = jnp.einsum(
        "kix,kit->xt", activation_values, branch_gradient, preferred_element_type=jnp.float32
    )
    act_grad = jnp.einsum(
        "nmw,pw->nmp", branch_gradient, down_weight, preferred_element_type=jnp.float32
    )
    preactivation_gradient = pull_act(act_grad)[0].astype(jnp.bfloat16)
    up_bias_grad = jnp.sum(preactivation_gradient.astype(jnp.float32), axis=(0, 1)).reshape(
        4, local_width
    )
    up_grad = jnp.einsum(
        "rzi,rzk->ik", second_hidden, preactivation_gradient, preferred_element_type=jnp.float32
    ).reshape(model_width, 4, local_width)
    down_slots = down_grad.reshape(4, local_width, model_width)
    hidden_two_part = jnp.einsum(
        "rnq,tq->rnt", preactivation_gradient, up_weight, preferred_element_type=jnp.float32
    )
    hidden_two_grad = lax.psum(hidden_two_part.astype(jnp.bfloat16), "tp").astype(jnp.float32)
    after_part, gain_two_part, shift_two_part, scale_two_part = pull_two(hidden_two_grad)
    after_here = out_grad + after_part
    gate_one_part = jnp.sum(after_here * attended, axis=1)
    shift_two_grad = shift_two_part[:, 0]
    scale_two_grad = scale_two_part[:, 0]
    attention_gradient = (gate_one * after_here).astype(jnp.bfloat16)
    output_weight_gradient = jnp.einsum(
        "kix,kit->xt", mixed_heads, attention_gradient, preferred_element_type=jnp.float32
    )
    mixed_grad = (
        jnp.einsum(
            "nmw,pw->nmp", attention_gradient, output_weight, preferred_element_type=jnp.float32
        )
        .astype(jnp.bfloat16)
        .reshape(head_shape)
    )

    def backward_sequence(inputs):
        query_seq, key_seq, value_seq, log_seq, grad_seq = inputs
        zero_rows = jnp.zeros(key_seq.shape, jnp.float32)

        def backward_block(totals, block_index):
            key_total, value_total = totals
            row_start = block_index * row_block
            query_rows = lax.dynamic_slice_in_dim(query_seq, row_start, row_block, 0)
            grad_rows = lax.dynamic_slice_in_dim(grad_seq, row_start, row_block, 0)
            log_rows = lax.dynamic_index_in_dim(log_seq, block_index, 0, keepdims=False)
            scores = (
                jnp.einsum("rhe,khe->hrk", query_rows, key_seq, preferred_element_type=jnp.float32)
                * 0.125
            )
            attn_probs = jnp.exp(scores - log_rows[:, :, None])
            value_total = value_total + jnp.einsum(
                "hrk,rhe->khe",
                attn_probs.astype(jnp.bfloat16),
                grad_rows,
                preferred_element_type=jnp.float32,
            )
            prob_grad = jnp.einsum(
                "rhe,khe->hrk", grad_rows, value_seq, preferred_element_type=jnp.float32
            )
            row_delta = jnp.sum(attn_probs * prob_grad, axis=-1, keepdims=True)
            score_grad = (attn_probs * (prob_grad - row_delta)).astype(jnp.bfloat16)
            query_part = (
                jnp.einsum("hrk,khe->rhe", score_grad, key_seq, preferred_element_type=jnp.float32)
                * 0.125
            )
            key_total = (
                key_total
                + jnp.einsum(
                    "hrk,rhe->khe", score_grad, query_rows, preferred_element_type=jnp.float32
                )
                * 0.125
            )
            return ((key_total, value_total), query_part)

        (key_total, value_total), query_parts = lax.scan(
            backward_block, (zero_rows, zero_rows), jnp.arange(block_count, dtype=jnp.int32)
        )
        return (query_parts.reshape(query_seq.shape), key_total, value_total)

    query_grad, key_grad, value_grad = lax.map(
        backward_sequence, (queries, key_rows, value_rows, log_totals, mixed_grad)
    )
    query_raw_grad, key_raw_grad = pull_rot((query_grad, key_grad))
    flat_shape = (seq_count, length, local_width)
    projection_gradient = jnp.stack(
        [
            query_raw_grad.reshape(flat_shape),
            key_raw_grad.reshape(flat_shape),
            value_grad.reshape(flat_shape),
        ],
        axis=2,
    ).astype(jnp.bfloat16)
    qkv_grad = jnp.einsum(
        "vqk,vqgu->kgu", first_hidden, projection_gradient, preferred_element_type=jnp.float32
    )
    hidden_one_grad = lax.psum(
        jnp.einsum(
            "orwg,xwg->orx",
            projection_gradient,
            query_key_value_weight,
            preferred_element_type=jnp.float32,
        ).astype(jnp.bfloat16),
        "tp",
    ).astype(jnp.float32)
    token_part, gain_one_grad, shift_one_grad, scale_one_grad = pull_one(hidden_one_grad)
    input_grad = after_here + token_part
    mod_grad = jnp.stack(
        [
            shift_one_grad[:, 0],
            scale_one_grad[:, 0],
            gate_one_part,
            shift_two_grad,
            scale_two_grad,
            gate_two_part,
        ],
        axis=1,
    )
    small_grad = jnp.concatenate(
        [gain_one_grad[None], gain_two_part[None], down_bias_grad[None], jnp.sum(mod_grad, axis=0)],
        axis=0,
    )
    mod_local = lax.dynamic_slice_in_dim(
        mod_grad, lax.axis_index("tp") * local_width, local_width, 2
    )
    ada_grad = jnp.einsum("sc,sad->cad", cond_low.astype(jnp.float32), mod_local, precision=highest)
    in_full = jnp.concatenate([qkv_grad, up_grad], axis=1)
    back_full = jnp.concatenate([output_weight_gradient[None], down_slots], axis=0)
    in_shard, back_shard, ada_shard, small_shard, bias_shard = (
        lax.psum_scatter(
            in_full.astype(jnp.bfloat16), "dp", scatter_dimension=0, tiled=True
        ).astype(jnp.float32),
        lax.psum_scatter(
            back_full.astype(jnp.bfloat16), "dp", scatter_dimension=2, tiled=True
        ).astype(jnp.float32),
        lax.psum_scatter(
            ada_grad.astype(jnp.bfloat16), "dp", scatter_dimension=0, tiled=True
        ).astype(jnp.float32),
        lax.psum_scatter(
            small_grad.astype(jnp.bfloat16), "dp", scatter_dimension=1, tiled=True
        ).astype(jnp.float32),
        lax.psum_scatter(
            up_bias_grad.astype(jnp.bfloat16), "dp", scatter_dimension=1, tiled=True
        ).astype(jnp.float32),
    )
    in_first_new, in_second_new, in_group = adam_step(
        in_weight, in_shard, in_first[0], in_second[0], rate_matrix, decay_rate
    )
    back_first_new, back_second_new, back_group = adam_step(
        back_weight, back_shard, back_first[0], back_second[0], rate_matrix, decay_rate
    )
    ada_first_new, ada_second_new, ada_group = adam_step(
        ada_weight, ada_shard, ada_first[0], ada_second[0], rate_matrix, decay_rate
    )
    small_first_new, small_second_new, small_group = adam_step(
        small_params, small_shard, small_first[0], small_second[0], rate_small, 0.0
    )
    bias_first_new, bias_second_new, bias_group = adam_step(
        up_bias, bias_shard, bias_first[0], bias_second[0], rate_small, 0.0
    )
    in_total, back_total, ada_total, small_total, bias_total = (
        lax.psum((in_weight - in_group).astype(jnp.bfloat16), "grp").astype(jnp.float32),
        lax.psum((back_weight - back_group).astype(jnp.bfloat16), "grp").astype(jnp.float32),
        lax.psum((ada_weight - ada_group).astype(jnp.bfloat16), "grp").astype(jnp.float32),
        lax.psum((small_params - small_group).astype(jnp.bfloat16), "grp").astype(jnp.float32),
        lax.psum((up_bias - bias_group).astype(jnp.bfloat16), "grp").astype(jnp.float32),
    )
    group_count = lax.axis_size("grp")
    in_diff = in_total / group_count
    back_diff = back_total / group_count
    ada_diff = ada_total / group_count
    small_diff = small_total / group_count
    bias_diff = bias_total / group_count
    in_moment_new = outer_mu * in_moment + in_diff
    back_moment_new = outer_mu * back_moment + back_diff
    ada_moment_new = outer_mu * ada_moment + ada_diff
    small_moment_new = outer_mu * small_moment + small_diff
    bias_moment_new = outer_mu * bias_moment + bias_diff
    in_weight_new = in_weight - outer_rate * (in_diff + outer_mu * in_moment_new)
    back_weight_new = back_weight - outer_rate * (back_diff + outer_mu * back_moment_new)
    ada_weight_new = ada_weight - outer_rate * (ada_diff + outer_mu * ada_moment_new)
    small_params_new = small_params - outer_rate * (small_diff + outer_mu * small_moment_new)
    up_bias_new = up_bias - outer_rate * (bias_diff + outer_mu * bias_moment_new)
    return (
        block_here,
        input_grad,
        in_first_new[None],
        back_first_new[None],
        ada_first_new[None],
        small_first_new[None],
        bias_first_new[None],
        in_second_new[None],
        back_second_new[None],
        ada_second_new[None],
        small_second_new[None],
        bias_second_new[None],
        in_weight_new,
        back_weight_new,
        ada_weight_new,
        small_params_new,
        up_bias_new,
        in_diff,
        back_diff,
        ada_diff,
        small_diff,
        bias_diff,
        in_moment_new,
        back_moment_new,
        ada_moment_new,
        small_moment_new,
        bias_moment_new,
    )


def solution(mesh):
    in_specs = (
        P(("dp", "grp"), None, None),
        P(("dp", "grp")),
        P(("dp", "grp"), None),
        P(("dp", "grp"), None, None),
        P(),
        P("dp", None, "tp"),
        P(None, "tp", "dp"),
        P("dp", None, "tp"),
        P(None, "dp"),
        P(None, ("tp", "dp")),
        P("grp", "dp", None, "tp"),
        P("grp", None, "tp", "dp"),
        P("grp", "dp", None, "tp"),
        P("grp", None, "dp"),
        P("grp", None, ("tp", "dp")),
        P("grp", "dp", None, "tp"),
        P("grp", None, "tp", "dp"),
        P("grp", "dp", None, "tp"),
        P("grp", None, "dp"),
        P("grp", None, ("tp", "dp")),
        P("dp", None, "tp"),
        P(None, "tp", "dp"),
        P("dp", None, "tp"),
        P(None, "dp"),
        P(None, ("tp", "dp")),
    )
    out_specs = (
        P(("dp", "grp"), None, None),
        P(("dp", "grp"), None, None),
        P("grp", "dp", None, "tp"),
        P("grp", None, "tp", "dp"),
        P("grp", "dp", None, "tp"),
        P("grp", None, "dp"),
        P("grp", None, ("tp", "dp")),
        P("grp", "dp", None, "tp"),
        P("grp", None, "tp", "dp"),
        P("grp", "dp", None, "tp"),
        P("grp", None, "dp"),
        P("grp", None, ("tp", "dp")),
        P("dp", None, "tp"),
        P(None, "tp", "dp"),
        P("dp", None, "tp"),
        P(None, "dp"),
        P(None, ("tp", "dp")),
        P("dp", None, "tp"),
        P(None, "tp", "dp"),
        P("dp", None, "tp"),
        P(None, "dp"),
        P(None, ("tp", "dp")),
        P("dp", None, "tp"),
        P(None, "tp", "dp"),
        P("dp", None, "tp"),
        P(None, "dp"),
        P(None, ("tp", "dp")),
    )
    return jax.shard_map(
        on_device, mesh=mesh, in_specs=in_specs, out_specs=out_specs, check_vma=False
    )
```

profile of v0, /device:TPU:0, one launch (start us, length us, event | category | flops | bytes accessed | tf_op | source)
XLA Modules:
  0.0 757.7 jit_solution(3076118809999083786)
XLA Ops:
  7.3 2.8 convert_element_type.179
  12.6 5.3 all_gather.20
  20.2 11.3 %all_gather.18 = bf16[128,6,192]{2,0,1:T(8,128)(2,1)S(1)} all-gather(bf16[64,6,192]{2,0,1:T(8,128)(2,1)S(1)} %convert_element_type.175), channel_id=1, replica_groups=mesh['tp'=4,'dp'=2,'grp'=4] {'dp'}, dimensions={0}, use_global_device_ids=true | all-gather | bytes 442368 | tf_op jit(solution)/shard_map/all_gather | solution.py:102
  33.3 10.7 %all_gather.19 = f32[2,6,768]{1,0,2:T(2,128)} all-gather(f32[2,6,192]{1,0,2:T(2,128)} %copy.133), channel_id=1, replica_groups=mesh['tp'=4,'dp'=2,'grp'=4] {'tp'}, dimensions={2}, use_global_device_ids=true | all-gather | bytes 46080 | tf_op jit(solution)/shard_map/all_gather | solution.py:118
  45.4 3.6 all-gather.4.cloned.1.call-done
  49.1 3.4 fusion.88
  56.2 41.4 %while.44 = (s32[]{:T(128)}, bf16[4,512,3,64]{1,3,2,0:T(8,128)(2,1)}, f32[4,3,512]{2,1,0:T(4,128)S(1)}, s32[4]{0:T(128)S(1)}, bf16[2,1024,3,64]{1,3,2,0:T(8,128)...) while((s32[]{:T(128)}, ...), condition=%wide.region_5.6_spmd, body=%wide.region_2.5_spmd.sunk | while | flops 416905760 | bytes 20109780 | solution.py:155
  59.4 2.3 multiply_reduce_fusion.7
  63.1 3.5 fusion.166
  73.4 3.5 fusion.166
  80.1 2.3 multiply_reduce_fusion.7
  83.8 3.5 fusion.166
  94.1 3.5 fusion.166
  97.6 2.6 copy.135
  100.3 3.1 reshape.263
  103.4 5.0 fusion.86
  108.5 4.8 all-gather
  113.4 2.4 slice.104
  115.8 2.4 slice.103
  118.3 110.7 %all-reduce.12.cloned.1.call-done = f32[2,1024,768]{2,1,0:T(8,128)} async-done(((f32[2,1024,768]{2,1,0:T(8,128)}), f32[2,1024,768]{2,1,0:T(8,128)}) %all-reduce.12.cloned.1.call-update) | async-done | bytes 6291472 | tf_op jit(solution)/shard_map/psum | solution.py:166
  229.0 3.7 fusion.129
  234.9 3.4 fusion.128
  238.3 8.3 %fusion.131 = (bf16[768]{0:T(1024)(128)(2,1)}, bf16[2,1024,768]{2,1,0:T(8,128)(2,1)S(1)}) fusion(bf16[768,768,1]{1,0,2:T(8,128)(2,1)S(1)} %bitcast.304, bf16[2,1024,768]{2,1,0:T(8,128)(2,1)S(1)} %copy-done.6, f32[2,1024]{1,0:T(2,128)S(1)} %convert_element_type.191, f32[2,768]{1,0:T(2,128)S(1)} %get-tuple-element.536, f32[2,1024,768]{2,1,0:T(8,128)S(1)} %fusion.128, ...), kind=kOutput, calls=%fused_computation.251 | convolution fusion | flops 2463104256 | bytes 13781504 | tf_op jit(solution)/shard_map/nmw,pw->nmp/dot_general | solution.py:193
  248.3 3.9 convolution_convert_fusion
  252.3 8.8 %convolution_convert_fusion.1 = bf16[2,1024,768]{2,1,0:T(8,128)(2,1)} fusion(bf16[768,768,1]{1,0,2:T(8,128)(2,1)} %bitcast.303, f32[2,1024,768]{2,1,0:T(8,128)} %copy-done.80, f32[768]{0:T(1024)S(1)} %reshape.274), kind=kOutput, calls=%fused_computation.119 | convolution fusion | flops 2433220608 | bytes 10619904 | tf_op jit(solution)/shard_map/wrp,pj->wrj/dot_general | solution.py:179
  261.2 59.9 %all-reduce.14.cloned.1.call-done = bf16[2,1024,768]{2,1,0:T(8,128)(2,1)} async-done(((bf16[2,1024,768]{2,1,0:T(8,128)(2,1)}), bf16[2,1024,768]{2,1,0:T(8,128)(2,1)}) %all-reduce.14.cloned.1.call-update) | async-done | bytes 3145744 | tf_op jit(solution)/shard_map/psum | solution.py:207
  321.0 4.9 fusion.56
  326.0 6.8 fusion.58
  332.9 5.9 multiply_reduce_fusion.3
  338.8 2.7 copy-done.5
  341.5 3.0 convolution_convert_fusion.2
  344.5 73.7 %while.46 = (s32[]{:T(128)}, f32[2,1024,3,64]{1,3,2,0:T(8,128)}, f32[2,1024,3,64]{1,3,2,0:T(8,128)}, bf16[2,1024,3,64]{1,3,2,0:T(8,128)(2,1)}, bf16[2,1024,3,64]...) while((s32[]{:T(128)}, f32[2,1024,3,64]{1,3,2,0:T(8,128)}, ...), condition=%wide.region_17.18_spmd, body=%wide.region_13.17_spmd.sunk | while | flops 1026587136 | bytes 76356288 | solution.py:269
  348.7 25.3 %while.47 = (s32[]{:T(128)}, f32[1024,3,64]{0,2,1:T(8,128)S(1)}, f32[1024,3,64]{0,2,1:T(8,128)S(1)}, f32[2,512,3,64]{1,3,2,0:T(8,128)}, s32[2]{0:T(128)S(1)}, /*...) while((s32[]{:T(128)}, f32[1024,3,64]{0,2,1:T(8,128)S(1)}, ...), condition=%wide.region_16.16_spmd.clone, body=%wide.region_14.15_spmd.clone.sunk | while | flops 1026587136 | bytes 59029832 | solution.py:264
  374.0 2.7 copy.214
  385.6 25.3 %while.47 = (s32[]{:T(128)}, f32[1024,3,64]{0,2,1:T(8,128)S(1)}, f32[1024,3,64]{0,2,1:T(8,128)S(1)}, f32[2,512,3,64]{1,3,2,0:T(8,128)}, s32[2]{0:T(128)S(1)}, /*...) while((s32[]{:T(128)}, f32[1024,3,64]{0,2,1:T(8,128)S(1)}, ...), condition=%wide.region_16.16_spmd.clone, body=%wide.region_14.15_spmd.clone.sunk | while | flops 1026587136 | bytes 59029832 | solution.py:264
  410.9 2.7 copy.214
  418.2 2.4 multiply_add_fusion.7
  421.9 5.3 bitcast_convert_fusion
  428.8 8.2 %bitcast_convert_fusion.2 = bf16[768,768]{0,1:T(8,128)(2,1)} fusion(bf16[2,1024,768]{2,1,0:T(8,128)(2,1)} %copy-done.81, f32[2,1024,768]{2,1,0:T(8,128)} %copy-done.2, f32[2,768]{1,0:T(2,128)S(1)} %copy-done.67, f32[2,768]{1,0:T(2,128)S(1)} %copy-done.38, f32[768]{0:T(1024)S(1)} %copy-done.50, f32[2,1024]{1,0:T(2,128)S(1)} %copy-done.42, ...), kind=kOutput, calls=%fused_computation.117 | convolution fusion | flops 2425946112 | bytes 10648576 | tf_op jit(solution)/shard_map/rzi,rzk->ik/dot_general | solution.py:200
  437.0 7.9 %bitcast_convert_fusion.1 = bf16[768,768]{1,0:T(8,128)(2,1)} fusion(bf16[2,1024,768]{2,1,0:T(8,128)(2,1)S(1)} %copy-done.7, f32[2,1024]{1,0:T(2,128)S(1)} %copy-done.34, f32[2,768]{1,0:T(2,128)S(1)} %copy-done.52, f32[2,1024,768]{2,1,0:T(8,128)} %copy-done.80, f32[768]{0:T(1024)S(1)} %copy-done.69), kind=kOutput, calls=%fused_computation.116 | convolution fusion | flops 2438529024 | bytes 10634240 | tf_op jit(solution)/shard_map/kix,kit->xt/dot_general | solution.py:190
  445.0 3.7 fusion.81
  450.0 5.4 copy.163
  455.4 5.3 reshape.292
  461.1 86.2 %all-reduce.18.cloned.1.call-done = (bf16[2,1024,768]{2,1,0:T(8,128)(2,1)}, bf16[2,1024,768]{2,1,0:T(8,128)(2,1)}) async-done(((bf16[2,1024,768]{2,1,0:T(8,128)(2,1)}, bf16[2,1024,768]{2,1,0:T(8,128)(2,1)}), (bf16[2,1024,768]{2,1,0:T(8,128)(2,1)}, bf16[2,1024,768]{2,1,0:T(8,128)(2,1)})) %all-reduce.18.cloned.1.call-update) | async-done | bytes 6291472 | tf_op jit(solution)/shard_map/psum | solution.py:183
  547.3 9.8 %multiply_reduce_fusion.2 = (f32[2,768]{1,0:T(2,128)S(1)}, bf16[2,1024,768]{2,1,0:T(8,128)(2,1)}, f32[2,1024]{1,0:T(2,128)S(1)}) fusion(bf16[2,1024,768]{2,1,0:T(8,128)(2,1)} %param.34, bf16[2,1024,768]{2,1,0:T(8,128)(2,1)} %get-tuple-element.484, f32[2,1024]{1,0:T(2,128)S(1)} %copy-done.34, f32[768]{0:T(1024)S(1)} %copy-done.59, ...), kind=kLoop, calls=%fused_computation.98 | loop fusion | flops 25162240 | bytes 22069248 | tf_op jit(solution)/shard_map/reduce_sum | solution.py:188
  557.2 4.4 fusion.57
  563.1 4.3 bitcast_convert_fusion.3
  569.0 4.1 copy.169
  573.2 2.8 fusion.75
  576.9 12.0 %reduce-scatter.18.cloned.1.call-done = bf16[384,960]{1,0:T(8,128)(2,1)} async-done(((bf16[768,960]{1,0:T(8,128)(2,1)}), bf16[384,960]{1,0:T(8,128)(2,1)}) %reduce-scatter.18.cloned.1.call-update) | async-done | bytes 737296
  588.9 3.3 reshape.293
  592.1 2.5 copy.164
  594.6 5.3 fusion.78
  601.1 3.9 reduce-scatter.14.cloned.1.call-done
  604.9 2.5 fusion.93
  607.4 32.9 %reduce-scatter.16.cloned.1.call-done = bf16[384,1344]{1,0:T(8,128)(2,1)} async-done(((bf16[768,1344]{1,0:T(8,128)(2,1)}), bf16[384,1344]{1,0:T(8,128)(2,1)}) %reduce-scatter.16.cloned.1.call-update) | async-done | bytes 1032208
  640.4 2.3 copy.170
  642.7 6.8 fusion.74
  650.2 6.7 add_add_fusion.2
  659.4 19.6 %all-reduce.4 = (bf16[9,384]{1,0:T(8,128)(2,1)S(1)}, bf16[4,96]{1,0:T(4,128)(2,1)S(1)}) all-reduce(bf16[9,384]{1,0:T(8,128)(2,1)S(1)} %get-tuple-element.542, bf16[4,96]{1,0:T(4,128)(2,1)S(1)} %get-tuple-element.545), channel_id=1, replica_groups=mesh['tp'=4,'dp'=2,'grp'=4] {'grp'}, use_global_device_ids=true, to_apply=%region_40.41 | all-reduce | flops 3840 | bytes 15360 | tf_op jit(solution)/shard_map/psum | solution.py:353
  680.2 60.6 %all-reduce.16.cloned.1.call-done = (bf16[384,7,192]{0,2,1:T(8,128)(2,1)}, bf16[5,192,384]{2,1,0:T(8,128)(2,1)}, bf16[64,6,192]{2,0,1:T(8,128)(2,1)}) async-done(((bf16[384,7,192]{0,2,1:T(8,128)(2,1)}, bf16[5,192,384]{2,1,0:T(8,128)(2,1)}, bf16[64,6,192]{2,0,1:T(8,128)(2,1)}), (bf16[384,7,192]{0,2,1:T(8,128)(2,1)}, bf16[5,192,384]{2,1,0:T(8,128)(2,1)}, ...) | async-done | bytes 1916944 | tf_op jit(solution)/shard_map/psum | solution.py:350
  740.8 2.4 multiply_subtract_fusion.2
  743.2 4.5 multiply_subtract_fusion.1
  747.7 3.3 multiply_subtract_fusion
  (347 shorter events, 98.8 us)
Async XLA Ops:
  7.2 24.3 %copy-start = (f32[64,128]{1,0:T(8,128)S(1)}, f32[64,128]{1,0:T(8,128)}, u32[]{:S(2)}) copy-start(f32[64,128]{1,0:T(8,128)} %param.35) | copy-start | bytes 98308
  7.2 10.7 %copy-start.3 = (bf16[2,1024,768]{2,1,0:T(8,128)(2,1)S(1)}, bf16[2,1024,768]{2,1,0:T(8,128)(2,1)}, u32[]{:S(2)}) copy-start(bf16[2,1024,768]{2,1,0:T(8,128)(2,1)} %param.31) | copy-start | bytes 9437188
  7.2 41.8 %all-gather.4.cloned.1.call-start = ((), (), s32[]{:S(2)}) async-start(), calls=%async_computation.5 | async-start | bytes 3096576 | tf_op jit(solution)/shard_map/all_gather | solution.py:100
  10.1 21.4 %copy-start.79 = (s32[2]{0:T(128)S(1)}, s32[2]{0:T(128)}, u32[]{:S(2)}) copy-start(s32[2]{0:T(128)} %param.32) | copy-start | bytes 28
  10.1 93.3 %all-gather.6.cloned.1.call-start = ((), (), s32[]{:S(2)}) async-start(), calls=%async_computation.6 | async-start | bytes 2211840 | tf_op jit(solution)/shard_map/all_gather | solution.py:101
  12.5 216.5 %all-reduce.12.cloned.1.call-start = ((), (), s32[]{:S(2)}) async-start(), calls=%async_computation.7 | async-start | bytes 12582912 | tf_op jit(solution)/shard_map/psum | solution.py:166
  18.5 34.0 %copy-start.29 = (f32[2,1024]{1,0:T(2,128)}, f32[2,1024]{1,0:T(2,128)S(1)}, u32[]{:S(2)}) copy-start(f32[2,1024]{1,0:T(2,128)S(1)} %broadcast_multiply_fusion.1) | copy-start | bytes 24580
  19.6 13.7 %copy-start.45 = (f32[2,1024]{1,0:T(2,128)}, f32[2,1024]{1,0:T(2,128)S(1)}, u32[]{:S(2)}) copy-start(f32[2,1024]{1,0:T(2,128)S(1)} %fusion.63) | copy-start | bytes 24580
  19.6 32.9 %copy-start.43 = (f32[2,1024]{1,0:T(2,128)}, f32[2,1024]{1,0:T(2,128)S(1)}, u32[]{:S(2)}) copy-start(f32[2,1024]{1,0:T(2,128)S(1)} %fusion.106) | copy-start | bytes 24580
  20.2 32.3 %copy-start.47 = (f32[768]{0:T(1024)}, f32[768]{0:T(1024)S(1)}, u32[]{:S(2)}) copy-start(f32[768]{0:T(1024)S(1)} %get-tuple-element.426) | copy-start | bytes 9220
  33.3 20.5 %copy-start.16 = (f32[1024,32]{0,1:T(8,128)}, f32[1024,32]{0,1:T(8,128)S(1)}, u32[]{:S(2)}) copy-start(f32[1024,32]{0,1:T(8,128)S(1)} %get-tuple-element.548) | copy-start | bytes 393220
  33.3 20.5 %copy-start.18 = (f32[1024,32]{0,1:T(8,128)}, f32[1024,32]{0,1:T(8,128)S(1)}, u32[]{:S(2)}) copy-start(f32[1024,32]{0,1:T(8,128)S(1)} %get-tuple-element.549) | copy-start | bytes 393220
  45.4 7.1 copy-start.35
  45.4 7.1 copy-start.64
  45.4 188.3 %copy-start.66 = (f32[2,768]{1,0:T(2,128)}, f32[2,768]{1,0:T(2,128)S(1)}, u32[]{:S(2)}) copy-start(f32[2,768]{1,0:T(2,128)S(1)} %get-tuple-element.537) | copy-start | bytes 18436
  45.4 192.9 %copy-start.51 = (f32[2,768]{1,0:T(2,128)}, f32[2,768]{1,0:T(2,128)S(1)}, u32[]{:S(2)}) copy-start(f32[2,768]{1,0:T(2,128)S(1)} %get-tuple-element.536) | copy-start | bytes 18436
  45.4 287.4 %copy-start.37 = (f32[2,768]{1,0:T(2,128)}, f32[2,768]{1,0:T(2,128)S(1)}, u32[]{:S(2)}) copy-start(f32[2,768]{1,0:T(2,128)S(1)} %get-tuple-element.538) | copy-start | bytes 18436
  45.4 293.4 %copy-start.39 = (f32[2,768]{1,0:T(2,128)}, f32[2,768]{1,0:T(2,128)S(1)}, u32[]{:S(2)}) copy-start(f32[2,768]{1,0:T(2,128)S(1)} %get-tuple-element.541) | copy-start | bytes 18436
  103.4 10.0 %copy-start.62 = (s32[2,1024]{1,0:T(2,128)S(1)}, s32[2,1024]{1,0:T(2,128)}, u32[]{:S(2)}) copy-start(s32[2,1024]{1,0:T(2,128)} %param.33) | copy-start | bytes 24580
  108.4 212.7 %all-reduce.14.cloned.1.call-start = ((), (), s32[]{:S(2)}) async-start(), calls=%async_computation.8 | async-start | bytes 6291456 | tf_op jit(solution)/shard_map/psum | solution.py:207
  113.4 138.9 %copy-start.68 = (f32[768]{0:T(1024)}, f32[768]{0:T(1024)S(1)}, u32[]{:S(2)}) copy-start(f32[768]{0:T(1024)S(1)} %reshape.274) | copy-start | bytes 9220
  113.4 219.4 %copy-start.33 = (f32[2,1024]{1,0:T(2,128)}, f32[2,1024]{1,0:T(2,128)S(1)}, u32[]{:S(2)}) copy-start(f32[2,1024]{1,0:T(2,128)S(1)} %convert_element_type.191) | copy-start | bytes 24580
  232.8 100.1 %copy-start.31 = (f32[2,1024]{1,0:T(2,128)}, f32[2,1024]{1,0:T(2,128)S(1)}, u32[]{:S(2)}) copy-start(f32[2,1024]{1,0:T(2,128)S(1)} %broadcast_multiply_fusion) | copy-start | bytes 24580
  233.6 99.2 %copy-start.41 = (f32[2,1024]{1,0:T(2,128)}, f32[2,1024]{1,0:T(2,128)S(1)}, u32[]{:S(2)}) copy-start(f32[2,1024]{1,0:T(2,128)S(1)} %fusion.107) | copy-start | bytes 24580
  238.3 8.4 %copy-start.80 = (f32[2,1024,768]{2,1,0:T(8,128)}, f32[2,1024,768]{2,1,0:T(8,128)S(1)}, u32[]{:S(2)}) copy-start(f32[2,1024,768]{2,1,0:T(8,128)S(1)} %fusion.128) | copy-start | bytes 18874372
  252.2 295.0 %all-reduce.18.cloned.1.call-start = ((), (), s32[]{:S(2)}) async-start(), calls=%async_computation.15 | async-start | bytes 12582912 | tf_op jit(solution)/shard_map/psum | solution.py:183
  321.0 11.8 %slice-start = ((s8[6291456]{0:T(1024)(128)(4,1)}), s8[4194304]{0:T(1024)(128)(4,1)S(1)}, s32[]{:S(2)}) async-start(s8[6291456]{0:T(1024)(128)(4,1)} %bitcast.294), calls=%async_computation.16 | async-start | bytes 8388608
  326.0 6.9 slice-start.1
  344.5 73.7 %copy-start.17 = (f32[1024,32]{0,1:T(8,128)S(1)}, f32[1024,32]{0,1:T(8,128)}, u32[]{:S(2)}) copy-start(f32[1024,32]{0,1:T(8,128)} %copy-done.16) | copy-start | bytes 393220
  344.5 73.7 %copy-start.19 = (f32[1024,32]{0,1:T(8,128)S(1)}, f32[1024,32]{0,1:T(8,128)}, u32[]{:S(2)}) copy-start(f32[1024,32]{0,1:T(8,128)} %copy-done.18) | copy-start | bytes 393220
  427.2 148.8 %reduce-scatter.22.cloned.1.call-start = ((), (), s32[]{:S(2)}) async-start(), calls=%async_computation.13 | async-start | bytes 73728
  428.7 8.2 %copy-start.7 = (bf16[2,1024,768]{2,1,0:T(8,128)(2,1)S(1)}, bf16[2,1024,768]{2,1,0:T(8,128)(2,1)}, u32[]{:S(2)}) copy-start(bf16[2,1024,768]{2,1,0:T(8,128)(2,1)} %param.34) | copy-start | bytes 9437188
  428.7 8.2 %copy-start.34 = (f32[2,1024]{1,0:T(2,128)S(1)}, f32[2,1024]{1,0:T(2,128)}, u32[]{:S(2)}) copy-start(f32[2,1024]{1,0:T(2,128)} %copy-done.33) | copy-start | bytes 24580
  428.7 8.2 %copy-start.52 = (f32[2,768]{1,0:T(2,128)S(1)}, f32[2,768]{1,0:T(2,128)}, u32[]{:S(2)}) copy-start(f32[2,768]{1,0:T(2,128)} %copy-done.51) | copy-start | bytes 18436
  428.8 8.2 %copy-start.69 = (f32[768]{0:T(1024)S(1)}, f32[768]{0:T(1024)}, u32[]{:S(2)}) copy-start(f32[768]{0:T(1024)} %copy-done.68) | copy-start | bytes 9220
  436.9 8.0 %copy-start.13 = (bf16[2,1024,192]{1,0,2:T(2,128)(2,1)S(1)}, bf16[2,1024,192]{1,0,2:T(2,128)(2,1)}, u32[]{:S(2)}) copy-start(bf16[2,1024,192]{1,0,2:T(2,128)(2,1)} %reshape.263) | copy-start | bytes 2359300
  436.9 8.0 %copy-start.40 = (f32[2,768]{1,0:T(2,128)S(1)}, f32[2,768]{1,0:T(2,128)}, u32[]{:S(2)}) copy-start(f32[2,768]{1,0:T(2,128)} %copy-done.39) | copy-start | bytes 18436
  444.9 144.0 %reduce-scatter.18.cloned.1.call-start = ((), (), s32[]{:S(2)}) async-start(), calls=%async_computation.11 | async-start | bytes 2359296
  448.7 98.6 %copy-start.4 = (bf16[2,1024,768]{2,1,0:T(8,128)(2,1)S(1)}, bf16[2,1024,768]{2,1,0:T(8,128)(2,1)}, u32[]{:S(2)}) copy-start(bf16[2,1024,768]{2,1,0:T(8,128)(2,1)} %param.31) | copy-start | bytes 9437188
  448.7 98.6 %copy-start.30 = (f32[2,1024]{1,0:T(2,128)S(1)}, f32[2,1024]{1,0:T(2,128)}, u32[]{:S(2)}) copy-start(f32[2,1024]{1,0:T(2,128)} %copy-done.29) | copy-start | bytes 24580
  448.7 98.6 %copy-start.36 = (f32[2,768]{1,0:T(2,128)S(1)}, f32[2,768]{1,0:T(2,128)}, u32[]{:S(2)}) copy-start(f32[2,768]{1,0:T(2,128)} %copy-done.35) | copy-start | bytes 18436
  448.7 98.5 %copy-start.48 = (f32[768]{0:T(1024)S(1)}, f32[768]{0:T(1024)}, u32[]{:S(2)}) copy-start(f32[768]{0:T(1024)} %copy-done.47) | copy-start | bytes 9220
  448.7 98.5 %copy-start.59 = (f32[768]{0:T(1024)S(1)}, f32[768]{0:T(1024)}, u32[]{:S(2)}) copy-start(f32[768]{0:T(1024)} %get-tuple-element.424) | copy-start | bytes 9220
  460.7 144.3 %reduce-scatter.14.cloned.1.call-start = ((), (), s32[]{:S(2)}) async-start(), calls=%async_computation.9 | async-start | bytes 589824 | tf_op jit(solution)/shard_map/reduce_scatter | solution.py:324
  547.3 9.8 %copy-start.46 = (f32[2,1024]{1,0:T(2,128)S(1)}, f32[2,1024]{1,0:T(2,128)}, u32[]{:S(2)}) copy-start(f32[2,1024]{1,0:T(2,128)} %copy-done.45) | copy-start | bytes 24580
  547.3 9.9 %copy-start.8 = (bf16[2,1024,768]{2,1,0:T(8,128)(2,1)S(1)}, bf16[2,1024,768]{2,1,0:T(8,128)(2,1)}, u32[]{:S(2)}) copy-start(bf16[2,1024,768]{2,1,0:T(8,128)(2,1)} %get-tuple-element.485) | copy-start | bytes 9437188
  547.3 9.9 %copy-start.44 = (f32[2,1024]{1,0:T(2,128)S(1)}, f32[2,1024]{1,0:T(2,128)}, u32[]{:S(2)}) copy-start(f32[2,1024]{1,0:T(2,128)} %copy-done.43) | copy-start | bytes 24580
  557.1 6.0 copy-start.65
  563.1 77.3 %reduce-scatter.16.cloned.1.call-start = ((), (), s32[]{:S(2)}) async-start(), calls=%async_computation.10 | async-start | bytes 3244032
  567.5 9.4 %copy-start.63 = (bf16[768]{0:T(1024)(128)(2,1)S(1)}, bf16[768]{0:T(1024)(128)(2,1)}, u32[]{:S(2)}) copy-start(bf16[768]{0:T(1024)(128)(2,1)} %get-tuple-element.416) | copy-start | bytes 4612
  573.2 83.8 %reduce-scatter.20.cloned.1.call-start = ((), (), s32[]{:S(2)}) async-start(), calls=%async_computation.12 | async-start | bytes 294912
  600.8 139.9 %all-reduce.16.cloned.1.call-start = ((), (), s32[]{:S(2)}) async-start(), calls=%async_computation.14 | async-start | bytes 3932160 | tf_op jit(solution)/shard_map/psum | solution.py:350
  642.7 6.9 copy-start.58
  642.7 6.9 copy-start.73
  642.7 6.9 copy-start.74
  650.2 7.9 %copy-start.28 = (f32[9,384]{1,0:T(8,128)S(1)}, f32[9,384]{1,0:T(8,128)}, u32[]{:S(2)}) copy-start(f32[9,384]{1,0:T(8,128)} %param.39) | copy-start | bytes 41476
  650.2 7.9 %copy-start.60 = (f32[1,9,384]{2,0,1:T(1,128)S(1)}, f32[1,9,384]{2,0,1:T(1,128)}, u32[]{:S(2)}) copy-start(f32[1,9,384]{2,0,1:T(1,128)} %param.44) | copy-start | bytes 41476
  650.2 7.9 %copy-start.61 = (f32[1,9,384]{2,0,1:T(1,128)S(1)}, f32[1,9,384]{2,0,1:T(1,128)}, u32[]{:S(2)}) copy-start(f32[1,9,384]{2,0,1:T(1,128)} %param.49) | copy-start | bytes 41476
  650.2 28.8 %copy-start.75 = (f32[4,96]{1,0:T(4,128)S(1)}, f32[4,96]{1,0:T(4,128)}, u32[]{:S(2)}) copy-start(f32[4,96]{1,0:T(4,128)} %param.55) | copy-start | bytes 4612
  650.2 29.4 %copy-start.56 = (f32[9,384]{1,0:T(8,128)S(1)}, f32[9,384]{1,0:T(8,128)}, u32[]{:S(2)}) copy-start(f32[9,384]{1,0:T(8,128)} %param.54) | copy-start | bytes 41476
  656.9 90.8 %copy-start.12 = (f32[384,7,192]{0,2,1:T(8,128)S(1)}, f32[384,7,192]{0,2,1:T(8,128)}, u32[]{:S(2)}) copy-start(f32[384,7,192]{0,2,1:T(8,128)} %param.36) | copy-start | bytes 6193156
  740.8 6.9 copy-start.15
  740.8 6.9 copy-start.24
  743.2 7.7 %copy-start.1 = (f32[64,128]{1,0:T(8,128)S(1)}, f32[64,128]{1,0:T(8,128)}, u32[]{:S(2)}) copy-start(f32[64,128]{1,0:T(8,128)} %param.35) | copy-start | bytes 98308
  (39 other events, 101.4 us)
Sparse Core Ops, SparseCore 0:
  10.2 38.7 all-gather.3
  51.2 26.9 all-gather.5
  108.5 120.4 all-reduce.11
  252.4 68.6 all-reduce.13
  427.3 119.8 all-reduce.17
  549.9 10.0 reduce-scatter.21
  562.8 26.0 reduce-scatter.17
  591.8 13.1 reduce-scatter.13
  607.8 32.5 reduce-scatter.15
  643.1 10.9 reduce-scatter.19
  657.4 83.3 all-reduce.15
where the time goes:
time: 763 us; the launch traced here: 758 us
  waiting for transfers between devices  370 us (48%)
  matrix products  116 us (15%)
  other arithmetic  99.2 us (13%)
  local copies, waits for them, and re-layouts  82.6 us (11%)
  blocking collectives  51.7 us (7%)
  loops' own time  21.7 us (3%)
  between operations  15.3 us (2%)
    psum x1, waiting for transfers between devices, on_device(): attended = lax.psum(attention_branch, 'tp')  111 us
    psum x1, waiting for transfers between devices, on_device(): lax.psum(feedforward_branch.astype(jnp.bfloat16), 'tp').astype(jnp.float32)  86.2 us
    psum x1, waiting for transfers between devices, on_device(): lax.psum((in_weight - in_group).astype(jnp.bfloat16), 'grp')  60.6 us
    psum x1, waiting for transfers between devices, on_device(): lax.psum(hidden_two_part.astype(jnp.bfloat16), 'tp').astype(jnp.float32)  59.9 us
    unnamed x15, waiting for transfers between devices  45.1 us
    unnamed x177, local copies, waits for them, and re-layouts  34.9 us
    psum x1, blocking collectives, on_device(): lax.psum((small_params - small_group).astype(jnp.bfloat16), 'grp')  19.6 us
    reduce_sum x3, other arithmetic, layer_norm(): return centered * lax.rsqrt(variance + norm_eps) * gain_row  16.2 us
  transfers between devices with their start and end apart: 11, of which 8 were waited for; matrix products, arithmetic and copies ran while one was open for 21% of the time, Pallas kernels for 0%

commit v1 on v0

v1 whole, which is shorter than its diff:
```python
import functools

import jax
import jax.numpy as jnp
import numpy as np
from jax import lax
from jax.experimental import pallas as pl
from jax.experimental.pallas import tpu as pltpu
from jax.sharding import PartitionSpec as P

HEAD_DIM = 64
STEP = 10
MESH = pl.DeviceIdType.MESH
ANY = pl.BlockSpec(memory_space=pl.ANY)
VMEM = pl.BlockSpec(memory_space=pltpu.VMEM)
MIB = 2**20

f32 = jnp.float32
bf16 = jnp.bfloat16
highest = lax.Precision.HIGHEST
norm_eps = 1e-05
beta_one = 0.9
beta_two = 0.999
adam_eps = 1e-08
decay_rate = 0.1
rate_matrix = 0.03
rate_small = 0.3
outer_mu = 0.9
outer_rate = 0.7
gelu_a = 0.7978845608028654
gelu_b = 0.044715


def nn(a, b):
    return lax.dot_general(a, b, (((1,), (0,)), ((), ())), preferred_element_type=f32)


def nt(a, b):
    return lax.dot_general(a, b, (((1,), (1,)), ((), ())), preferred_element_type=f32)


def tn(a, b):
    return lax.dot_general(a, b, (((0,), (0,)), ((), ())), preferred_element_type=f32)


def fold(values):
    return jnp.sum(values.reshape(values.shape[0] // 8, 8, values.shape[1]), axis=0)


def normalize(values):
    mean = jnp.mean(values, axis=-1, keepdims=True)
    centered = values - mean
    variance = jnp.mean(centered * centered, axis=-1, keepdims=True)
    inverse = lax.rsqrt(variance + norm_eps)
    return centered * inverse, inverse


def norm_pull(grad_hat, hat, inverse):
    first = jnp.mean(grad_hat, axis=-1, keepdims=True)
    second = jnp.mean(grad_hat * hat, axis=-1, keepdims=True)
    return inverse * (grad_hat - first - hat * second)


def adam_parts(gradient, first, second):
    first_new = beta_one * first + (1.0 - beta_one) * gradient
    second_new = beta_two * second + (1.0 - beta_two) * gradient * gradient
    return first_new, second_new


def adam_diff(weight, first_new, second_new, rate, decay):
    first_hat = first_new / (1.0 - beta_one**STEP)
    second_hat = second_new / (1.0 - beta_two**STEP)
    return rate * (first_hat / (jnp.sqrt(second_hat) + adam_eps) + decay * weight)


def mod_kernel(cores, cond, wa, ps, bu, mod_out, ps_out, bu_out, c_got, parts, got, ps_low, bu_low, csem, psem, bsem, msem):
    t, d = lax.axis_index("tp"), lax.axis_index("dp")
    n_tp = mod_out.shape[0]
    s = t // cores
    c = lax.rem(t, cores)
    barrier = pltpu.get_barrier_semaphore()
    others = []
    for dt in range(n_tp):
        for dd in range(2):
            if dt or dd:
                others.append((lax.rem(t + dt, n_tp), lax.rem(d + dd, 2)))
    for pt, pd in others:
        pl.semaphore_signal(barrier, inc=1, device_id={"tp": pt, "dp": pd}, device_id_type=MESH)
    pl.semaphore_wait(barrier, len(others))
    cc = pltpu.make_async_remote_copy(
        src_ref=cond.at[1 - d], dst_ref=c_got, send_sem=csem.at[0], recv_sem=csem.at[1],
        device_id={"dp": 1 - d}, device_id_type=MESH)
    cc.start()
    ps_low[...] = ps[...].astype(bf16).astype(f32)
    bu_low[...] = bu[...].astype(bf16).astype(f32)
    ps_out[d] = ps_low[...]
    bu_out[s, d] = bu_low[...]
    pc = pltpu.make_async_remote_copy(
        src_ref=ps_low, dst_ref=ps_out.at[d], send_sem=psem.at[0], recv_sem=psem.at[1],
        device_id={"dp": 1 - d}, device_id_type=MESH)
    pc.start()
    bcs = []
    for ds, dd in ((0, 1), (1, 0), (1, 1)):
        bc = pltpu.make_async_remote_copy(
            src_ref=bu_low, dst_ref=bu_out.at[s, d], send_sem=bsem.at[0, ds, dd], recv_sem=bsem.at[1, ds, dd],
            device_id={"tp": lax.rem(s + ds, 2) * cores + c, "dp": lax.rem(d + dd, 2)}, device_id_type=MESH)
        bc.start()
        bcs.append(bc)
    parts[...] = jnp.zeros_like(parts)
    mine = cond[d].astype(bf16)
    for a in range(6):
        product = nn(mine, wa[a].astype(bf16))
        for ss in range(2):
            parts[d, ss, a : a + 1, :] = product[ss : ss + 1]
    cc.wait()
    theirs = c_got[...].astype(bf16)
    for a in range(6):
        product = nn(theirs, wa[a].astype(bf16))
        for ss in range(2):
            parts[1 - d, ss, a : a + 1, :] = product[ss : ss + 1]
    sends = []
    for i, (pt, pd) in enumerate(others):
        mc = pltpu.make_async_remote_copy(
            src_ref=parts.at[pd, pt // cores], dst_ref=got.at[t, d], send_sem=msem.at[0, i], recv_sem=msem.at[1, i],
            device_id={"tp": pt, "dp": pd}, device_id_type=MESH)
        mc.start()
        sends.append(mc)
    got[t, d] = parts[d, s]
    for mc in sends:
        mc.wait()
    pc.wait()
    for bc in bcs:
        bc.wait()
    mod_out[...] = got[:, 0] + got[:, 1]


def exchange_modulation(cores, cond, wa, ps, bu):
    n_tp = lax.axis_size("tp")
    half_c, width = wa.shape[1:]
    return pl.pallas_call(
        functools.partial(mod_kernel, cores),
        out_shape=(
            jax.ShapeDtypeStruct((n_tp, 8, width), f32),
            jax.ShapeDtypeStruct((2,) + ps.shape, f32),
            jax.ShapeDtypeStruct((2, 2) + bu.shape, f32),
        ),
        in_specs=[VMEM] * 4,
        out_specs=(VMEM,) * 3,
        scratch_shapes=[
            pltpu.VMEM((8, half_c), f32),
            pltpu.VMEM((2, 2, 8, width), f32),
            pltpu.VMEM((n_tp, 2, 8, width), f32),
            pltpu.VMEM(ps.shape, f32),
            pltpu.VMEM(bu.shape, f32),
            pltpu.SemaphoreType.DMA((2,)),
            pltpu.SemaphoreType.DMA((2,)),
            pltpu.SemaphoreType.DMA((2, 2, 2)),
            pltpu.SemaphoreType.DMA((2, 2 * n_tp - 1)),
        ],
        compiler_params=pltpu.CompilerParams(collective_id=0, has_side_effects=True),
        name="mod_exchange",
    )(cond, wa, ps, bu)


def gather_kernel(cores, wi, wb, wq, wo, wu, wd, lsem, ssem, rsem):
    t, d = lax.axis_index("tp"), lax.axis_index("dp")
    s = t // cores
    c = lax.rem(t, cores)
    rows, cols = wi.shape[1:]
    xdev = {"dp": 1 - d}
    ydev = {"tp": (1 - s) * cores + c}

    def block(a, ss, dd):
        where = (pl.ds(pl.multiple_of(ss * rows, 16), rows), pl.ds(pl.multiple_of(dd * cols, 128), cols))
        if a < 3:
            return wq.at[(a,) + where]
        if a == 3:
            return wo.at[where]
        if a < 8:
            return wu.at[(a - 4,) + where]
        return wd.at[(a - 8,) + where]

    def own(a):
        if a < 3:
            return wi.at[a]
        if a == 3:
            return wb.at[0]
        if a < 8:
            return wi.at[a - 1]
        return wb.at[a - 7]

    def remote(kind, a, source, target, device):
        return pltpu.make_async_remote_copy(
            src_ref=source, dst_ref=target, send_sem=ssem.at[kind, a], recv_sem=rsem.at[kind, a],
            device_id=device, device_id_type=MESH)

    barrier = pltpu.get_barrier_semaphore()
    for dev in (xdev, ydev):
        pl.semaphore_signal(barrier, inc=1, device_id=dev, device_id_type=MESH)
    pl.semaphore_wait(barrier, 2)
    xs, ys, zs, ls = [], [], [], []
    for a in range(12):
        xs.append(remote(0, a, own(a), block(a, s, d), xdev))
        ys.append(remote(1, a, own(a), block(a, s, d), ydev))
        xs[a].start()
        ys[a].start()
        ls.append(pltpu.make_async_copy(own(a), block(a, s, d), lsem.at[a]))
        ls[a].start()
    for a in range(12):
        if a % 2 == 0:
            xs[a].wait_recv()
            zs.append(remote(2, a, block(a, s, 1 - d), block(a, s, 1 - d), ydev))
        else:
            ys[a].wait_recv()
            zs.append(remote(2, a, block(a, 1 - s, d), block(a, 1 - s, d), xdev))
        zs[a].start()
    for a in range(12):
        xs[a].wait_send()
        ys[a].wait_send()
        (ys if a % 2 == 0 else xs)[a].wait_recv()
        zs[a].wait()
        ls[a].wait()


def gather_weights(cores, wi, wb):
    rows, cols = wi.shape[1:]
    full = (2 * rows, 2 * cols)
    return pl.pallas_call(
        functools.partial(gather_kernel, cores),
        out_shape=(
            jax.ShapeDtypeStruct((3,) + full, bf16),
            jax.ShapeDtypeStruct(full, bf16),
            jax.ShapeDtypeStruct((4,) + full, bf16),
            jax.ShapeDtypeStruct((4,) + full, bf16),
        ),
        in_specs=[ANY, ANY],
        out_specs=(ANY,) * 4,
        scratch_shapes=[
            pltpu.SemaphoreType.DMA((12,)),
            pltpu.SemaphoreType.DMA((3, 12)),
            pltpu.SemaphoreType.DMA((3, 12)),
        ],
        compiler_params=pltpu.CompilerParams(collective_id=1, has_side_effects=True),
        name="weight_gather",
    )(wi, wb)


def turn(values, cosine, sine):
    heads = values.shape[0] // HEAD_DIM
    half = HEAD_DIM // 2
    out = []
    for h in range(heads):
        low = values[h * HEAD_DIM : h * HEAD_DIM + half]
        high = values[h * HEAD_DIM + half : (h + 1) * HEAD_DIM]
        out.append(low * cosine - high * sine)
        out.append(high * cosine + low * sine)
    return jnp.concatenate(out, axis=0)


def project_kernel(tok, vecs, wq, cosine, sine, h1, q_t, k_t, v_t, k_r, v_r):
    hat, _ = normalize(tok[...].astype(f32))
    hidden = hat * vecs[0:1] * (1.0 + vecs[4:5]) + vecs[3:4]
    low = hidden.astype(bf16)
    h1[...] = low
    cos, sin = cosine[...], sine[...]
    q_t[...] = (turn(nt(wq[0], low), cos, sin) * 0.125).astype(bf16)
    keys = turn(nt(wq[1], low), cos, sin)
    k_t[...] = keys.astype(bf16)
    k_r[...] = keys.T.astype(bf16)
    values = nt(wq[2], low)
    v_t[...] = values.astype(bf16)
    v_r[...] = values.T.astype(bf16)


def project(tok, vecs, wq, cosine, sine):
    length, width = tok.shape
    heads_width = wq.shape[1]
    step = 256
    half = HEAD_DIM // 2
    return pl.pallas_call(
        project_kernel,
        grid=(length // step,),
        out_shape=(
            jax.ShapeDtypeStruct((length, width), bf16),
            jax.ShapeDtypeStruct((heads_width, length), bf16),
            jax.ShapeDtypeStruct((heads_width, length), bf16),
            jax.ShapeDtypeStruct((heads_width, length), bf16),
            jax.ShapeDtypeStruct((length, heads_width), bf16),
            jax.ShapeDtypeStruct((length, heads_width), bf16),
        ),
        in_specs=[
            pl.BlockSpec((step, width), lambda i: (i, 0)),
            pl.BlockSpec(vecs.shape, lambda i: (0, 0)),
            pl.BlockSpec(wq.shape, lambda i: (0, 0, 0)),
            pl.BlockSpec((half, step), lambda i: (0, i)),
            pl.BlockSpec((half, step), lambda i: (0, i)),
        ],
        out_specs=(
            pl.BlockSpec((step, width), lambda i: (i, 0)),
            pl.BlockSpec((heads_width, step), lambda i: (0, i)),
            pl.BlockSpec((heads_width, step), lambda i: (0, i)),
            pl.BlockSpec((heads_width, step), lambda i: (0, i)),
            pl.BlockSpec((step, heads_width), lambda i: (i, 0)),
            pl.BlockSpec((step, heads_width), lambda i: (i, 0)),
        ),
        compiler_params=pltpu.CompilerParams(vmem_limit_bytes=48 * MIB),
        name="project",
    )(tok, vecs, wq, cosine, sine)


def only_head(pair, h):
    row = lax.broadcasted_iota(jnp.int32, pair.shape, 0)
    return jnp.where(row // HEAD_DIM == h, pair, jnp.zeros_like(pair))


def attend_kernel(k_r, q_t, v_t, probs, inv, o_t):
    for h in range(2):
        scores = nn(k_r[...], only_head(q_t[...], h))
        top = jnp.max(scores, axis=0, keepdims=True)
        shifted = jnp.exp(scores - top)
        inverse = 1.0 / jnp.sum(shifted, axis=0, keepdims=True)
        low = shifted.astype(bf16)
        probs[h] = low
        inv[0, h : h + 1, :] = inverse
        rows = slice(h * HEAD_DIM, (h + 1) * HEAD_DIM)
        o_t[rows, :] = (nn(v_t[rows, :], low) * inverse).astype(bf16)


def attend(k_r, q_t, v_t):
    length, heads_width = k_r.shape
    pairs = heads_width // (2 * HEAD_DIM)
    step = 256
    pw = 2 * HEAD_DIM
    return pl.pallas_call(
        attend_kernel,
        grid=(pairs, length // step),
        out_shape=(
            jax.ShapeDtypeStruct((2 * pairs, length, length), bf16),
            jax.ShapeDtypeStruct((pairs, 2, length), f32),
            jax.ShapeDtypeStruct((heads_width, length), bf16),
        ),
        in_specs=[
            pl.BlockSpec((length, pw), lambda p, i: (0, p)),
            pl.BlockSpec((pw, step), lambda p, i: (p, i)),
            pl.BlockSpec((pw, length), lambda p, i: (p, 0)),
        ],
        out_specs=(
            pl.BlockSpec((2, length, step), lambda p, i: (p, 0, i)),
            pl.BlockSpec((1, 2, step), lambda p, i: (p, 0, i)),
            pl.BlockSpec((pw, step), lambda p, i: (p, i)),
        ),
        compiler_params=pltpu.CompilerParams(vmem_limit_bytes=48 * MIB),
        name="attend",
    )(k_r, q_t, v_t)


def sibling_of(cores):
    t = lax.axis_index("tp")
    s = t // cores
    c = lax.rem(t, cores)
    return s, c, {"tp": s * cores + (1 - c)}


def greet(device):
    barrier = pltpu.get_barrier_semaphore()
    pl.semaphore_signal(barrier, inc=1, device_id=device, device_id_type=MESH)
    pl.semaphore_wait(barrier, 1)


def mix_kernel(cores, o_t, wo, tok, vecs, attn, x1, h2, away, got, tbuf, tsem, asem, hsem):
    s, c, sibling = sibling_of(cores)
    half = attn.shape[0]
    own = pl.ds(pl.multiple_of(c * half, 128), half)
    other = pl.ds(pl.multiple_of((1 - c) * half, 128), half)
    tc = pltpu.make_async_copy(tok.at[own], tbuf, tsem)
    tc.start()
    greet(sibling)
    away[...] = tn(o_t[:, other], wo[...])
    send = pltpu.make_async_remote_copy(
        src_ref=away, dst_ref=got, send_sem=asem.at[0], recv_sem=asem.at[1], device_id=sibling, device_id_type=MESH)
    send.start()
    attn[...] = tn(o_t[:, own], wo[...])
    tc.wait()
    send.wait()
    step = 128

    @pl.loop(0, half // step)
    def _(i):
        r = pl.ds(pl.multiple_of(i * step, step), step)
        total = attn[r] + got[r]
        attn[r] = total
        rows = tbuf[r].astype(f32) + vecs[5:6] * total
        x1[r] = rows
        hat, _ = normalize(rows)
        hidden = hat * vecs[1:2] * (1.0 + vecs[7:8]) + vecs[6:7]
        h2[pl.ds(pl.multiple_of(c * half + i * step, step), step)] = hidden.astype(bf16)

    back = pltpu.make_async_remote_copy(
        src_ref=h2.at[own], dst_ref=h2.at[own], send_sem=hsem.at[0], recv_sem=hsem.at[1],
        device_id=sibling, device_id_type=MESH)
    back.start()
    back.wait()


def mix(cores, o_t, wo, tok, vecs):
    length, width = tok.shape
    half = length // cores
    return pl.pallas_call(
        functools.partial(mix_kernel, cores),
        out_shape=(
            jax.ShapeDtypeStruct((half, width), f32),
            jax.ShapeDtypeStruct((half, width), f32),
            jax.ShapeDtypeStruct((length, width), bf16),
        ),
        in_specs=[VMEM, VMEM, ANY, VMEM],
        out_specs=(VMEM,) * 3,
        scratch_shapes=[
            pltpu.VMEM((half, width), f32),
            pltpu.VMEM((half, width), f32),
            pltpu.VMEM((half, width), bf16),
            pltpu.SemaphoreType.DMA,
            pltpu.SemaphoreType.DMA((2,)),
            pltpu.SemaphoreType.DMA((2,)),
        ],
        compiler_params=pltpu.CompilerParams(collective_id=2, has_side_effects=True, vmem_limit_bytes=48 * MIB),
        name="attention_mix",
    )(o_t, wo, tok, vecs)


def feed_kernel(h2, gy, vecs, bias, wu, wd, mlp, dh2, gu, gd, gb, z_s, du_s, gm_s, b_s):
    length, width = h2.shape
    hidden = wu.shape[0]
    chunk = width
    step = 256
    b_s[...] = jnp.zeros_like(b_s)

    @pl.loop(0, length // step)
    def _(i):
        r = pl.ds(pl.multiple_of(i * step, step), step)
        rows = h2[r]
        gm = (gy[r].astype(f32) * vecs[8:9]).astype(bf16)
        gm_s[r] = gm
        forward = jnp.zeros((step, width), f32)
        backward = jnp.zeros((step, width), f32)
        for j in range(hidden // chunk):
            cols = slice(j * chunk, (j + 1) * chunk)
            u = nt(rows, wu[cols]) + bias[:, cols]
            square = u * u
            inner = jnp.tanh(gelu_a * (u + gelu_b * square * u))
            z = (0.5 * u * (1.0 + inner)).astype(bf16)
            slope = 0.5 * (1.0 + inner) + 0.5 * u * (1.0 - inner * inner) * gelu_a * (1.0 + 3.0 * gelu_b * square)
            du = (nt(gm, wd[cols]) * slope).astype(bf16)
            z_s[r, cols] = z
            du_s[r, cols] = du
            b_s[:, cols] += fold(du.astype(f32))
            forward += nn(z, wd[cols])
            backward += nn(du, wu[cols])
        mlp[r] = forward.astype(bf16)
        dh2[r] = backward.astype(bf16)

    gb[...] = jnp.sum(b_s[...], axis=0, keepdims=True)
    for j in range(hidden // step):
        cols = slice(j * step, (j + 1) * step)
        gd[cols] = tn(z_s[:, cols], gm_s[...]).astype(bf16)
        gu[cols] = tn(du_s[:, cols], h2[...]).astype(bf16)


def feed(h2, gy, vecs, bias, wu, wd):
    length, width = h2.shape
    hidden = wu.shape[0]
    return pl.pallas_call(
        feed_kernel,
        out_shape=(
            jax.ShapeDtypeStruct((length, width), bf16),
            jax.ShapeDtypeStruct((length, width), bf16),
            jax.ShapeDtypeStruct((hidden, width), bf16),
            jax.ShapeDtypeStruct((hidden, width), bf16),
            jax.ShapeDtypeStruct((1, hidden), f32),
        ),
        in_specs=[VMEM] * 6,
        out_specs=(VMEM,) * 5,
        scratch_shapes=[
            pltpu.VMEM((length, hidden), bf16),
            pltpu.VMEM((length, hidden), bf16),
            pltpu.VMEM((length, width), bf16),
            pltpu.VMEM((8, hidden), f32),
        ],
        compiler_params=pltpu.CompilerParams(vmem_limit_bytes=56 * MIB),
        name="feed_forward",
    )(h2, gy, vecs, bias, wu, wd)


def middle_kernel(cores, mlp, dh2, x1, attn, gy, vecs, out, dx1, ga, stats, got, acc, msem, gsem):
    s, c, sibling = sibling_of(cores)
    half = x1.shape[0]
    own = pl.ds(pl.multiple_of(c * half, 128), half)
    other = pl.ds(pl.multiple_of((1 - c) * half, 128), half)
    greet(sibling)
    sends = []
    for i, ref in enumerate((mlp, dh2)):
        cp = pltpu.make_async_remote_copy(
            src_ref=ref.at[other], dst_ref=got.at[i], send_sem=msem.at[0, i], recv_sem=msem.at[1, i],
            device_id=sibling, device_id_type=MESH)
        cp.start()
        sends.append(cp)
    acc[...] = jnp.zeros_like(acc)
    for cp in sends:
        cp.wait()
    step = 128

    @pl.loop(0, half // step)
    def _(i):
        r = pl.ds(pl.multiple_of(i * step, step), step)
        g = pl.ds(pl.multiple_of(c * half + i * step, step), step)
        rows = x1[r]
        branch = mlp[g].astype(f32) + got[0, r].astype(f32) + vecs[2:3]
        out[r] = (rows + vecs[8:9] * branch).astype(bf16)
        grad = gy[g].astype(f32)
        dh = dh2[g].astype(f32) + got[1, r].astype(f32)
        hat, inverse = normalize(rows)
        acc[0] += fold(dh)
        acc[1] += fold(dh * hat)
        total = grad + norm_pull(dh * (vecs[1:2] * (1.0 + vecs[7:8])), hat, inverse)
        dx1[r] = total
        acc[2] += fold(total * attn[r])
        acc[3] += fold(grad * branch)
        acc[4] += fold((vecs[8:9] * grad).astype(bf16).astype(f32))
        ga[g] = (vecs[5:6] * total).astype(bf16)

    back = pltpu.make_async_remote_copy(
        src_ref=ga.at[own], dst_ref=ga.at[own], send_sem=gsem.at[0], recv_sem=gsem.at[1],
        device_id=sibling, device_id_type=MESH)
    back.start()
    stats[...] = jnp.zeros_like(stats)
    for i in range(5):
        stats[i : i + 1] = jnp.sum(acc[i], axis=0, keepdims=True)
    back.wait()


def middle(cores, mlp, dh2, x1, attn, gy, vecs):
    length, width = mlp.shape
    half = length // cores
    return pl.pallas_call(
        functools.partial(middle_kernel, cores),
        out_shape=(
            jax.ShapeDtypeStruct((half, width), bf16),
            jax.ShapeDtypeStruct((half, width), f32),
            jax.ShapeDtypeStruct((length, width), bf16),
            jax.ShapeDtypeStruct((8, width), f32),
        ),
        in_specs=[VMEM] * 6,
        out_specs=(VMEM,) * 4,
        scratch_shapes=[
            pltpu.VMEM((2, half, width), bf16),
            pltpu.VMEM((5, 8, width), f32),
            pltpu.SemaphoreType.DMA((2, 2)),
            pltpu.SemaphoreType.DMA((2,)),
        ],
        compiler_params=pltpu.CompilerParams(collective_id=3, has_side_effects=True, vmem_limit_bytes=48 * MIB),
        name="middle",
    )(mlp, dh2, x1, attn, gy, vecs)


def pull_kernel(ga, wo, o_t, inv, probs, q_t, k_t, v_t, v_r, cosine, sine, h1, wq, dh1, gq, go, do_s, ds_s, dqkv):
    p = pl.program_id(0)
    length, width = ga.shape
    pw = 2 * HEAD_DIM
    heads_width = wq.shape[1]
    step = 256
    do_t = nt(wo[...], ga[...])
    go[...] = nn(o_t[...], ga[...]).astype(bf16)
    for h in range(2):
        rows = slice(h * HEAD_DIM, (h + 1) * HEAD_DIM)
        do_s[rows] = (do_t[rows] * inv[0, h : h + 1, :]).astype(bf16)
    raw = []
    for h in range(2):
        rows = slice(h * HEAD_DIM, (h + 1) * HEAD_DIM)
        delta = jnp.sum(do_s[rows].astype(f32) * o_t[rows].astype(f32), axis=0, keepdims=True)
        dq = []
        for i in range(length // step):
            cols = slice(i * step, (i + 1) * step)
            dp = nn(v_r[...], only_head(do_s[:, cols], h))
            ds = (probs[h, :, cols].astype(f32) * (dp - delta[:, cols])).astype(bf16)
            ds_s[:, cols] = ds
            dq.append(nn(k_t[rows], ds))
        dk = nt(q_t[rows], ds_s[...])
        dv = nt(do_s[rows], probs[h])
        raw.append((jnp.concatenate(dq, axis=1) * 0.125, dk, dv))
    cos, sin = cosine[...], sine[...]
    for k in range(3):
        both = jnp.concatenate([raw[0][k], raw[1][k]], axis=0)
        if k < 2:
            both = turn(both, cos, -sin)
        at = pl.multiple_of(k * heads_width + p * pw, pw)
        dqkv[pl.ds(at, pw)] = both.astype(bf16)

    @pl.when(p == pl.num_programs(0) - 1)
    def _():
        for k in range(3):
            part = slice(k * heads_width, (k + 1) * heads_width)
            gq[k] = nn(dqkv[part], h1[...]).astype(bf16)

        @pl.loop(0, length // step)
        def _(i):
            r = pl.ds(pl.multiple_of(i * step, step), step)
            total = jnp.zeros((step, width), f32)
            for k in range(3):
                part = slice(k * heads_width, (k + 1) * heads_width)
                total += tn(dqkv[part, r], wq[k])
            dh1[r] = total.astype(bf16)


def pull_attention(ga, wo, o_t, inv, probs, q_t, k_t, v_r, cosine, sine, h1, wq):
    length, width = ga.shape
    heads_width = wq.shape[1]
    pw = 2 * HEAD_DIM
    pairs = heads_width // pw
    half = HEAD_DIM // 2

    def body(ga, wo, o_t, inv, probs, q_t, k_t, v_r, cosine, sine, h1, wq, *rest):
        return pull_kernel(ga, wo, o_t, inv, probs, q_t, k_t, None, v_r, cosine, sine, h1, wq, *rest)

    return pl.pallas_call(
        body,
        grid=(pairs,),
        out_shape=(
            jax.ShapeDtypeStruct((length, width), bf16),
            jax.ShapeDtypeStruct((3, heads_width, width), bf16),
            jax.ShapeDtypeStruct((heads_width, width), bf16),
        ),
        in_specs=[
            pl.BlockSpec((length, width), lambda p: (0, 0)),
            pl.BlockSpec((pw, width), lambda p: (p, 0)),
            pl.BlockSpec((pw, length), lambda p: (p, 0)),
            pl.BlockSpec((1, 2, length), lambda p: (p, 0, 0)),
            pl.BlockSpec((2, length, length), lambda p: (p, 0, 0)),
            pl.BlockSpec((pw, length), lambda p: (p, 0)),
            pl.BlockSpec((pw, length), lambda p: (p, 0)),
            pl.BlockSpec((length, pw), lambda p: (0, p)),
            pl.BlockSpec((half, length), lambda p: (0, 0)),
            pl.BlockSpec((half, length), lambda p: (0, 0)),
            pl.BlockSpec((length, width), lambda p: (0, 0)),
            pl.BlockSpec((3, heads_width, width), lambda p: (0, 0, 0)),
        ],
        out_specs=(
            pl.BlockSpec((length, width), lambda p: (0, 0)),
            pl.BlockSpec((3, heads_width, width), lambda p: (0, 0, 0)),
            pl.BlockSpec((pw, width), lambda p: (p, 0)),
        ),
        scratch_shapes=[
            pltpu.VMEM((pw, length), bf16),
            pltpu.VMEM((length, length), bf16),
            pltpu.VMEM((3 * heads_width, length), bf16),
        ],
        compiler_params=pltpu.CompilerParams(vmem_limit_bytes=56 * MIB),
        name="attention_pull",
    )(ga, wo, o_t, inv, probs, q_t, k_t, v_r, cosine, sine, h1, wq)


def last_kernel(cores, spans, dh1, dx1, tok, out, vecs, stats, gb, cond, block_out, grad_out, shared,
                got, tbuf, grad, acc, small, dsem, tsem, osem, fsem, lsem, vsem):
    t, d = lax.axis_index("tp"), lax.rem(lax.axis_index("dp"), spans)
    n_tp = shared.shape[0]
    s, c, sibling = sibling_of(cores)
    across = {"tp": (1 - s) * cores + c}
    half = dx1.shape[0]
    own = pl.ds(pl.multiple_of(c * half, 128), half)
    other = pl.ds(pl.multiple_of((1 - c) * half, 128), half)
    barrier = pltpu.get_barrier_semaphore()
    others = []
    for dt in range(n_tp):
        for dd in range(spans):
            if dt or dd:
                dev = {"tp": lax.rem(t + dt, n_tp)}
                if spans > 1:
                    dev["dp"] = lax.rem(d + dd, spans)
                others.append(dev)
    for dev in others:
        pl.semaphore_signal(barrier, inc=1, device_id=dev, device_id_type=MESH)
    tc = pltpu.make_async_copy(tok.at[own], tbuf, tsem)
    tc.start()
    pl.semaphore_wait(barrier, len(others))

    def spread(kind, source, target):
        copies = []
        for i, dev in enumerate((sibling, across)):
            copies.append(pltpu.make_async_remote_copy(
                src_ref=source, dst_ref=target.at[s, own], send_sem=osem.at[0, kind, i], recv_sem=osem.at[1, kind, i],
                device_id=dev, device_id_type=MESH))
            copies[i].start()
        local = pltpu.make_async_copy(source, target.at[s, own], lsem.at[kind])
        local.start()
        return copies, local

    def pass_on(kind, copies, target):
        copies[1].wait_recv()
        forward = pltpu.make_async_remote_copy(
            src_ref=target.at[1 - s, own], dst_ref=target.at[1 - s, own], send_sem=fsem.at[0, kind],
            recv_sem=fsem.at[1, kind], device_id=sibling, device_id_type=MESH)
        forward.start()
        return forward

    first = pltpu.make_async_remote_copy(
        src_ref=dh1.at[other], dst_ref=got, send_sem=dsem.at[0], recv_sem=dsem.at[1],
        device_id=sibling, device_id_type=MESH)
    first.start()
    ocopies, olocal = spread(0, out, block_out)
    acc[...] = jnp.zeros_like(acc)
    tc.wait()
    first.wait()
    step = 128

    @pl.loop(0, half // step)
    def _(i):
        r = pl.ds(pl.multiple_of(i * step, step), step)
        g = pl.ds(pl.multiple_of(c * half + i * step, step), step)
        dh = dh1[g].astype(f32) + got[r].astype(f32)
        hat, inverse = normalize(tbuf[r].astype(f32))
        acc[0] += fold(dh)
        acc[1] += fold(dh * hat)
        total = dx1[r] + norm_pull(dh * (vecs[0:1] * (1.0 + vecs[4:5])), hat, inverse)
        grad[r] = total.astype(bf16)

    gcopies, glocal = spread(1, grad, grad_out)
    shift1 = jnp.sum(acc[0], axis=0, keepdims=True)
    turn1 = jnp.sum(acc[1], axis=0, keepdims=True)
    small[...] = jnp.zeros_like(small)
    small[0:1] = shift1
    small[1:2] = turn1 * vecs[0:1]
    small[2:3] = stats[2:3]
    small[3:4] = stats[0:1]
    small[4:5] = stats[1:2] * vecs[1:2]
    small[5:6] = stats[3:4]
    small[6:7] = turn1 * (1.0 + vecs[4:5])
    small[7:8] = stats[1:2] * (1.0 + vecs[7:8])
    small[8:9] = stats[4:5]
    small[9:11] = gb[...]
    small[11:12, 0 : cond.shape[1]] = cond[...]
    shared[t, d] = small[...]
    vsends = []
    for i, dev in enumerate(others):
        cp = pltpu.make_async_remote_copy(
            src_ref=small, dst_ref=shared.at[t, d], send_sem=vsem.at[0, i], recv_sem=vsem.at[1, i],
            device_id=dev, device_id_type=MESH)
        cp.start()
        vsends.append(cp)
    forwards = [pass_on(0, ocopies, block_out), pass_on(1, gcopies, grad_out)]
    for copies, local, forward in zip((ocopies, gcopies), (olocal, glocal), forwards):
        copies[0].wait()
        copies[1].wait_send()
        local.wait()
        forward.wait()
    for cp in vsends:
        cp.wait()


def last(cores, spans, seqs, dh1, dx1, tok, out, vecs, stats, gb, cond):
    length, width = tok.shape
    n_tp = lax.axis_size("tp")
    half = length // cores
    return pl.pallas_call(
        functools.partial(last_kernel, cores, spans),
        out_shape=(
            jax.ShapeDtypeStruct((seqs, length, width), bf16),
            jax.ShapeDtypeStruct((seqs, length, width), bf16),
            jax.ShapeDtypeStruct((n_tp, spans, 16, width), f32),
        ),
        in_specs=[VMEM, VMEM, ANY, ANY, VMEM, VMEM, VMEM, VMEM],
        out_specs=(ANY, ANY, VMEM),
        scratch_shapes=[
            pltpu.VMEM((half, width), bf16),
            pltpu.VMEM((half, width), bf16),
            pltpu.VMEM((half, width), bf16),
            pltpu.VMEM((2, 8, width), f32),
            pltpu.VMEM((16, width), f32),
            pltpu.SemaphoreType.DMA((2,)),
            pltpu.SemaphoreType.DMA,
            pltpu.SemaphoreType.DMA((2, 2, 2)),
            pltpu.SemaphoreType.DMA((2, 2)),
            pltpu.SemaphoreType.DMA((2,)),
            pltpu.SemaphoreType.DMA((2, spans * n_tp - 1)),
        ],
        compiler_params=pltpu.CompilerParams(collective_id=4, has_side_effects=True, vmem_limit_bytes=48 * MIB),
        name="last_norm",
    )(dh1, dx1, tok, out, vecs, stats, gb, cond)


def step_kernel(cores, gq, go, gu, gd, wi, wb, mi, mb, vi, vb, ea, es, eb,
                gsum, total, ta, ts, tb,
                grads, wts, firsts, seconds, got_a, send_b, got_b, diff, got_p, got_h, a_p, a_h, s_all, b_all, a_low, s_low, b_low,
                lsem, asem, bsem, psem, hsem, fsem, esem, ap_sem, ah_sem, af_sem, ss_sem, bs_sem):
    t, d, g = lax.axis_index("tp"), lax.axis_index("dp"), lax.axis_index("grp")
    s = t // cores
    c = lax.rem(t, cores)
    rows, cols = wi.shape[1:]
    xdev = {"dp": 1 - d}
    ydev = {"tp": (1 - s) * cores + c}
    inner = jnp.logical_or(g == 1, g == 2)
    outer = jnp.logical_not(inner)
    low_side = g < 2
    pair = jnp.where(g == 0, 1, jnp.where(g == 1, 0, jnp.where(g == 2, 3, 2)))
    pdev = {"grp": pair}
    mdev = {"grp": 3 - g}
    mine = jnp.where(g == 1, 0, 1)
    hrows = rows // 2

    def remote(source, target, send, recv, device):
        return pltpu.make_async_remote_copy(
            src_ref=source, dst_ref=target, send_sem=send, recv_sem=recv, device_id=device, device_id_type=MESH)

    def r_at(ss):
        return pl.ds(pl.multiple_of(ss * rows, 16), rows)

    def c_at(dd):
        return pl.ds(pl.multiple_of(dd * cols, 128), cols)

    loads = []
    for a in range(12):
        ref = gq.at[a] if a < 3 else gu.at[a - 3] if a < 7 else go if a == 7 else gd.at[a - 8]
        loads.append(pltpu.make_async_copy(ref, grads.at[a], lsem.at[a]))
    for i, (src, dst) in enumerate(((wi, wts), (mi, firsts), (vi, seconds))):
        loads.append(pltpu.make_async_copy(src, dst.at[pl.ds(0, 7)], lsem.at[12 + i]))
    for i, (src, dst) in enumerate(((wb, wts), (mb, firsts), (vb, seconds))):
        loads.append(pltpu.make_async_copy(src, dst.at[pl.ds(7, 5)], lsem.at[15 + i]))
    for cp in loads:
        cp.start()

    barrier = pltpu.get_barrier_semaphore()
    for dev in (xdev, ydev, {"grp": lax.rem(g + 1, 4)}, {"grp": lax.rem(g + 2, 4)}, {"grp": lax.rem(g + 3, 4)}):
        pl.semaphore_signal(barrier, inc=1, device_id=dev, device_id_type=MESH)
    pl.semaphore_wait(barrier, 5)

    a_low[...] = ea[...].astype(bf16)
    s_low[...] = es[...].astype(bf16).astype(f32)
    b_low[...] = eb[...].astype(bf16).astype(f32)
    tiny = []
    for i in range(3):
        dev = {"grp": lax.rem(g + 1 + i, 4)}
        tiny.append(remote(s_low, s_all.at[g], ss_sem.at[0, i], ss_sem.at[1, i], dev))
        tiny.append(remote(b_low, b_all.at[g], bs_sem.at[0, i], bs_sem.at[1, i], dev))
    for cp in tiny:
        cp.start()
    s_all[g] = s_low[...]
    b_all[g] = b_low[...]

    def first_send(a, k):
        if a % 2 == 0:
            return remote(grads.at[a, r_at(1 - s), pl.ds(k * cols, cols)], got_a.at[a, k], asem.at[0, a, k], asem.at[1, a, k], ydev)
        return remote(grads.at[a, pl.ds(k * rows, rows), c_at(1 - d)], got_a.at[a, k], asem.at[0, a, k], asem.at[1, a, k], xdev)

    def first_wait(a):
        for k in range(2):
            remote(got_a.at[a, k], got_a.at[a, k], asem.at[0, a, k], asem.at[1, a, k], xdev).wait()

    for a in range(12):
        loads[a].wait()
        for k in range(2):
            first_send(a, k).start()
    for cp in loads[12:]:
        cp.wait()

    def second_send(a, parity):
        dev = xdev if parity == 0 else ydev
        return remote(send_b.at[a], got_b.at[a], bsem.at[0, a], bsem.at[1, a], dev)

    def pair_send(a):
        return remote(diff.at[a], got_p.at[a], psem.at[0, a], psem.at[1, a], pdev)

    def h_at(k):
        return pl.ds(pl.multiple_of(k * hrows, 16), hrows)

    def half_send(a):
        return remote(got_p.at[a, h_at(1 - mine)], got_h.at[a], hsem.at[0, a], hsem.at[1, a], mdev)

    def final_mid(a):
        return remote(total.at[a, h_at(mine)], total.at[a, h_at(mine)], fsem.at[0, a, 0], fsem.at[1, a, 0], mdev)

    def final_pair(a):
        return remote(total.at[a, h_at(mine)], total.at[a, h_at(mine)], fsem.at[0, a, 1], fsem.at[1, a, 1], pdev)

    def final_pass(a):
        return remote(total.at[a, h_at(1 - mine)], total.at[a, h_at(1 - mine)], fsem.at[0, a, 2], fsem.at[1, a, 2], pdev)

    def stage_b(a, parity):
        first_wait(a)
        if parity == 0:
            send_b[a] = (grads[a, r_at(s), c_at(1 - d)].astype(f32) + got_a[a, 1 - d].astype(f32)).astype(bf16)
        else:
            send_b[a] = (grads[a, r_at(1 - s), c_at(d)].astype(f32) + got_a[a, 1 - s].astype(f32)).astype(bf16)
        second_send(a, parity).start()

    def stage_c(a, parity):
        second_send(a, parity).wait()
        keep = got_a[a, d] if parity == 0 else got_a[a, s]
        gradient = grads[a, r_at(s), c_at(d)].astype(f32) + keep.astype(f32) + got_b[a].astype(f32)
        gsum[a] = gradient
        first_new, second_new = adam_parts(gradient, firsts[a], seconds[a])
        diff[a] = adam_diff(wts[a], first_new, second_new, rate_matrix, decay_rate).astype(bf16)

        @pl.when(outer)
        def _():
            pair_send(a).start()

    def stage_d(a):
        pair_send(a).wait_recv()
        got_p[a] = (diff[a].astype(f32) + got_p[a].astype(f32)).astype(bf16)
        half_send(a).start()

    def stage_e(a):
        half_send(a).wait_recv()
        total[a, h_at(mine)] = (got_p[a, h_at(mine)].astype(f32) + got_h[a].astype(f32)).astype(bf16)
        final_mid(a).start()
        final_pair(a).start()

    def stage_f(a):
        remote(got_h.at[a], got_h.at[a], fsem.at[0, a, 0], fsem.at[1, a, 0], mdev).wait_recv()
        final_pass(a).start()

    n = 6

    @pl.loop(0, n + 4)
    def _(i):
        @pl.when(i < n)
        def _():
            for k in range(2):
                stage_b(2 * i + k, k)

        @pl.when(jnp.logical_and(i >= 1, i < n + 1))
        def _():
            for k in range(2):
                stage_c(2 * (i - 1) + k, k)

        @pl.when(jnp.logical_and(inner, jnp.logical_and(i >= 2, i < n + 2)))
        def _():
            for k in range(2):
                stage_d(2 * (i - 2) + k)

        @pl.when(jnp.logical_and(inner, jnp.logical_and(i >= 3, i < n + 3)))
        def _():
            for k in range(2):
                stage_e(2 * (i - 3) + k)

        @pl.when(jnp.logical_and(inner, i >= 4))
        def _():
            for k in range(2):
                stage_f(2 * (i - 4) + k)

    ah = a_low.shape[0] // 2

    def ada_at(ref, k):
        return ref.at[pl.ds(k * ah, ah)]

    a_pair = remote(a_low, a_p, ap_sem.at[0], ap_sem.at[1], pdev)
    a_half = remote(ada_at(a_p, 1 - mine), a_h, ah_sem.at[0], ah_sem.at[1], mdev)
    a_mid = remote(ada_at(ta, mine), ada_at(ta, mine), af_sem.at[0, 0], af_sem.at[1, 0], mdev)
    a_out = remote(ada_at(ta, mine), ada_at(ta, mine), af_sem.at[0, 1], af_sem.at[1, 1], pdev)
    a_pass = remote(ada_at(ta, 1 - mine), ada_at(ta, 1 - mine), af_sem.at[0, 2], af_sem.at[1, 2], pdev)

    @pl.when(outer)
    def _():
        a_pair.start()
        a_pair.wait_send()
        remote(a_h, a_h, af_sem.at[0, 1], af_sem.at[1, 1], pdev).wait_recv()
        remote(a_h, a_h, af_sem.at[0, 2], af_sem.at[1, 2], pdev).wait_recv()

        @pl.loop(0, 12)
        def _(a):
            pair_send(a).wait_send()
            remote(got_h.at[a], got_h.at[a], fsem.at[0, a, 1], fsem.at[1, a, 1], pdev).wait_recv()
            remote(got_h.at[a], got_h.at[a], fsem.at[0, a, 2], fsem.at[1, a, 2], pdev).wait_recv()

    @pl.when(inner)
    def _():
        a_pair.wait_recv()
        a_p[...] = (a_p[...].astype(f32) + a_low[...].astype(f32)).astype(bf16)
        a_half.start()
        a_half.wait()
        ta[pl.ds(mine * ah, ah)] = (a_p[pl.ds(mine * ah, ah)].astype(f32) + a_h[...].astype(f32)).astype(bf16)
        a_mid.start()
        a_out.start()
        a_mid.wait()
        a_pass.start()
        a_out.wait_send()
        a_pass.wait_send()

        @pl.loop(0, 12)
        def _(a):
            half_send(a).wait_send()
            final_mid(a).wait_send()
            final_pair(a).wait_send()
            final_pass(a).wait_send()

    for cp in tiny:
        cp.wait()
    ts[...] = (s_all[0] + s_all[1]) + (s_all[2] + s_all[3])
    tb[...] = (b_all[0] + b_all[1]) + (b_all[2] + b_all[3])


def step_exchange(cores, gq, go, gu, gd, wi, wb, mi, mb, vi, vb, ea, es, eb):
    rows, cols = wi.shape[1:]
    slot = (12, rows, cols)
    dma = pltpu.SemaphoreType.DMA
    return pl.pallas_call(
        functools.partial(step_kernel, cores),
        out_shape=(
            jax.ShapeDtypeStruct(slot, f32),
            jax.ShapeDtypeStruct(slot, bf16),
            jax.ShapeDtypeStruct(ea.shape, bf16),
            jax.ShapeDtypeStruct(es.shape, f32),
            jax.ShapeDtypeStruct(eb.shape, f32),
        ),
        in_specs=[ANY] * 10 + [VMEM] * 3,
        out_specs=(VMEM,) * 5,
        scratch_shapes=[
            pltpu.VMEM((12, 2 * rows, 2 * cols), bf16),
            pltpu.VMEM(slot, f32),
            pltpu.VMEM(slot, f32),
            pltpu.VMEM(slot, f32),
            pltpu.VMEM((12, 2, rows, cols), bf16),
            pltpu.VMEM(slot, bf16),
            pltpu.VMEM(slot, bf16),
            pltpu.VMEM(slot, bf16),
            pltpu.VMEM(slot, bf16),
            pltpu.VMEM((12, rows // 2, cols), bf16),
            pltpu.VMEM(ea.shape, bf16),
            pltpu.VMEM((ea.shape[0] // 2,) + ea.shape[1:], bf16),
            pltpu.VMEM((4,) + es.shape, f32),
            pltpu.VMEM((4,) + eb.shape, f32),
            pltpu.VMEM(ea.shape, bf16),
            pltpu.VMEM(es.shape, f32),
            pltpu.VMEM(eb.shape, f32),
            dma((18,)),
            dma((2, 12, 2)),
            dma((2, 12)),
            dma((2, 12)),
            dma((2, 12)),
            dma((2, 12, 3)),
            dma((2,)),
            dma((2,)),
            dma((2,)),
            dma((2, 3)),
            dma((2, 3)),
            dma((2, 3)),
        ],
        compiler_params=pltpu.CompilerParams(collective_id=5, has_side_effects=True, vmem_limit_bytes=58 * MIB),
        name="step_exchange",
    )(gq, go, gu, gd, wi, wb, mi, mb, vi, vb, ea, es, eb)


def angle_tables(length):
    half = HEAD_DIM // 2
    frequency = np.float32(10000.0) ** (np.float32(-2.0) * np.arange(half, dtype=np.float32) / np.float32(HEAD_DIM))
    angles = frequency[:, None] * np.arange(length, dtype=np.float32)[None, :]
    return jnp.asarray(np.cos(angles)), jnp.asarray(np.sin(angles))


def on_device(
    tokens, sigma_index, absorbed, cotangent, time_table,
    in_weight, back_weight, ada_weight, small_params, up_bias,
    in_first, back_first, ada_first, small_first, bias_first,
    in_second, back_second, ada_second, small_second, bias_second,
    in_moment, back_moment, ada_moment, small_moment, bias_moment,
):
    n_tp, n_dp, n_grp = lax.axis_size("tp"), lax.axis_size("dp"), lax.axis_size("grp")
    seqs, length, width = tokens.shape
    cores = n_tp // seqs
    part = in_weight.shape[2]
    heads_width = seqs * part
    direct = n_dp == 2 and n_grp == 4 and seqs == 2 and cores == 2
    t, d = lax.axis_index("tp"), lax.axis_index("dp")
    s = t // cores
    c = lax.rem(t, cores)
    groups = [[a * cores + b for a in range(seqs)] for b in range(cores)]

    table_ids = jnp.arange(time_table.shape[0], dtype=jnp.int32)
    onehot = (sigma_index[:, None] == table_ids[None, :]).astype(f32)
    condition = jax.nn.silu(jnp.dot(onehot, time_table, precision=highest))
    cond_low = condition.astype(bf16).astype(f32)
    cond_width = cond_low.shape[1]

    wi_t = jnp.transpose(in_weight, (1, 2, 0))
    wa_t = jnp.transpose(ada_weight, (1, 0, 2))
    tok = lax.dynamic_index_in_dim(tokens, s, 0, keepdims=False)
    flags = lax.dynamic_index_in_dim(absorbed, s, 0, keepdims=False)
    gy = lax.dynamic_index_in_dim(cotangent, s, 0, keepdims=False) * flags.astype(bf16)[:, None]
    cond_row = lax.dynamic_index_in_dim(cond_low, s, 0, keepdims=True)

    if direct:
        cond_in = jnp.zeros((2, 8, cond_width // 2), f32)
        cond_in = cond_in.at[:, :seqs].set(jnp.transpose(cond_low.reshape(seqs, 2, cond_width // 2), (1, 0, 2)))
        mod_parts, ps_all, bu_all = exchange_modulation(cores, cond_in, wa_t, small_params, up_bias)
        small_rows = jnp.transpose(ps_all, (1, 0, 2)).reshape(9, width)
        mod_rows = jnp.transpose(mod_parts[:, :6], (1, 0, 2)).reshape(6, width) + small_rows[3:9]
        bias_row = jnp.transpose(bu_all, (2, 0, 1, 3)).reshape(1, 4 * heads_width)
        wq, wo, wu, wd = gather_weights(cores, wi_t.astype(bf16), back_weight.astype(bf16))
    else:
        def over_tp(x, axis):
            return lax.all_gather(x, "tp", axis=axis, tiled=True, axis_index_groups=groups)

        wi_all = over_tp(lax.all_gather(wi_t.astype(bf16), "dp", axis=2, tiled=True), 1)
        wb_all = over_tp(lax.all_gather(back_weight.astype(bf16), "dp", axis=2, tiled=True), 1)
        wq, wo, wu, wd = wi_all[:3], wb_all[0], wi_all[3:], wb_all[1:]
        bu_all = over_tp(lax.all_gather(up_bias.astype(bf16), "dp", axis=1, tiled=True)[None], 0)
        bias_row = jnp.transpose(bu_all, (1, 0, 2)).reshape(1, 4 * heads_width).astype(f32)
        small_rows = lax.all_gather(small_params.astype(bf16), "dp", axis=1, tiled=True).astype(f32)
        wa_all = lax.all_gather(ada_weight.astype(bf16), "dp", axis=0, tiled=True)
        mod_part = jnp.einsum("sc,cad->sad", cond_low.astype(bf16), wa_all, preferred_element_type=f32)
        mod_all = lax.all_gather(mod_part, "tp", axis=2, tiled=True)
        mod_rows = lax.dynamic_index_in_dim(mod_all, s, 0, keepdims=False) + small_rows[3:9]

    vecs = jnp.concatenate([small_rows[0:3], mod_rows, jnp.zeros((7, width), f32)], axis=0)
    cosine, sine = angle_tables(length)
    wu = wu.reshape(4 * heads_width, width)
    wd = wd.reshape(4 * heads_width, width)

    h1, q_t, k_t, v_t, k_r, v_r = project(tok, vecs, wq, cosine, sine)
    probs, inv, o_t = attend(k_r, q_t, v_t)
    attn, x1, h2 = mix(cores, o_t, wo, tok, vecs)
    mlp, dh2, gu, gd, gb = feed(h2, gy, vecs, bias_row, wu, wd)
    out, dx1, ga, stats = middle(cores, mlp, dh2, x1, attn, gy, vecs)
    dh1, gq, go = pull_attention(ga, wo, o_t, inv, probs, q_t, k_t, v_r, cosine, sine, h1, wq)
    gb = gb.reshape(2, width)
    gu = gu.reshape(4, heads_width, width)
    gd = gd.reshape(4, heads_width, width)
    block_out, grad_low, shared = last(cores, 2 if direct else 1, seqs, dh1, dx1, tok, out, vecs, stats, gb, cond_row)
    input_grad = grad_low.astype(f32)

    if not direct:
        shared = lax.all_gather(shared[:, 0], "dp", axis=1)
    by_seq = shared.reshape(seqs, cores, n_dp, 16, width).sum(axis=1)
    dmod = by_seq[:, :, 0:6]
    conds = shared.reshape(seqs, cores, n_dp, 16, width)[:, 0, :, 11, :cond_width]
    small_grad = jnp.concatenate([by_seq[:, :, 6:9].sum(axis=(0, 1)), dmod.sum(axis=(0, 1))], axis=0)
    bias_sum = shared.reshape(seqs, cores, n_dp, 16, width)[:, :, :, 9:11].sum(axis=(0, 2))
    bias_sum = bias_sum.reshape(cores, 4, seqs, part)
    mine = lax.dynamic_index_in_dim(lax.dynamic_index_in_dim(bias_sum, c, 0, keepdims=False), s, 1, keepdims=False)
    bias_grad = lax.dynamic_slice_in_dim(mine, d * (part // n_dp), part // n_dp, 1)
    small_shard = lax.dynamic_slice_in_dim(small_grad, d * (width // n_dp), width // n_dp, 1)
    dmod_cols = lax.dynamic_slice_in_dim(dmod, t * part, part, 3)
    cond_cols = lax.dynamic_slice_in_dim(conds, d * (cond_width // n_dp), cond_width // n_dp, 2)
    ada_grad = jnp.sum(cond_cols[:, :, None, :, None] * dmod_cols[:, :, :, None, :], axis=(0, 1))

    am, av = jnp.transpose(ada_first[0], (1, 0, 2)), jnp.transpose(ada_second[0], (1, 0, 2))
    ada_m, ada_v = adam_parts(ada_grad, am, av)
    ada_d = adam_diff(wa_t, ada_m, ada_v, rate_matrix, decay_rate)
    small_m, small_v = adam_parts(small_shard, small_first[0], small_second[0])
    small_d = adam_diff(small_params, small_m, small_v, rate_small, 0.0)
    bias_m, bias_v = adam_parts(bias_grad, bias_first[0], bias_second[0])
    bias_d = adam_diff(up_bias, bias_m, bias_v, rate_small, 0.0)

    mi, vi = jnp.transpose(in_first[0], (1, 2, 0)), jnp.transpose(in_second[0], (1, 2, 0))
    mb, vb = back_first[0], back_second[0]
    if direct:
        gsum, total, ada_t, small_t, bias_t = step_exchange(
            cores, gq, go, gu, gd, wi_t, back_weight, mi, mb, vi, vb, ada_d, small_d, bias_d)
        gi, gbk = gsum[:7], gsum[7:]
        di, db = total[:7].astype(f32), total[7:].astype(f32)
        ada_t = ada_t.astype(f32)
    else:
        def scatter(x):
            x = lax.psum_scatter(x, "tp", scatter_dimension=1, tiled=True, axis_index_groups=groups)
            return lax.psum_scatter(x, "dp", scatter_dimension=2, tiled=True).astype(f32)

        def over_groups(x):
            return lax.psum(x.astype(bf16), "grp").astype(f32)

        gi = scatter(jnp.concatenate([gq, gu], axis=0))
        gbk = scatter(jnp.concatenate([go[None], gd], axis=0))
        im, iv = adam_parts(gi, mi, vi)
        bm, bv = adam_parts(gbk, mb, vb)
        di = over_groups(adam_diff(wi_t, im, iv, rate_matrix, decay_rate))
        db = over_groups(adam_diff(back_weight, bm, bv, rate_matrix, decay_rate))
        ada_t, small_t, bias_t = over_groups(ada_d), over_groups(small_d), over_groups(bias_d)
    in_m, in_v = adam_parts(gi, mi, vi)
    back_m, back_v = adam_parts(gbk, mb, vb)

    def outer(weight, moment, summed):
        diff = summed / n_grp
        moment_new = outer_mu * moment + diff
        return weight - outer_rate * (diff + outer_mu * moment_new), diff, moment_new

    def back_in(x):
        return jnp.transpose(x, (2, 0, 1))

    def back_ada(x):
        return jnp.transpose(x, (1, 0, 2))

    in_w, in_diff, in_mom = (back_in(x) for x in outer(wi_t, jnp.transpose(in_moment, (1, 2, 0)), di))
    back_w, back_diff, back_mom = outer(back_weight, back_moment, db)
    ada_w, ada_diff, ada_mom = (back_ada(x) for x in outer(wa_t, jnp.transpose(ada_moment, (1, 0, 2)), ada_t))
    small_w, small_diff, small_mom = outer(small_params, small_moment, small_t)
    bias_w, bias_diff, bias_mom = outer(up_bias, bias_moment, bias_t)
    return (
        block_out, input_grad,
        back_in(in_m)[None], back_m[None], back_ada(ada_m)[None], small_m[None], bias_m[None],
        back_in(in_v)[None], back_v[None], back_ada(ada_v)[None], small_v[None], bias_v[None],
        in_w, back_w, ada_w, small_w, bias_w,
        in_diff, back_diff, ada_diff, small_diff, bias_diff,
        in_mom, back_mom, ada_mom, small_mom, bias_mom,
    )


def solution(mesh):
    rows = P(("dp", "grp"), None, None)
    shared = (
        P("dp", None, "tp"), P(None, "tp", "dp"), P("dp", None, "tp"), P(None, "dp"), P(None, ("tp", "dp")),
    )
    grouped = (
        P("grp", "dp", None, "tp"), P("grp", None, "tp", "dp"), P("grp", "dp", None, "tp"),
        P("grp", None, "dp"), P("grp", None, ("tp", "dp")),
    )
    in_specs = (rows, P(("dp", "grp")), P(("dp", "grp"), None), rows, P()) + shared + grouped + grouped + shared
    out_specs = (rows, rows) + grouped + grouped + shared + shared + shared
    return jax.shard_map(on_device, mesh=mesh, in_specs=in_specs, out_specs=out_specs, check_vma=False)
```

time: 763 us -> 385 us (0.50)
  waiting for transfers between devices: 370 us -> 0 us
  Pallas kernels: 0 us -> 327 us
  matrix products: 116 us -> 0.18 us
  other arithmetic: 99.2 us -> 30.4 us
  local copies, waits for them, and re-layouts: 82.6 us -> 24.9 us
  blocking collectives: 51.7 us -> 0 us
  loops' own time: 21.7 us -> 0 us
  between operations: 15.3 us -> 1.15 us
    pallas_call x0 -> x10, Pallas kernels: none -> 327 us  [the longest x1 113 us: step_exchange(): pl.pallas_call(functools.partial(step_kernel, cores), out_shape=(jax.Shap...]
    psum x4 -> x0, waiting for transfers between devices: 317 us -> none  [the longest x1 111 us: on_device(): attended = lax.psum(attention_branch, 'tp')]
    dot_general x42 -> x0, matrix products: 116 us -> none  [the longest x4 13.9 us: forward_block(): jnp.einsum('hrk,khe->rhe', attn_probs, value_seq, preferred_element_type=...]
    unnamed x15 -> x0, waiting for transfers between devices: 45.1 us -> none
    reduce_sum x15 -> x5, other arithmetic: 46 us -> 2.34 us  [the longest x1 1.12 us: on_device(): by_seq = shared.reshape(seqs, cores, n_dp, 16, width).sum(axis=1)]
    all_gather x4 -> x0, blocking collectives: 32.1 us -> none  [the longest x1 11.3 us: on_device(): lax.all_gather(ada_weight.astype(jnp.bfloat16), 'dp', axis=0, tiled=True)]
    another operation x4 -> x0, loops' own time: 21.7 us -> none  [the longest x2 11.1 us: backward_sequence(): lax.scan(backward_block, (zero_rows, zero_rows), jnp.arange(block_count,...]
    convert_element_type x15 -> x4, other arithmetic: 26.7 us -> 6.84 us  [the longest x1 3.19 us: on_device(): input_grad = grad_low.astype(f32)]
  transfers between devices with their start and end apart: 11 -> 0, of which waited for: 8 -> 0; matrix products, arithmetic and copies ran while one was open for 21% -> 0% of each run, Pallas kernels for 0% -> 0%
where the time goes in v1:
time: 385 us; the launch traced here: 384 us
  Pallas kernels  327 us (85%)
  other arithmetic  30.4 us (8%)
  local copies, waits for them, and re-layouts  24.9 us (6%)
    pallas_call x1, Pallas kernels, step_exchange(): pl.pallas_call(functools.partial(step_kernel, cores), out_shape=(jax.Shap...  113 us
    pallas_call x1, Pallas kernels, gather_weights(): pl.pallas_call(functools.partial(gather_kernel, cores), out_shape=(jax.Sh...  60.7 us
    pallas_call x1, Pallas kernels, last(): pl.pallas_call(functools.partial(last_kernel, cores, spans), out_shape=(j...  43.6 us
    pallas_call x1, Pallas kernels, pull_attention(): pl.pallas_call(body, grid=(pairs,), out_shape=(jax.ShapeDtypeStruct((leng...  32.2 us
    pallas_call x1, Pallas kernels, feed(): pl.pallas_call(feed_kernel, out_shape=(jax.ShapeDtypeStruct((length, widt...  22.3 us
    pallas_call x1, Pallas kernels, attend(): pl.pallas_call(attend_kernel, grid=(pairs, length // step), out_shape=(ja...  20 us
    unnamed x115, local copies, waits for them, and re-layouts  18.6 us
    pallas_call x1, Pallas kernels, exchange_modulation(): pl.pallas_call(functools.partial(mod_kernel, cores), out_shape=(jax.Shape...  11.3 us

profile of v1, /device:TPU:0, one launch (start us, length us, event | category | flops | bytes accessed | tf_op | source)
XLA Modules:
  0.0 384.0 jit_solution(17514129820435628421)
XLA Ops:
  0.7 1.8 copy-done
  2.6 1.2 dynamic-slice_bitcast_fusion.tok
  3.8 0.2 fusion.38
  4.0 0.1 reshape.180
  4.1 0.6 scatter.4.cond
  4.7 11.3 %mod_exchange.1 = (f32[4,8,192]{2,1,0:T(8,128)}, f32[2,9,384]{2,1,0:T(8,128)}, f32[2,2,4,96]{3,2,1,0:T(4,128)}) custom-call(f32[2,8,64]{2,1,0:T(8,128)} %scatter.4.cond, f32[6,64,192]{2,1,0:T(8,128)} %bitcast.139, f32[9,384]{1,0:T(8,128)} %ps.1, f32[4,96]{1,0:T(4,128)} %bu.1), custom_call_target="tpu_custom_call" | custom-call | tf_op jit(solution)/shard_map/mod_exchange/pallas_call | solution.py:140
  16.1 0.9 slice.74
  17.0 0.8 slice_bitcast_fusion
  17.8 0.1 reshape.181
  17.9 0.7 slice.73
  18.6 0.1 pad.7.clone
  18.7 0.1 maximum_maximum_fusion.vecs
  18.8 2.7 bitcast_convert_fusion.wi
  21.5 0.9 convert_element_type.38.wb
  22.4 60.7 %weight_gather.1 = (bf16[3,384,768]{2,1,0:T(8,128)(2,1)}, bf16[384,768]{1,0:T(8,128)(2,1)}, bf16[4,384,768]{2,1,0:T(8,128)(2,1)}, bf16[4,384,768]{2,1,0:T(8,128)(2,1)}) custom-call(bf16[7,192,384]{2,1,0:T(8,128)(2,1)} %bitcast_convert_fusion.wi, bf16[5,192,384]{2,1,0:T(8,128)(2,1)} %convert_element_type.38.wb), custom_call_target="tpu_custom_call" | custom-call | tf_op jit(solution)/shard_map/weight_gather/pallas_call | solution.py:228
  83.1 6.1 %project.1 = (bf16[1024,768]{1,0:T(8,128)(2,1)S(1)}, bf16[384,1024]{1,0:T(8,128)(2,1)S(1)}, bf16[384,1024]{1,0:T(8,128)(2,1)S(1)}, bf16[384,1024]{1,0:T(8,128)(2...) custom-call(bf16[1024,768]{1,0:T(8,128)(2,1)} %dynamic-slice_bitcast_fusion.tok, ...), custom_call_target="tpu_custom_call" | custom-call | tf_op jit(solution)/shard_map/project/pallas_call | solution.py:280
  89.2 1.2 copy-done.8
  90.4 0.9 copy-done.15
  91.3 0.9 copy-done.16
  92.2 20.0 %attend.1 = (bf16[6,1024,1024]{2,1,0:T(8,128)(2,1)}, f32[3,2,1024]{2,1,0:T(2,128)S(1)}, bf16[384,1024]{1,0:T(8,128)(2,1)S(1)}) custom-call(bf16[1024,384]{1,0:T(8,128)(2,1)S(1)} %get-tuple-element.81.k_r, bf16[384,1024]{1,0:T(8,128)(2,1)S(1)} %get-tuple-element.82.q_t, bf16[384,1024]{1,0:T(8,128)(2,1)S(1)} %get-tuple-element.83.v_t), custom_call_target="tpu_custom_call" | custom-call | tf_op jit(solution)/shard_map/attend/pallas_call | solution.py:334
  112.2 0.6 copy-done.21
  112.8 7.2 %attention_mix.1 = (f32[512,768]{1,0:T(8,128)S(1)}, f32[512,768]{1,0:T(8,128)S(1)}, bf16[1024,768]{1,0:T(8,128)(2,1)S(1)}) custom-call(bf16[384,1024]{1,0:T(8,128)(2,1)S(1)} %get-tuple-element.84.o_t, bf16[384,768]{1,0:T(8,128)(2,1)S(1)} %copy-done.5, bf16[1024,768]{1,0:T(8,128)(2,1)} %dynamic-slice_bitcast_fusion.tok, f32[16,768]{1,0:T(8,128)S(1)} %maximum_maximum_fusion.vecs), custom_call_target="tpu_custom_call" | custom-call | tf_op jit(solution)/shard_map/attention_mix/pallas_call | solution.py:408
  120.0 1.1 copy-done.13
  121.2 1.5 bitcast_multiply_fusion.gy
  122.8 0.1 copy-done.11
  122.8 0.5 copy-done.12
  123.3 0.7 reshape.182.bias
  124.0 22.3 %feed_forward.1 = (bf16[1024,768]{1,0:T(8,128)(2,1)}, bf16[1024,768]{1,0:T(8,128)(2,1)}, bf16[1536,768]{1,0:T(8,128)(2,1)}, bf16[1536,768]{1,0:T(8,128)(2,1)}, f32[1,1536]{1,0:T(1,128)}) custom-call(bf16[1024,768]{1,0:T(8,128)(2,1)} %copy-done.13, bf16[1024,768]{1,0:T(8,128)(2,1)} %bitcast_multiply_fusion.gy, f32[16,768]{1,0:T(8,128)} %copy-done.6, ...), custom_call_target="tpu_custom_call" | custom-call | tf_op jit(solution)/shard_map/feed_forward/pallas_call | solution.py:471
  146.3 1.4 copy-done.14
  147.7 10.5 %middle.1 = (bf16[512,768]{1,0:T(8,128)(2,1)S(1)}, f32[512,768]{1,0:T(8,128)S(1)}, bf16[1024,768]{1,0:T(8,128)(2,1)S(1)}, f32[8,768]{1,0:T(8,128)S(1)}) custom-call(bf16[1024,768]{1,0:T(8,128)(2,1)S(1)} %copy-done.14, bf16[1024,768]{1,0:T(8,128)(2,1)} %get-tuple-element.91.dh2, f32[512,768]{1,0:T(8,128)} %copy-done.12, f32[512,768]{1,0:T(8,128)} %copy-done.11, ...), custom_call_target="tpu_custom_call" | custom-call | tf_op jit(solution)/shard_map/middle/pallas_call | solution.py:543
  158.3 1.1 copy-done.9
  159.4 0.9 copy-done.17
  160.3 32.2 %attention_pull.1 = (bf16[1024,768]{1,0:T(8,128)(2,1)}, bf16[3,384,768]{2,1,0:T(8,128)(2,1)}, bf16[384,768]{1,0:T(8,128)(2,1)}) custom-call(bf16[1024,768]{1,0:T(8,128)(2,1)} %copy-done.9, bf16[384,768]{1,0:T(8,128)(2,1)} %get-tuple-element.85.wo, bf16[384,1024]{1,0:T(8,128)(2,1)} %copy-done.4, f32[3,2,1024]{2,1,0:T(2,128)} %copy-done.21, ...), custom_call_target="tpu_custom_call" | custom-call | tf_op jit(solution)/shard_map/attention_pull/pallas_call | solution.py:623
  192.6 1.4 copy-done.10
  194.0 1.1 copy-done.18
  195.2 43.6 %last_norm.1 = (bf16[2,1024,768]{2,1,0:T(8,128)(2,1)}, bf16[2,1024,768]{2,1,0:T(8,128)(2,1)}, f32[4,2,16,768]{3,2,1,0:T(8,128)}) custom-call(bf16[1024,768]{1,0:T(8,128)(2,1)S(1)} %copy-done.10, f32[512,768]{1,0:T(8,128)S(1)} %get-tuple-element.101.dx1, bf16[1024,768]{1,0:T(8,128)(2,1)S(1)} %copy-done.2, bf16[512,768]{1,0:T(8,128)(2,1)S(1)} %copy-done.18, ...), custom_call_target="tpu_custom_call" | custom-call | tf_op jit(solution)/shard_map/last_norm/pallas_call | solution.py:761
  238.9 1.1 bitcast_reduce_fusion
  240.1 0.1 fusion.23
  240.2 0.6 fusion.22
  240.8 0.1 constant_dynamic-slice_fusion.1
  240.9 0.7 slice.75
  241.6 0.1 constant_dynamic-slice_fusion.2
  241.7 0.2 multiply_reduce_fusion
  241.9 1.0 fusion.18.ea
  243.0 1.0 slice_reduce_fusion
  243.9 0.1 reshape.189
  244.0 0.1 constant_dynamic-slice_fusion
  244.1 0.6 add_multiply_fusion.1.eb
  244.7 113.3 %step_exchange.1 = (f32[12,192,384]{2,1,0:T(8,128)}, bf16[12,192,384]{2,1,0:T(8,128)(2,1)}, bf16[6,64,192]{2,1,0:T(8,128)(2,1)}, f32[9,384]{1,0:T(8,128)}, f32[4,96]{1,0:T(4,128)}) custom-call(bf16[3,384,768]{2,1,0:T(8,128)(2,1)} %get-tuple-element.107.gq, bf16[384,768]{1,0:T(8,128)(2,1)} %get-tuple-element.108.go, bf16[4,384,768]{2,1,0:T(8,128)(2,1)} %bitcast.140, ...), custom_call_target="tpu_custom_call" | custom-call | tf_op jit(solution)/shard_map/step_exchange/pallas_call | solution.py:1003
  358.1 4.7 %fusion.3 = (f32[384,7,192]{0,2,1:T(8,128)}, f32[384,7,192]{0,2,1:T(8,128)}, f32[384,7,192]{0,2,1:T(8,128)}) fusion(f32[384,7,192]{0,2,1:T(8,128)S(1)} %copy-done.33, bf16[12,192,384]{2,1,0:T(8,128)(2,1)} %get-tuple-element.113, f32[384,7,192]{0,2,1:T(8,128)S(1)} %copy-done.22), kind=kLoop, calls=%fused_computation.9 | loop fusion | flops 4128768 | bytes 11354112 | tf_op jit(solution)/shard_map/transpose | solution.py:1183
  362.9 3.9 %multiply_subtract_fusion = (f32[5,192,384]{2,1,0:T(8,128)}, f32[5,192,384]{2,1,0:T(8,128)}, f32[5,192,384]{2,1,0:T(8,128)}) fusion(f32[5,192,384]{2,1,0:T(8,128)S(1)} %copy-done.24, f32[5,192,384]{2,1,0:T(8,128)S(1)} %copy-done.37, bf16[12,192,384]{2,1,0:T(8,128)(2,1)} %get-tuple-element.113), kind=kLoop, calls=%fused_computation.15 | loop fusion | flops 2949120 | bytes 8110080 | tf_op jit(solution)/shard_map/sub | solution.py:1180
  366.8 1.1 copy-done.29
  367.9 2.6 fusion.1
  370.5 2.1 fusion.5
  372.6 1.1 fusion.19
  373.8 0.6 multiply_subtract_fusion.1
  374.4 0.6 multiply_subtract_fusion.2
  375.0 1.0 fusion.13
  376.0 0.6 copy.83
  376.6 0.6 copy.84
  377.2 3.2 convert_element_type.41
  380.4 0.6 fusion.29
  381.0 1.7 copy.104
  382.7 1.4 copy-done.1
  (108 shorter events, 0.4 us)
Async XLA Ops:
  0.7 1.9 copy-start
  0.7 3.1 copy-start.55
  0.7 3.1 copy-start.54
  16.1 5.4 %copy-start.23 = (f32[5,192,384]{2,1,0:T(8,128)S(1)}, f32[5,192,384]{2,1,0:T(8,128)}, u32[]{:S(2)}) copy-start(f32[5,192,384]{2,1,0:T(8,128)} %wb.1) | copy-start | bytes 4423684
  18.8 94.0 %copy-start.6 = (f32[16,768]{1,0:T(8,128)}, f32[16,768]{1,0:T(8,128)S(1)}, u32[]{:S(2)}) copy-start(f32[16,768]{1,0:T(8,128)S(1)} %maximum_maximum_fusion.vecs) | copy-start | bytes 147460
  21.5 61.7 %copy-start.19 = (f32[32,1024]{1,0:T(8,128)S(1)}, f32[32,1024]{1,0:T(8,128)}, u32[]{:S(2)}) copy-start(f32[32,1024]{1,0:T(8,128)} %constant.206.clone.cosine) | copy-start | bytes 393220
  21.5 61.7 %copy-start.20 = (f32[32,1024]{1,0:T(8,128)S(1)}, f32[32,1024]{1,0:T(8,128)}, u32[]{:S(2)}) copy-start(f32[32,1024]{1,0:T(8,128)} %constant.207.clone.sine) | copy-start | bytes 393220
  89.2 1.2 copy-start.8
  90.4 0.9 copy-start.15
  91.3 0.9 copy-start.16
  92.2 27.8 %copy-start.3 = (bf16[384,1024]{1,0:T(8,128)(2,1)}, bf16[384,1024]{1,0:T(8,128)(2,1)S(1)}, u32[]{:S(2)}) copy-start(bf16[384,1024]{1,0:T(8,128)(2,1)S(1)} %get-tuple-element.82.q_t) | copy-start | bytes 2359300
  92.2 20.6 %copy-start.5 = (bf16[384,768]{1,0:T(8,128)(2,1)S(1)}, bf16[384,768]{1,0:T(8,128)(2,1)}, u32[]{:S(2)}) copy-start(bf16[384,768]{1,0:T(8,128)(2,1)} %get-tuple-element.85.wo) | copy-start | bytes 1769476
  92.2 29.0 %copy-start.38 = (bf16[2,1024,768]{2,1,0:T(8,128)(2,1)S(1)}, bf16[2,1024,768]{2,1,0:T(8,128)(2,1)}, u32[]{:S(2)}) copy-start(bf16[2,1024,768]{2,1,0:T(8,128)(2,1)} %param.32) | copy-start | bytes 9437188
  112.2 0.6 copy-start.21
  112.8 10.0 %copy-start.4 = (bf16[384,1024]{1,0:T(8,128)(2,1)}, bf16[384,1024]{1,0:T(8,128)(2,1)S(1)}, u32[]{:S(2)}) copy-start(bf16[384,1024]{1,0:T(8,128)(2,1)S(1)} %get-tuple-element.84.o_t) | copy-start | bytes 2359300
  112.8 8.4 %copy-start.51 = (s32[2,1024]{1,0:T(2,128)S(1)}, s32[2,1024]{1,0:T(2,128)}, u32[]{:S(2)}) copy-start(s32[2,1024]{1,0:T(2,128)} %param.31) | copy-start | bytes 24580
  120.0 1.1 copy-start.13
  121.1 1.7 copy-start.11
  121.1 2.2 copy-start.12
  121.2 2.2 copy-start.49
  124.0 22.3 %copy-start.7 = (f32[16,768]{1,0:T(8,128)S(1)}, f32[16,768]{1,0:T(8,128)}, u32[]{:S(2)}) copy-start(f32[16,768]{1,0:T(8,128)} %copy-done.6) | copy-start | bytes 147460
  146.3 1.4 copy-start.14
  158.3 1.1 copy-start.9
  159.4 0.9 copy-start.17
  160.3 32.2 %copy-start.50 = (f32[1,1536]{1,0:T(1,128)S(1)}, f32[1,1536]{1,0:T(1,128)}, u32[]{:S(2)}) copy-start(f32[1,1536]{1,0:T(1,128)} %get-tuple-element.104) | copy-start | bytes 18436
  160.3 32.3 %copy-start.2 = (bf16[1024,768]{1,0:T(8,128)(2,1)S(1)}, bf16[1024,768]{1,0:T(8,128)(2,1)}, u32[]{:S(2)}) copy-start(bf16[1024,768]{1,0:T(8,128)(2,1)} %dynamic-slice_bitcast_fusion.tok) | copy-start | bytes 4718596
  192.6 1.4 copy-start.10
  194.0 1.1 copy-start.18
  195.1 44.9 %copy-start.42 = (f32[1,9,384]{2,0,1:T(1,128)S(1)}, f32[1,9,384]{2,0,1:T(1,128)}, u32[]{:S(2)}) copy-start(f32[1,9,384]{2,0,1:T(1,128)} %param.47) | copy-start | bytes 41476
  195.2 45.0 %copy-start.40 = (f32[9,384]{1,0:T(8,128)S(1)}, f32[9,384]{1,0:T(8,128)}, u32[]{:S(2)}) copy-start(f32[9,384]{1,0:T(8,128)} %ps.1) | copy-start | bytes 41476
  195.2 45.0 %copy-start.46 = (f32[1,9,384]{2,0,1:T(1,128)S(1)}, f32[1,9,384]{2,0,1:T(1,128)}, u32[]{:S(2)}) copy-start(f32[1,9,384]{2,0,1:T(1,128)} %param.42) | copy-start | bytes 41476
  238.8 3.1 copy-start.30
  238.8 3.1 copy-start.34
  238.8 3.1 copy-start.35
  238.8 5.3 %copy-start.45 = (f32[4,96]{1,0:T(4,128)S(1)}, f32[4,96]{1,0:T(4,128)}, u32[]{:S(2)}) copy-start(f32[4,96]{1,0:T(4,128)} %bu.1) | copy-start | bytes 4612
  238.9 5.3 %copy-start.47 = (f32[1,4,96]{2,1,0:T(4,128)S(1)}, f32[1,4,96]{2,1,0:T(4,128)}, u32[]{:S(2)}) copy-start(f32[1,4,96]{2,1,0:T(4,128)} %param.48) | copy-start | bytes 4612
  238.9 5.3 %copy-start.48 = (f32[1,4,96]{2,1,0:T(4,128)S(1)}, f32[1,4,96]{2,1,0:T(4,128)}, u32[]{:S(2)}) copy-start(f32[1,4,96]{2,1,0:T(4,128)} %param.43) | copy-start | bytes 4612
  244.7 113.3 %copy-start.22 = (f32[384,7,192]{0,2,1:T(8,128)S(1)}, f32[384,7,192]{0,2,1:T(8,128)}, u32[]{:S(2)}) copy-start(f32[384,7,192]{0,2,1:T(8,128)} %param.34) | copy-start | bytes 6193156
  244.7 113.3 %copy-start.33 = (f32[384,7,192]{0,2,1:T(8,128)S(1)}, f32[384,7,192]{0,2,1:T(8,128)}, u32[]{:S(2)}) copy-start(f32[384,7,192]{0,2,1:T(8,128)} %param.49) | copy-start | bytes 6193156
  358.1 4.8 %copy-start.24 = (f32[5,192,384]{2,1,0:T(8,128)S(1)}, f32[5,192,384]{2,1,0:T(8,128)}, u32[]{:S(2)}) copy-start(f32[5,192,384]{2,1,0:T(8,128)} %wb.1) | copy-start | bytes 4423684
  358.1 4.8 %copy-start.37 = (f32[5,192,384]{2,1,0:T(8,128)S(1)}, f32[5,192,384]{2,1,0:T(8,128)}, u32[]{:S(2)}) copy-start(f32[5,192,384]{2,1,0:T(8,128)} %param.50) | copy-start | bytes 4423684
  362.9 3.9 %copy-start.25 = (f32[1,384,7,192]{1,3,2,0:T(8,128)S(1)}, f32[1,384,7,192]{1,3,2,0:T(8,128)}, u32[]{:S(2)}) copy-start(f32[1,384,7,192]{1,3,2,0:T(8,128)} %param.39) | copy-start | bytes 6193156
  362.9 3.9 %copy-start.26 = (f32[1,384,7,192]{1,3,2,0:T(8,128)S(1)}, f32[1,384,7,192]{1,3,2,0:T(8,128)}, u32[]{:S(2)}) copy-start(f32[1,384,7,192]{1,3,2,0:T(8,128)} %param.44) | copy-start | bytes 6193156
  362.9 5.1 %copy-start.29 = (f32[12,192,384]{2,1,0:T(8,128)S(1)}, f32[12,192,384]{2,1,0:T(8,128)}, u32[]{:S(2)}) copy-start(f32[12,192,384]{2,1,0:T(8,128)} %get-tuple-element.112) | copy-start | bytes 10616836
  367.9 2.6 copy-start.27
  367.9 2.6 copy-start.28
  370.5 2.1 copy-start.39
  370.5 2.1 copy-start.41
  372.6 1.2 copy-start.43
  372.6 1.2 copy-start.44
  372.6 1.8 copy-start.52
  372.6 1.8 copy-start.53
  372.6 2.4 copy-start.36
  372.6 4.6 %copy-start.32 = (bf16[2,1024,768]{2,1,0:T(8,128)(2,1)S(1)}, bf16[2,1024,768]{2,1,0:T(8,128)(2,1)}, u32[]{:S(2)}) copy-start(bf16[2,1024,768]{2,1,0:T(8,128)(2,1)} %get-tuple-element.106) | copy-start | bytes 9437188
  377.2 3.8 copy-start.31
  381.0 3.0 copy-start.1

commit v2 on v1

--- a/solution.py
+++ b/solution.py
@@ -1,4 +1,5 @@
 import functools
+from types import SimpleNamespace
 
 import jax
 import jax.numpy as jnp
@@ -73,176 +74,13 @@
     return rate * (first_hat / (jnp.sqrt(second_hat) + adam_eps) + decay * weight)
 
 
-def mod_kernel(cores, cond, wa, ps, bu, mod_out, ps_out, bu_out, c_got, parts, got, ps_low, bu_low, csem, psem, bsem, msem):
-    t, d = lax.axis_index("tp"), lax.axis_index("dp")
-    n_tp = mod_out.shape[0]
-    s = t // cores
-    c = lax.rem(t, cores)
-    barrier = pltpu.get_barrier_semaphore()
-    others = []
-    for dt in range(n_tp):
-        for dd in range(2):
-            if dt or dd:
-                others.append((lax.rem(t + dt, n_tp), lax.rem(d + dd, 2)))
-    for pt, pd in others:
-        pl.semaphore_signal(barrier, inc=1, device_id={"tp": pt, "dp": pd}, device_id_type=MESH)
-    pl.semaphore_wait(barrier, len(others))
-    cc = pltpu.make_async_remote_copy(
-        src_ref=cond.at[1 - d], dst_ref=c_got, send_sem=csem.at[0], recv_sem=csem.at[1],
-        device_id={"dp": 1 - d}, device_id_type=MESH)
-    cc.start()
-    ps_low[...] = ps[...].astype(bf16).astype(f32)
-    bu_low[...] = bu[...].astype(bf16).astype(f32)
-    ps_out[d] = ps_low[...]
-    bu_out[s, d] = bu_low[...]
-    pc = pltpu.make_async_remote_copy(
-        src_ref=ps_low, dst_ref=ps_out.at[d], send_sem=psem.at[0], recv_sem=psem.at[1],
-        device_id={"dp": 1 - d}, device_id_type=MESH)
-    pc.start()
-    bcs = []
-    for ds, dd in ((0, 1), (1, 0), (1, 1)):
-        bc = pltpu.make_async_remote_copy(
-            src_ref=bu_low, dst_ref=bu_out.at[s, d], send_sem=bsem.at[0, ds, dd], recv_sem=bsem.at[1, ds, dd],
-            device_id={"tp": lax.rem(s + ds, 2) * cores + c, "dp": lax.rem(d + dd, 2)}, device_id_type=MESH)
-        bc.start()
-        bcs.append(bc)
-    parts[...] = jnp.zeros_like(parts)
-    mine = cond[d].astype(bf16)
-    for a in range(6):
-        product = nn(mine, wa[a].astype(bf16))
-        for ss in range(2):
-            parts[d, ss, a : a + 1, :] = product[ss : ss + 1]
-    cc.wait()
-    theirs = c_got[...].astype(bf16)
-    for a in range(6):
-        product = nn(theirs, wa[a].astype(bf16))
-        for ss in range(2):
-            parts[1 - d, ss, a : a + 1, :] = product[ss : ss + 1]
-    sends = []
-    for i, (pt, pd) in enumerate(others):
-        mc = pltpu.make_async_remote_copy(
-            src_ref=parts.at[pd, pt // cores], dst_ref=got.at[t, d], send_sem=msem.at[0, i], recv_sem=msem.at[1, i],
-            device_id={"tp": pt, "dp": pd}, device_id_type=MESH)
-        mc.start()
-        sends.append(mc)
-    got[t, d] = parts[d, s]
-    for mc in sends:
-        mc.wait()
-    pc.wait()
-    for bc in bcs:
-        bc.wait()
-    mod_out[...] = got[:, 0] + got[:, 1]
-
-
-def exchange_modulation(cores, cond, wa, ps, bu):
-    n_tp = lax.axis_size("tp")
-    half_c, width = wa.shape[1:]
-    return pl.pallas_call(
-        functools.partial(mod_kernel, cores),
-        out_shape=(
-            jax.ShapeDtypeStruct((n_tp, 8, width), f32),
-            jax.ShapeDtypeStruct((2,) + ps.shape, f32),
-            jax.ShapeDtypeStruct((2, 2) + bu.shape, f32),
-        ),
-        in_specs=[VMEM] * 4,
-        out_specs=(VMEM,) * 3,
-        scratch_shapes=[
-            pltpu.VMEM((8, half_c), f32),
-            pltpu.VMEM((2, 2, 8, width), f32),
-            pltpu.VMEM((n_tp, 2, 8, width), f32),
-            pltpu.VMEM(ps.shape, f32),
-            pltpu.VMEM(bu.shape, f32),
-            pltpu.SemaphoreType.DMA((2,)),
-            pltpu.SemaphoreType.DMA((2,)),
-            pltpu.SemaphoreType.DMA((2, 2, 2)),
-            pltpu.SemaphoreType.DMA((2, 2 * n_tp - 1)),
-        ],
-        compiler_params=pltpu.CompilerParams(collective_id=0, has_side_effects=True),
-        name="mod_exchange",
-    )(cond, wa, ps, bu)
-
-
-def gather_kernel(cores, wi, wb, wq, wo, wu, wd, lsem, ssem, rsem):
-    t, d = lax.axis_index("tp"), lax.axis_index("dp")
-    s = t // cores
-    c = lax.rem(t, cores)
-    rows, cols = wi.shape[1:]
-    xdev = {"dp": 1 - d}
-    ydev = {"tp": (1 - s) * cores + c}
-
-    def block(a, ss, dd):
-        where = (pl.ds(pl.multiple_of(ss * rows, 16), rows), pl.ds(pl.multiple_of(dd * cols, 128), cols))
-        if a < 3:
-            return wq.at[(a,) + where]
-        if a == 3:
-            return wo.at[where]
-        if a < 8:
-            return wu.at[(a - 4,) + where]
-        return wd.at[(a - 8,) + where]
-
-    def own(a):
-        if a < 3:
-            return wi.at[a]
-        if a == 3:
-            return wb.at[0]
-        if a < 8:
-            return wi.at[a - 1]
-        return wb.at[a - 7]
-
-    def remote(kind, a, source, target, device):
-        return pltpu.make_async_remote_copy(
-            src_ref=source, dst_ref=target, send_sem=ssem.at[kind, a], recv_sem=rsem.at[kind, a],
-            device_id=device, device_id_type=MESH)
-
-    barrier = pltpu.get_barrier_semaphore()
-    for dev in (xdev, ydev):
-        pl.semaphore_signal(barrier, inc=1, device_id=dev, device_id_type=MESH)
-    pl.semaphore_wait(barrier, 2)
-    xs, ys, zs, ls = [], [], [], []
-    for a in range(12):
-        xs.append(remote(0, a, own(a), block(a, s, d), xdev))
-        ys.append(remote(1, a, own(a), block(a, s, d), ydev))
-        xs[a].start()
-        ys[a].start()
-        ls.append(pltpu.make_async_copy(own(a), block(a, s, d), lsem.at[a]))
-        ls[a].start()
-    for a in range(12):
-        if a % 2 == 0:
-            xs[a].wait_recv()
-            zs.append(remote(2, a, block(a, s, 1 - d), block(a, s, 1 - d), ydev))
-        else:
-            ys[a].wait_recv()
-            zs.append(remote(2, a, block(a, 1 - s, d), block(a, 1 - s, d), xdev))
-        zs[a].start()
-    for a in range(12):
-        xs[a].wait_send()
-        ys[a].wait_send()
-        (ys if a % 2 == 0 else xs)[a].wait_recv()
-        zs[a].wait()
-        ls[a].wait()
-
-
-def gather_weights(cores, wi, wb):
-    rows, cols = wi.shape[1:]
-    full = (2 * rows, 2 * cols)
-    return pl.pallas_call(
-        functools.partial(gather_kernel, cores),
-        out_shape=(
-            jax.ShapeDtypeStruct((3,) + full, bf16),
-            jax.ShapeDtypeStruct(full, bf16),
-            jax.ShapeDtypeStruct((4,) + full, bf16),
-            jax.ShapeDtypeStruct((4,) + full, bf16),
-        ),
-        in_specs=[ANY, ANY],
-        out_specs=(ANY,) * 4,
-        scratch_shapes=[
-            pltpu.SemaphoreType.DMA((12,)),
-            pltpu.SemaphoreType.DMA((3, 12)),
-            pltpu.SemaphoreType.DMA((3, 12)),
-        ],
-        compiler_params=pltpu.CompilerParams(collective_id=1, has_side_effects=True),
-        name="weight_gather",
-    )(wi, wb)
+def at(start, size, unit=128):
+    return pl.ds(pl.multiple_of(start, unit), size)
+
+
+def remote(source, target, send, recv, device):
+    return pltpu.make_async_remote_copy(
+        src_ref=source, dst_ref=target, send_sem=send, recv_sem=recv, device_id=device, device_id_type=MESH)
 
 
 def turn(values, cosine, sine):
@@ -257,308 +95,473 @@
     return jnp.concatenate(out, axis=0)
 
 
-def project_kernel(tok, vecs, wq, cosine, sine, h1, q_t, k_t, v_t, k_r, v_r):
-    hat, _ = normalize(tok[...].astype(f32))
-    hidden = hat * vecs[0:1] * (1.0 + vecs[4:5]) + vecs[3:4]
-    low = hidden.astype(bf16)
-    h1[...] = low
-    cos, sin = cosine[...], sine[...]
-    q_t[...] = (turn(nt(wq[0], low), cos, sin) * 0.125).astype(bf16)
-    keys = turn(nt(wq[1], low), cos, sin)
-    k_t[...] = keys.astype(bf16)
-    k_r[...] = keys.T.astype(bf16)
-    values = nt(wq[2], low)
-    v_t[...] = values.astype(bf16)
-    v_r[...] = values.T.astype(bf16)
-
-
-def project(tok, vecs, wq, cosine, sine):
-    length, width = tok.shape
-    heads_width = wq.shape[1]
-    step = 256
-    half = HEAD_DIM // 2
-    return pl.pallas_call(
-        project_kernel,
-        grid=(length // step,),
-        out_shape=(
-            jax.ShapeDtypeStruct((length, width), bf16),
-            jax.ShapeDtypeStruct((heads_width, length), bf16),
-            jax.ShapeDtypeStruct((heads_width, length), bf16),
-            jax.ShapeDtypeStruct((heads_width, length), bf16),
-            jax.ShapeDtypeStruct((length, heads_width), bf16),
-            jax.ShapeDtypeStruct((length, heads_width), bf16),
-        ),
-        in_specs=[
-            pl.BlockSpec((step, width), lambda i: (i, 0)),
-            pl.BlockSpec(vecs.shape, lambda i: (0, 0)),
-            pl.BlockSpec(wq.shape, lambda i: (0, 0, 0)),
-            pl.BlockSpec((half, step), lambda i: (0, i)),
-            pl.BlockSpec((half, step), lambda i: (0, i)),
-        ],
-        out_specs=(
-            pl.BlockSpec((step, width), lambda i: (i, 0)),
-            pl.BlockSpec((heads_width, step), lambda i: (0, i)),
-            pl.BlockSpec((heads_width, step), lambda i: (0, i)),
-            pl.BlockSpec((heads_width, step), lambda i: (0, i)),
-            pl.BlockSpec((step, heads_width), lambda i: (i, 0)),
-            pl.BlockSpec((step, heads_width), lambda i: (i, 0)),
-        ),
-        compiler_params=pltpu.CompilerParams(vmem_limit_bytes=48 * MIB),
-        name="project",
-    )(tok, vecs, wq, cosine, sine)
-
-
 def only_head(pair, h):
     row = lax.broadcasted_iota(jnp.int32, pair.shape, 0)
     return jnp.where(row // HEAD_DIM == h, pair, jnp.zeros_like(pair))
 
 
-def attend_kernel(k_r, q_t, v_t, probs, inv, o_t):
-    for h in range(2):
-        scores = nn(k_r[...], only_head(q_t[...], h))
+def greet(devices):
+    barrier = pltpu.get_barrier_semaphore()
+    for device in devices:
+        pl.semaphore_signal(barrier, inc=1, device_id=device, device_id_type=MESH)
+    pl.semaphore_wait(barrier, len(devices))
+
+
+def plane_devices(t, d, n_tp, spans):
+    others = []
+    for dt in range(n_tp):
+        for dd in range(spans):
+            if dt or dd:
+                dev = {"tp": lax.rem(t + dt, n_tp)}
+                if spans > 1:
+                    dev["dp"] = lax.rem(d + dd, spans)
+                others.append(dev)
+    return others
+
+
+def forward_kernel(direct, cores, n_tp, names, *args):
+    R = SimpleNamespace(**dict(zip(names, args)))
+    t, d = lax.axis_index("tp"), lax.axis_index("dp")
+    s = t // cores
+    c = lax.rem(t, cores)
+    length, width = R.tok.shape
+    half = length // cores
+    slot_rows = R.weights.shape[1]
+    rows, cols = slot_rows // 2, width // 2
+    own, other = at(c * half, half), at((1 - c) * half, half)
+    sibling = {"tp": s * cores + (1 - c)}
+    xdev = {"dp": 1 - d}
+    ydev = {"tp": (1 - s) * cores + c}
+
+    tok_load = pltpu.make_async_copy(R.tok_all.at[s], R.tok, R.load_sem.at[0])
+    cot_load = pltpu.make_async_copy(R.cot_all.at[s], R.cot, R.load_sem.at[1])
+
+    if direct:
+        stages = (R.attn, R.x1, R.away)
+
+        def staged(a):
+            return stages[a // 4].at[pl.ds((a % 4 // 2) * rows, rows), pl.ds((a % 2) * cols, cols)]
+
+        weight_loads = []
+        for a in range(12):
+            source = R.wi.at[a] if a < 3 else R.wb.at[0] if a == 3 else R.wi.at[a - 1] if a < 8 else R.wb.at[a - 7]
+            weight_loads.append(pltpu.make_async_copy(source, staged(a), R.stage_sem.at[a]))
+            weight_loads[a].start()
+    else:
+        weight_load = pltpu.make_async_copy(R.weights_in, R.weights, R.stage_sem.at[0])
+        weight_load.start()
+    tok_load.start()
+    cot_load.start()
+
+    def block(a, ss, dd):
+        return R.weights.at[a, at(ss * rows, rows, 16), at(dd * cols, cols)]
+
+    def hop(kind, a):
+        if kind == 0:
+            ref, dev = block(a, s, d), xdev
+        elif kind == 1:
+            ref, dev = block(a, s, d), ydev
+        elif kind == 2:
+            ref, dev = block(a, s, 1 - d), ydev
+        else:
+            ref, dev = block(a, 1 - s, d), xdev
+        k = min(kind, 2)
+        return remote(ref, ref, R.wsend.at[k, a], R.wrecv.at[k, a], dev)
+
+    def pass_on(m):
+        hop(0, 2 * m).wait_recv()
+        hop(2, 2 * m).start()
+        hop(1, 2 * m + 1).wait_recv()
+        hop(3, 2 * m + 1).start()
+
+    def arrived(m):
+        hop(1, 2 * m).wait_recv()
+        hop(2, 2 * m).wait_recv()
+        hop(0, 2 * m + 1).wait_recv()
+        hop(3, 2 * m + 1).wait_recv()
+
+    if direct:
+        others = plane_devices(t, d, n_tp, 2)
+        R.cond[...] = jnp.zeros_like(R.cond)
+        for ss in range(2):
+            row = R.table[pl.ds(R.sigma[ss], 1), :]
+            R.cond[ss : ss + 1, :] = (row / (1.0 + jnp.exp(-row))).astype(bf16).astype(f32)
+        turned = pltpu.roll(R.cond[...], R.cond.shape[1] // 2, 1)
+        R.cond_near[...] = jnp.where(d == 0, R.cond[...], turned)
+        R.cond_far[...] = jnp.where(d == 1, R.cond[...], turned)
+        R.ps_low[...] = R.ps[...].astype(bf16).astype(f32)
+        R.bu_low[...] = R.bu[...].astype(bf16).astype(f32)
+        greet(others)
+        cc = remote(R.cond_far, R.cond_got, R.small_sem.at[0, 0], R.small_sem.at[1, 0], xdev)
+        cc.start()
+        pc = remote(R.ps_low, R.ps_all.at[d], R.small_sem.at[0, 1], R.small_sem.at[1, 1], xdev)
+        pc.start()
+        bcs = []
+        for i, (ds, dd) in enumerate(((0, 1), (1, 0), (1, 1))):
+            dev = {"tp": lax.rem(s + ds, 2) * cores + c, "dp": lax.rem(d + dd, 2)}
+            bcs.append(remote(R.bu_low, R.bu_all.at[s, d], R.small_sem.at[0, 2 + i], R.small_sem.at[1, 2 + i], dev))
+            bcs[i].start()
+
+        def launch(a):
+            weight_loads[a].wait()
+            R.weights[a, at(s * rows, rows, 16), at(d * cols, cols)] = staged(a)[...].astype(bf16)
+            hop(0, a).start()
+            hop(1, a).start()
+
+        for a in range(4):
+            launch(a)
+        R.ps_all[d] = R.ps_low[...]
+        R.bu_all[s, d] = R.bu_low[...]
+        span = R.wa.shape[1]
+        R.parts[...] = jnp.zeros_like(R.parts)
+
+        def partial_mod(source, dd):
+            lhs = source[...][:, :span].astype(bf16)
+            for a in range(6):
+                product = nn(lhs, R.wa[a].astype(bf16))
+                for ss in range(2):
+                    R.parts[dd, ss, a : a + 1, :] = product[ss : ss + 1]
+
+        partial_mod(R.cond_near, d)
+        cc.wait()
+        partial_mod(R.cond_got, 1 - d)
+        mods = []
+        for i, dev in enumerate(others):
+            mods.append(remote(
+                R.parts.at[dev["dp"], dev["tp"] // cores], R.mod_got.at[t, d], R.mod_sem.at[0, i], R.mod_sem.at[1, i], dev))
+            mods[i].start()
+        R.mod_got[t, d] = R.parts[d, s]
+        R.cond_out[d] = R.cond_near[...]
+        R.cond_out[1 - d] = R.cond_got[...]
+        for a in range(4, 12):
+            launch(a)
+        pass_on(0)
+        pc.wait()
+        for bc in bcs:
+            bc.wait()
+        for mc in mods:
+            mc.wait()
+        small_rows = jnp.concatenate([R.ps_all[0], R.ps_all[1]], axis=1)
+        mod_rows = jnp.concatenate([R.mod_got[tt, 0] + R.mod_got[tt, 1] for tt in range(n_tp)], axis=1)
+        R.vecs[...] = jnp.zeros_like(R.vecs)
+        R.vecs[0:3] = small_rows[0:3]
+        R.vecs[3:9] = mod_rows[0:6] + small_rows[3:9]
+        R.bias[...] = jnp.concatenate(
+            [R.bu_all[ss, dd, j : j + 1, :] for j in range(4) for ss in range(2) for dd in range(2)], axis=1)
+        pass_on(1)
+    else:
+        greet([sibling])
+        R.vecs[...] = R.vecs_in[...]
+        R.bias[...] = R.bias_in[...]
+        R.cond_out[...] = jnp.zeros_like(R.cond_out)
+
+    tok_load.wait()
+    step = 256
+
+    @pl.loop(0, length // step)
+    def _(i):
+        r = at(i * step, step)
+        hat, _ = normalize(R.tok[r].astype(f32))
+        hidden = hat * (R.vecs[0:1] * (1.0 + R.vecs[4:5])) + R.vecs[3:4]
+        R.h1[r] = hidden.astype(bf16)
+
+    outs = []
+
+    def emit(source, target):
+        cp = pltpu.make_async_copy(source, target, R.out_sem.at[len(outs)])
+        cp.start()
+        outs.append(cp)
+
+    emit(R.h1, R.h1_out)
+
+    if direct:
+        arrived(0)
+        arrived(1)
+        pass_on(2)
+    else:
+        weight_load.wait()
+    emit(R.weights.at[pl.ds(0, 4)], R.wq_out)
+
+    @pl.loop(0, length // step)
+    def _(i):
+        r = at(i * step, step)
+        low = R.h1[r]
+        cos, sin = R.cosine[:, r], R.sine[:, r]
+        R.q_t[:, r] = (turn(nt(R.weights[0], low), cos, sin) * 0.125).astype(bf16)
+        keys = turn(nt(R.weights[1], low), cos, sin).astype(bf16)
+        R.k_t[:, r] = keys
+        R.k_r[r] = keys.T
+        values = nt(R.weights[2], low).astype(bf16)
+        R.v_t[:, r] = values
+        R.v_r[r] = values.T
+
+    emit(R.q_t, R.q_out)
+    emit(R.k_t, R.k_out)
+    emit(R.v_r, R.v_out)
+
+    heads = R.probs.shape[0]
+
+    @pl.loop(0, heads)
+    def _(h):
+        pair = at(h // 2 * 2 * HEAD_DIM, 2 * HEAD_DIM)
+        one = at(h * HEAD_DIM, HEAD_DIM, HEAD_DIM)
+        scores = nn(R.k_r[:, pair], only_head(R.q_t[pair, :], lax.rem(h, 2)))
         top = jnp.max(scores, axis=0, keepdims=True)
         shifted = jnp.exp(scores - top)
         inverse = 1.0 / jnp.sum(shifted, axis=0, keepdims=True)
         low = shifted.astype(bf16)
-        probs[h] = low
-        inv[0, h : h + 1, :] = inverse
-        rows = slice(h * HEAD_DIM, (h + 1) * HEAD_DIM)
-        o_t[rows, :] = (nn(v_t[rows, :], low) * inverse).astype(bf16)
-
-
-def attend(k_r, q_t, v_t):
-    length, heads_width = k_r.shape
-    pairs = heads_width // (2 * HEAD_DIM)
-    step = 256
-    pw = 2 * HEAD_DIM
-    return pl.pallas_call(
-        attend_kernel,
-        grid=(pairs, length // step),
-        out_shape=(
-            jax.ShapeDtypeStruct((2 * pairs, length, length), bf16),
-            jax.ShapeDtypeStruct((pairs, 2, length), f32),
-            jax.ShapeDtypeStruct((heads_width, length), bf16),
-        ),
-        in_specs=[
-            pl.BlockSpec((length, pw), lambda p, i: (0, p)),
-            pl.BlockSpec((pw, step), lambda p, i: (p, i)),
-            pl.BlockSpec((pw, length), lambda p, i: (p, 0)),
-        ],
-        out_specs=(
-            pl.BlockSpec((2, length, step), lambda p, i: (p, 0, i)),
-            pl.BlockSpec((1, 2, step), lambda p, i: (p, 0, i)),
-            pl.BlockSpec((pw, step), lambda p, i: (p, i)),
-        ),
-        compiler_params=pltpu.CompilerParams(vmem_limit_bytes=48 * MIB),
-        name="attend",
-    )(k_r, q_t, v_t)
-
-
-def sibling_of(cores):
-    t = lax.axis_index("tp")
-    s = t // cores
-    c = lax.rem(t, cores)
-    return s, c, {"tp": s * cores + (1 - c)}
-
-
-def greet(device):
-    barrier = pltpu.get_barrier_semaphore()
-    pl.semaphore_signal(barrier, inc=1, device_id=device, device_id_type=MESH)
-    pl.semaphore_wait(barrier, 1)
-
-
-def mix_kernel(cores, o_t, wo, tok, vecs, attn, x1, h2, away, got, tbuf, tsem, asem, hsem):
-    s, c, sibling = sibling_of(cores)
-    half = attn.shape[0]
-    own = pl.ds(pl.multiple_of(c * half, 128), half)
-    other = pl.ds(pl.multiple_of((1 - c) * half, 128), half)
-    tc = pltpu.make_async_copy(tok.at[own], tbuf, tsem)
-    tc.start()
-    greet(sibling)
-    away[...] = tn(o_t[:, other], wo[...])
-    send = pltpu.make_async_remote_copy(
-        src_ref=away, dst_ref=got, send_sem=asem.at[0], recv_sem=asem.at[1], device_id=sibling, device_id_type=MESH)
-    send.start()
-    attn[...] = tn(o_t[:, own], wo[...])
-    tc.wait()
-    send.wait()
-    step = 128
+        R.probs[h] = low
+        R.inv_out[h] = inverse
+        R.o_t[one, :] = (nn(R.v_t[one, :], low) * inverse).astype(bf16)
+        if direct:
+            @pl.when(jnp.logical_and(h >= 1, h < 4))
+            def _():
+                pass_on(h + 2)
+
+    for h in range(heads):
+        emit(R.probs.at[h], R.probs_out.at[h])
+    emit(R.o_t, R.o_out)
+
+    away = remote(R.away, R.got, R.pair_sem.at[0, 0], R.pair_sem.at[1, 0], sibling)
+    R.away[...] = tn(R.o_t[:, other], R.weights[3])
+    away.start()
+    R.attn[...] = tn(R.o_t[:, own], R.weights[3])
+    away.wait()
+    small = 128
+
+    @pl.loop(0, half // small)
+    def _(i):
+        r = at(i * small, small)
+        total = R.attn[r] + R.got[r]
+        R.attn[r] = total
+        after = R.tok[at(c * half + i * small, small)].astype(f32) + R.vecs[5:6] * total
+        R.x1[r] = after
+        hat, _ = normalize(after)
+        hidden = hat * (R.vecs[1:2] * (1.0 + R.vecs[7:8])) + R.vecs[6:7]
+        R.h2[at(c * half + i * small, small)] = hidden.astype(bf16)
+
+    share = remote(R.h2.at[own], R.h2.at[own], R.pair_sem.at[0, 1], R.pair_sem.at[1, 1], sibling)
+    share.start()
+    for cp in outs:
+        cp.wait()
+    flags = jnp.broadcast_to(R.flags[pl.ds(s, 1), :].astype(f32), (128, length)).T
+    R.column[...] = flags
+    cot_load.wait()
+
+    chunks = 2
+    if direct:
+        arrived(2)
+        arrived(3)
+
+    def weight(first, j):
+        return R.weights[first + 2 * j : first + 2 * j + 2].reshape(2 * slot_rows, width)
+
+    def up(r):
+        low = R.h2[r]
+        for j in range(chunks):
+            u = nt(low, weight(4, j)) + R.bias[:, j * width : (j + 1) * width]
+            square = u * u
+            inner = jnp.tanh(gelu_a * (u + gelu_b * square * u))
+            z = 0.5 * u * (1.0 + inner)
+            slope = 0.5 * (1.0 + inner) + 0.5 * u * (1.0 - inner * inner) * gelu_a * (1.0 + 3.0 * gelu_b * square)
+            R.probs[j, r, 0:width] = z.astype(bf16)
+            R.probs[2 + j, r, 0:width] = slope.astype(bf16)
 
     @pl.loop(0, half // step)
     def _(i):
-        r = pl.ds(pl.multiple_of(i * step, step), step)
-        total = attn[r] + got[r]
-        attn[r] = total
-        rows = tbuf[r].astype(f32) + vecs[5:6] * total
-        x1[r] = rows
-        hat, _ = normalize(rows)
-        hidden = hat * vecs[1:2] * (1.0 + vecs[7:8]) + vecs[6:7]
-        h2[pl.ds(pl.multiple_of(c * half + i * step, step), step)] = hidden.astype(bf16)
-
-    back = pltpu.make_async_remote_copy(
-        src_ref=h2.at[own], dst_ref=h2.at[own], send_sem=hsem.at[0], recv_sem=hsem.at[1],
-        device_id=sibling, device_id_type=MESH)
-    back.start()
-    back.wait()
-
-
-def mix(cores, o_t, wo, tok, vecs):
-    length, width = tok.shape
-    half = length // cores
-    return pl.pallas_call(
-        functools.partial(mix_kernel, cores),
-        out_shape=(
-            jax.ShapeDtypeStruct((half, width), f32),
-            jax.ShapeDtypeStruct((half, width), f32),
-            jax.ShapeDtypeStruct((length, width), bf16),
-        ),
-        in_specs=[VMEM, VMEM, ANY, VMEM],
-        out_specs=(VMEM,) * 3,
-        scratch_shapes=[
-            pltpu.VMEM((half, width), f32),
-            pltpu.VMEM((half, width), f32),
-            pltpu.VMEM((half, width), bf16),
-            pltpu.SemaphoreType.DMA,
-            pltpu.SemaphoreType.DMA((2,)),
-            pltpu.SemaphoreType.DMA((2,)),
-        ],
-        compiler_params=pltpu.CompilerParams(collective_id=2, has_side_effects=True, vmem_limit_bytes=48 * MIB),
-        name="attention_mix",
-    )(o_t, wo, tok, vecs)
-
-
-def feed_kernel(h2, gy, vecs, bias, wu, wd, mlp, dh2, gu, gd, gb, z_s, du_s, gm_s, b_s):
-    length, width = h2.shape
-    hidden = wu.shape[0]
-    chunk = width
-    step = 256
-    b_s[...] = jnp.zeros_like(b_s)
-
-    @pl.loop(0, length // step)
+        up(at(c * half + i * step, step))
+
+    share.wait()
+
+    @pl.loop(0, half // step)
     def _(i):
-        r = pl.ds(pl.multiple_of(i * step, step), step)
-        rows = h2[r]
-        gm = (gy[r].astype(f32) * vecs[8:9]).astype(bf16)
-        gm_s[r] = gm
+        up(at((1 - c) * half + i * step, step))
+
+    if direct:
+        arrived(4)
+        arrived(5)
+    R.bias_sum[...] = jnp.zeros_like(R.bias_sum)
+
+    def down(r):
+        grad = R.cot[r].astype(f32) * jnp.concatenate([R.column[r]] * (width // 128), axis=1)
+        R.cot[r] = grad.astype(bf16)
+        gm = (R.vecs[8:9] * grad).astype(bf16)
+        R.probs[4, r, 0:width] = gm
         forward = jnp.zeros((step, width), f32)
         backward = jnp.zeros((step, width), f32)
-        for j in range(hidden // chunk):
-            cols = slice(j * chunk, (j + 1) * chunk)
-            u = nt(rows, wu[cols]) + bias[:, cols]
-            square = u * u
-            inner = jnp.tanh(gelu_a * (u + gelu_b * square * u))
-            z = (0.5 * u * (1.0 + inner)).astype(bf16)
-            slope = 0.5 * (1.0 + inner) + 0.5 * u * (1.0 - inner * inner) * gelu_a * (1.0 + 3.0 * gelu_b * square)
-            du = (nt(gm, wd[cols]) * slope).astype(bf16)
-            z_s[r, cols] = z
-            du_s[r, cols] = du
-            b_s[:, cols] += fold(du.astype(f32))
-            forward += nn(z, wd[cols])
-            backward += nn(du, wu[cols])
-        mlp[r] = forward.astype(bf16)
-        dh2[r] = backward.astype(bf16)
-
-    gb[...] = jnp.sum(b_s[...], axis=0, keepdims=True)
-    for j in range(hidden // step):
-        cols = slice(j * step, (j + 1) * step)
-        gd[cols] = tn(z_s[:, cols], gm_s[...]).astype(bf16)
-        gu[cols] = tn(du_s[:, cols], h2[...]).astype(bf16)
-
-
-def feed(h2, gy, vecs, bias, wu, wd):
-    length, width = h2.shape
-    hidden = wu.shape[0]
-    return pl.pallas_call(
-        feed_kernel,
-        out_shape=(
-            jax.ShapeDtypeStruct((length, width), bf16),
-            jax.ShapeDtypeStruct((length, width), bf16),
-            jax.ShapeDtypeStruct((hidden, width), bf16),
-            jax.ShapeDtypeStruct((hidden, width), bf16),
-            jax.ShapeDtypeStruct((1, hidden), f32),
-        ),
-        in_specs=[VMEM] * 6,
-        out_specs=(VMEM,) * 5,
-        scratch_shapes=[
-            pltpu.VMEM((length, hidden), bf16),
-            pltpu.VMEM((length, hidden), bf16),
-            pltpu.VMEM((length, width), bf16),
-            pltpu.VMEM((8, hidden), f32),
-        ],
-        compiler_params=pltpu.CompilerParams(vmem_limit_bytes=56 * MIB),
-        name="feed_forward",
-    )(h2, gy, vecs, bias, wu, wd)
-
-
-def middle_kernel(cores, mlp, dh2, x1, attn, gy, vecs, out, dx1, ga, stats, got, acc, msem, gsem):
-    s, c, sibling = sibling_of(cores)
-    half = x1.shape[0]
-    own = pl.ds(pl.multiple_of(c * half, 128), half)
-    other = pl.ds(pl.multiple_of((1 - c) * half, 128), half)
-    greet(sibling)
-    sends = []
-    for i, ref in enumerate((mlp, dh2)):
-        cp = pltpu.make_async_remote_copy(
-            src_ref=ref.at[other], dst_ref=got.at[i], send_sem=msem.at[0, i], recv_sem=msem.at[1, i],
-            device_id=sibling, device_id_type=MESH)
-        cp.start()
-        sends.append(cp)
-    acc[...] = jnp.zeros_like(acc)
-    for cp in sends:
-        cp.wait()
-    step = 128
+        for j in range(chunks):
+            du = (nt(gm, weight(8, j)) * R.probs[2 + j, r, 0:width].astype(f32)).astype(bf16)
+            R.probs[2 + j, r, 0:width] = du
+            R.bias_sum[:, j * width : (j + 1) * width] += fold(du.astype(f32))
+            forward += nn(R.probs[j, r, 0:width], weight(8, j))
+            backward += nn(du, weight(4, j))
+        R.probs[5, r, 0:width] = forward.astype(bf16)
+        R.dh2[r] = backward.astype(bf16)
 
     @pl.loop(0, half // step)
     def _(i):
-        r = pl.ds(pl.multiple_of(i * step, step), step)
-        g = pl.ds(pl.multiple_of(c * half + i * step, step), step)
-        rows = x1[r]
-        branch = mlp[g].astype(f32) + got[0, r].astype(f32) + vecs[2:3]
-        out[r] = (rows + vecs[8:9] * branch).astype(bf16)
-        grad = gy[g].astype(f32)
-        dh = dh2[g].astype(f32) + got[1, r].astype(f32)
-        hat, inverse = normalize(rows)
-        acc[0] += fold(dh)
-        acc[1] += fold(dh * hat)
-        total = grad + norm_pull(dh * (vecs[1:2] * (1.0 + vecs[7:8])), hat, inverse)
-        dx1[r] = total
-        acc[2] += fold(total * attn[r])
-        acc[3] += fold(grad * branch)
-        acc[4] += fold((vecs[8:9] * grad).astype(bf16).astype(f32))
-        ga[g] = (vecs[5:6] * total).astype(bf16)
-
-    back = pltpu.make_async_remote_copy(
-        src_ref=ga.at[own], dst_ref=ga.at[own], send_sem=gsem.at[0], recv_sem=gsem.at[1],
-        device_id=sibling, device_id_type=MESH)
-    back.start()
-    stats[...] = jnp.zeros_like(stats)
+        down(at((1 - c) * half + i * step, step))
+
+    trades = [
+        remote(R.probs.at[5, other, pl.ds(0, width)], R.trade.at[0], R.pair_sem.at[0, 2], R.pair_sem.at[1, 2], sibling),
+        remote(R.dh2.at[other], R.trade.at[1], R.pair_sem.at[0, 3], R.pair_sem.at[1, 3], sibling),
+    ]
+    for cp in trades:
+        cp.start()
+
+    @pl.loop(0, half // step)
+    def _(i):
+        down(at(c * half + i * step, step))
+
+    R.acc[...] = jnp.zeros_like(R.acc)
+    for cp in trades:
+        cp.wait()
+
+    @pl.loop(0, half // small)
+    def _(i):
+        r = at(i * small, small)
+        g = at(c * half + i * small, small)
+        after = R.x1[r]
+        branch = R.probs[5, g, 0:width].astype(f32) + R.trade[0, r].astype(f32) + R.vecs[2:3]
+        R.out[r] = (after + R.vecs[8:9] * branch).astype(bf16)
+        grad = R.cot[g].astype(f32)
+        dh = R.dh2[g].astype(f32) + R.trade[1, r].astype(f32)
+        hat, inverse = normalize(after)
+        total = grad + norm_pull(dh * (R.vecs[1:2] * (1.0 + R.vecs[7:8])), hat, inverse)
+        R.x1[r] = total
+        R.ga[g] = (R.vecs[5:6] * total).astype(bf16)
+        R.acc[0] += fold(dh)
+        R.acc[1] += fold(dh * hat)
+        R.acc[2] += fold(total * R.attn[r])
+        R.acc[3] += fold(grad * branch)
+        R.acc[4] += fold(R.probs[4, g, 0:width].astype(f32))
+
+    give = remote(R.ga.at[own], R.ga.at[own], R.pair_sem.at[0, 4], R.pair_sem.at[1, 4], sibling)
+    give.start()
+    outs.clear()
+    emit(R.x1, R.dx1_out)
+    emit(R.out, R.block_half)
+    emit(R.vecs, R.vecs_out)
+    R.stats[...] = jnp.zeros_like(R.stats)
     for i in range(5):
-        stats[i : i + 1] = jnp.sum(acc[i], axis=0, keepdims=True)
-    back.wait()
-
-
-def middle(cores, mlp, dh2, x1, attn, gy, vecs):
-    length, width = mlp.shape
+        R.stats[i : i + 1] = jnp.sum(R.acc[i], axis=0, keepdims=True)
+    R.gb[...] = jnp.sum(R.bias_sum[...], axis=0, keepdims=True)
+
+    for k in range(4):
+        where = pl.ds((k % 2) * slot_rows, slot_rows)
+        R.gd[k] = tn(R.probs[k // 2, :, where], R.probs[4, :, 0:width]).astype(bf16)
+        emit(R.gd.at[k], R.gd_out.at[k])
+    for k in range(4):
+        where = pl.ds((k % 2) * slot_rows, slot_rows)
+        R.gu[k] = tn(R.probs[2 + k // 2, :, where], R.h2[...]).astype(bf16)
+        emit(R.gu.at[k], R.gu_out.at[k])
+    give.wait()
+    emit(R.ga, R.ga_out)
+    if direct:
+        for a in range(12):
+            hop(0, a).wait_send()
+            hop(1, a).wait_send()
+            hop(2 + a % 2, a).wait_send()
+    for cp in outs:
+        cp.wait()
+
+
+def forward(direct, cores, length, width, slot_rows, first, tokens, flags, cotangent, cosine, sine):
+    n_tp = lax.axis_size("tp")
     half = length // cores
-    return pl.pallas_call(
-        functools.partial(middle_kernel, cores),
-        out_shape=(
-            jax.ShapeDtypeStruct((half, width), bf16),
-            jax.ShapeDtypeStruct((half, width), f32),
-            jax.ShapeDtypeStruct((length, width), bf16),
-            jax.ShapeDtypeStruct((8, width), f32),
-        ),
-        in_specs=[VMEM] * 6,
-        out_specs=(VMEM,) * 4,
-        scratch_shapes=[
-            pltpu.VMEM((2, half, width), bf16),
-            pltpu.VMEM((5, 8, width), f32),
-            pltpu.SemaphoreType.DMA((2, 2)),
-            pltpu.SemaphoreType.DMA((2,)),
-        ],
-        compiler_params=pltpu.CompilerParams(collective_id=3, has_side_effects=True, vmem_limit_bytes=48 * MIB),
-        name="middle",
-    )(mlp, dh2, x1, attn, gy, vecs)
+    heads = slot_rows // HEAD_DIM
+    dma = pltpu.SemaphoreType.DMA
+    smem = pl.BlockSpec(memory_space=pltpu.SMEM)
+    arr = jax.ShapeDtypeStruct
+    vm = pltpu.VMEM
+    if direct:
+        lead = [("sigma", smem), ("table", VMEM), ("wa", VMEM), ("ps", VMEM), ("bu", VMEM), ("wi", ANY), ("wb", ANY)]
+        cond_shape = (2, 8, 128)
+    else:
+        lead = [("weights_in", ANY), ("vecs_in", VMEM), ("bias_in", VMEM)]
+        cond_shape = (2, 8, 128)
+    ins = lead + [("tok_all", ANY), ("flags", VMEM), ("cot_all", ANY), ("cosine", VMEM), ("sine", VMEM)]
+    outs = [
+        ("h1_out", arr((length, width), bf16), ANY),
+        ("wq_out", arr((4, slot_rows, width), bf16), ANY),
+        ("q_out", arr((slot_rows, length), bf16), ANY),
+        ("k_out", arr((slot_rows, length), bf16), ANY),
+        ("v_out", arr((length, slot_rows), bf16), ANY),
+        ("probs_out", arr((heads, length, length), bf16), ANY),
+        ("inv_out", arr((heads, 1, length), f32), VMEM),
+        ("o_out", arr((slot_rows, length), bf16), ANY),
+        ("dx1_out", arr((half, width), f32), ANY),
+        ("block_half", arr((half, width), bf16), ANY),
+        ("vecs_out", arr((16, width), f32), ANY),
+        ("stats", arr((8, width), f32), VMEM),
+        ("gb", arr((1, 4 * slot_rows), f32), VMEM),
+        ("gd_out", arr((4, slot_rows, width), bf16), ANY),
+        ("gu_out", arr((4, slot_rows, width), bf16), ANY),
+        ("ga_out", arr((length, width), bf16), ANY),
+        ("cond_out", arr(cond_shape, f32), VMEM),
+    ]
+    scratch = [
+        ("tok", vm((length, width), bf16)),
+        ("cot", vm((length, width), bf16)),
+        ("weights", vm((12, slot_rows, width), bf16)),
+        ("h1", vm((length, width), bf16)),
+        ("q_t", vm((slot_rows, length), bf16)),
+        ("k_t", vm((slot_rows, length), bf16)),
+        ("v_t", vm((slot_rows, length), bf16)),
+        ("k_r", vm((length, slot_rows), bf16)),
+        ("v_r", vm((length, slot_rows), bf16)),
+        ("probs", vm((heads, length, length), bf16)),
+        ("o_t", vm((slot_rows, length), bf16)),
+        ("away", vm((half, width), f32)),
+        ("got", vm((half, width), f32)),
+        ("attn", vm((half, width), f32)),
+        ("x1", vm((half, width), f32)),
+        ("h2", vm((length, width), bf16)),
+        ("column", vm((length, 128), f32)),
+        ("bias_sum", vm((8, 4 * slot_rows), f32)),
+        ("bias", vm((1, 4 * slot_rows), f32)),
+        ("vecs", vm((16, width), f32)),
+        ("dh2", vm((length, width), bf16)),
+        ("trade", vm((2, half, width), bf16)),
+        ("out", vm((half, width), bf16)),
+        ("ga", vm((length, width), bf16)),
+        ("acc", vm((5, 8, width), f32)),
+        ("gd", vm((4, slot_rows, width), bf16)),
+        ("gu", vm((4, slot_rows, width), bf16)),
+        ("load_sem", dma((2,))),
+        ("stage_sem", dma((12,))),
+        ("out_sem", dma((16,))),
+        ("pair_sem", dma((2, 5))),
+    ]
+    if direct:
+        wa, ps, bu = first[2:5]
+        scratch += [
+            ("cond", vm((8, 128), f32)),
+            ("cond_near", vm((8, 128), f32)),
+            ("cond_far", vm((8, 128), f32)),
+            ("cond_got", vm((8, 128), f32)),
+            ("ps_low", vm(ps.shape, f32)),
+            ("bu_low", vm(bu.shape, f32)),
+            ("ps_all", vm((2,) + ps.shape, f32)),
+            ("bu_all", vm((2, 2) + bu.shape, f32)),
+            ("parts", vm((2, 2, 8, wa.shape[2]), f32)),
+            ("mod_got", vm((n_tp, 2, 8, wa.shape[2]), f32)),
+            ("wsend", dma((3, 12))),
+            ("wrecv", dma((3, 12))),
+            ("small_sem", dma((2, 5))),
+            ("mod_sem", dma((2, 2 * n_tp - 1))),
+        ]
+    names = [n for n, _ in ins] + [o[0] for o in outs] + [n for n, _ in scratch]
+    results = pl.pallas_call(
+        functools.partial(forward_kernel, direct, cores, n_tp, names),
+        out_shape=tuple(o[1] for o in outs),
+        in_specs=[spec for _, spec in ins],
+        out_specs=tuple(o[2] for o in outs),
+        scratch_shapes=[shape for _, shape in scratch],
+        compiler_params=pltpu.CompilerParams(collective_id=0, has_side_effects=True, vmem_limit_bytes=60 * MIB),
+        name="forward",
+    )(*first, tokens, flags, cotangent, cosine, sine)
+    return SimpleNamespace(**dict(zip([o[0] for o in outs], results)))
 
 
 def pull_kernel(ga, wo, o_t, inv, probs, q_t, k_t, v_t, v_r, cosine, sine, h1, wq, dh1, gq, go, do_s, ds_s, dqkv):
@@ -657,7 +660,14 @@
     )(ga, wo, o_t, inv, probs, q_t, k_t, v_r, cosine, sine, h1, wq)
 
 
-def last_kernel(cores, spans, dh1, dx1, tok, out, vecs, stats, gb, cond, block_out, grad_out, shared,
+def sibling_of(cores):
+    t = lax.axis_index("tp")
+    s = t // cores
+    c = lax.rem(t, cores)
+    return s, c, {"tp": s * cores + (1 - c)}
+
+
+def last_kernel(cores, spans, dh1, dx1, tok, out, vecs, stats, gb, block_out, grad_out, shared,
                 got, tbuf, grad, acc, small, dsem, tsem, osem, fsem, lsem, vsem):
     t, d = lax.axis_index("tp"), lax.rem(lax.axis_index("dp"), spans)
     n_tp = shared.shape[0]
@@ -735,7 +745,6 @@
     small[7:8] = stats[1:2] * (1.0 + vecs[7:8])
     small[8:9] = stats[4:5]
     small[9:11] = gb[...]
-    small[11:12, 0 : cond.shape[1]] = cond[...]
     shared[t, d] = small[...]
     vsends = []
     for i, dev in enumerate(others):
@@ -754,7 +763,7 @@
         cp.wait()
 
 
-def last(cores, spans, seqs, dh1, dx1, tok, out, vecs, stats, gb, cond):
+def last(cores, spans, seqs, dh1, dx1, tok, out, vecs, stats, gb):
     length, width = tok.shape
     n_tp = lax.axis_size("tp")
     half = length // cores
@@ -765,7 +774,7 @@
             jax.ShapeDtypeStruct((seqs, length, width), bf16),
             jax.ShapeDtypeStruct((n_tp, spans, 16, width), f32),
         ),
-        in_specs=[VMEM, VMEM, ANY, ANY, VMEM, VMEM, VMEM, VMEM],
+        in_specs=[VMEM, VMEM, ANY, ANY, VMEM, VMEM, VMEM],
         out_specs=(ANY, ANY, VMEM),
         scratch_shapes=[
             pltpu.VMEM((half, width), bf16),
@@ -782,7 +791,7 @@
         ],
         compiler_params=pltpu.CompilerParams(collective_id=4, has_side_effects=True, vmem_limit_bytes=48 * MIB),
         name="last_norm",
-    )(dh1, dx1, tok, out, vecs, stats, gb, cond)
+    )(dh1, dx1, tok, out, vecs, stats, gb)
 
 
 def step_kernel(cores, gq, go, gu, gd, wi, wb, mi, mb, vi, vb, ea, es, eb,
@@ -1072,34 +1081,22 @@
     c = lax.rem(t, cores)
     groups = [[a * cores + b for a in range(seqs)] for b in range(cores)]
 
-    table_ids = jnp.arange(time_table.shape[0], dtype=jnp.int32)
-    onehot = (sigma_index[:, None] == table_ids[None, :]).astype(f32)
-    condition = jax.nn.silu(jnp.dot(onehot, time_table, precision=highest))
-    cond_low = condition.astype(bf16).astype(f32)
-    cond_width = cond_low.shape[1]
-
     wi_t = jnp.transpose(in_weight, (1, 2, 0))
     wa_t = jnp.transpose(ada_weight, (1, 0, 2))
-    tok = lax.dynamic_index_in_dim(tokens, s, 0, keepdims=False)
-    flags = lax.dynamic_index_in_dim(absorbed, s, 0, keepdims=False)
-    gy = lax.dynamic_index_in_dim(cotangent, s, 0, keepdims=False) * flags.astype(bf16)[:, None]
-    cond_row = lax.dynamic_index_in_dim(cond_low, s, 0, keepdims=True)
-
+    cosine, sine = angle_tables(length)
     if direct:
-        cond_in = jnp.zeros((2, 8, cond_width // 2), f32)
-        cond_in = cond_in.at[:, :seqs].set(jnp.transpose(cond_low.reshape(seqs, 2, cond_width // 2), (1, 0, 2)))
-        mod_parts, ps_all, bu_all = exchange_modulation(cores, cond_in, wa_t, small_params, up_bias)
-        small_rows = jnp.transpose(ps_all, (1, 0, 2)).reshape(9, width)
-        mod_rows = jnp.transpose(mod_parts[:, :6], (1, 0, 2)).reshape(6, width) + small_rows[3:9]
-        bias_row = jnp.transpose(bu_all, (2, 0, 1, 3)).reshape(1, 4 * heads_width)
-        wq, wo, wu, wd = gather_weights(cores, wi_t.astype(bf16), back_weight.astype(bf16))
+        first = (sigma_index, time_table, wa_t, small_params, up_bias, wi_t, back_weight)
     else:
         def over_tp(x, axis):
             return lax.all_gather(x, "tp", axis=axis, tiled=True, axis_index_groups=groups)
 
+        table_ids = jnp.arange(time_table.shape[0], dtype=jnp.int32)
+        onehot = (sigma_index[:, None] == table_ids[None, :]).astype(f32)
+        condition = jax.nn.silu(jnp.dot(onehot, time_table, precision=highest))
+        cond_low = condition.astype(bf16).astype(f32)
         wi_all = over_tp(lax.all_gather(wi_t.astype(bf16), "dp", axis=2, tiled=True), 1)
         wb_all = over_tp(lax.all_gather(back_weight.astype(bf16), "dp", axis=2, tiled=True), 1)
-        wq, wo, wu, wd = wi_all[:3], wb_all[0], wi_all[3:], wb_all[1:]
+        weights = jnp.concatenate([wi_all[:3], wb_all[:1], wi_all[3:], wb_all[1:]], axis=0)
         bu_all = over_tp(lax.all_gather(up_bias.astype(bf16), "dp", axis=1, tiled=True)[None], 0)
         bias_row = jnp.transpose(bu_all, (1, 0, 2)).reshape(1, 4 * heads_width).astype(f32)
         small_rows = lax.all_gather(small_params.astype(bf16), "dp", axis=1, tiled=True).astype(f32)
@@ -1107,29 +1104,30 @@
         mod_part = jnp.einsum("sc,cad->sad", cond_low.astype(bf16), wa_all, preferred_element_type=f32)
         mod_all = lax.all_gather(mod_part, "tp", axis=2, tiled=True)
         mod_rows = lax.dynamic_index_in_dim(mod_all, s, 0, keepdims=False) + small_rows[3:9]
-
-    vecs = jnp.concatenate([small_rows[0:3], mod_rows, jnp.zeros((7, width), f32)], axis=0)
-    cosine, sine = angle_tables(length)
-    wu = wu.reshape(4 * heads_width, width)
-    wd = wd.reshape(4 * heads_width, width)
-
-    h1, q_t, k_t, v_t, k_r, v_r = project(tok, vecs, wq, cosine, sine)
-    probs, inv, o_t = attend(k_r, q_t, v_t)
-    attn, x1, h2 = mix(cores, o_t, wo, tok, vecs)
-    mlp, dh2, gu, gd, gb = feed(h2, gy, vecs, bias_row, wu, wd)
-    out, dx1, ga, stats = middle(cores, mlp, dh2, x1, attn, gy, vecs)
-    dh1, gq, go = pull_attention(ga, wo, o_t, inv, probs, q_t, k_t, v_r, cosine, sine, h1, wq)
-    gb = gb.reshape(2, width)
-    gu = gu.reshape(4, heads_width, width)
-    gd = gd.reshape(4, heads_width, width)
-    block_out, grad_low, shared = last(cores, 2 if direct else 1, seqs, dh1, dx1, tok, out, vecs, stats, gb, cond_row)
+        vecs = jnp.concatenate([small_rows[0:3], mod_rows, jnp.zeros((7, width), f32)], axis=0)
+        first = (weights, vecs, bias_row)
+
+    fw = forward(direct, cores, length, width, heads_width, first, tokens, absorbed, cotangent, cosine, sine)
+    wq, wo = fw.wq_out[:3], fw.wq_out[3]
+    inv = fw.inv_out.reshape(-1, 2, length)
+    dh1, gq, go = pull_attention(
+        fw.ga_out, wo, fw.o_out, inv, fw.probs_out, fw.q_out, fw.k_out, fw.v_out, cosine, sine, fw.h1_out, wq)
+    gb = fw.gb.reshape(2, width)
+    gu, gd = fw.gu_out, fw.gd_out
+    tok = lax.dynamic_index_in_dim(tokens, s, 0, keepdims=False)
+    if direct:
+        conds = jnp.transpose(fw.cond_out[:, :seqs, : wa_t.shape[1]], (1, 0, 2))
+    else:
+        conds = jnp.transpose(lax.all_gather(cond_low, "dp", axis=0), (1, 0, 2))
+        conds = lax.dynamic_slice_in_dim(conds, d * wa_t.shape[1], wa_t.shape[1], 2)
+    block_out, grad_low, shared = last(
+        cores, 2 if direct else 1, seqs, dh1, fw.dx1_out, tok, fw.block_half, fw.vecs_out, fw.stats, gb)
     input_grad = grad_low.astype(f32)
 
     if not direct:
         shared = lax.all_gather(shared[:, 0], "dp", axis=1)
     by_seq = shared.reshape(seqs, cores, n_dp, 16, width).sum(axis=1)
     dmod = by_seq[:, :, 0:6]
-    conds = shared.reshape(seqs, cores, n_dp, 16, width)[:, 0, :, 11, :cond_width]
     small_grad = jnp.concatenate([by_seq[:, :, 6:9].sum(axis=(0, 1)), dmod.sum(axis=(0, 1))], axis=0)
     bias_sum = shared.reshape(seqs, cores, n_dp, 16, width)[:, :, :, 9:11].sum(axis=(0, 2))
     bias_sum = bias_sum.reshape(cores, 4, seqs, part)
@@ -1137,8 +1135,7 @@
     bias_grad = lax.dynamic_slice_in_dim(mine, d * (part // n_dp), part // n_dp, 1)
     small_shard = lax.dynamic_slice_in_dim(small_grad, d * (width // n_dp), width // n_dp, 1)
     dmod_cols = lax.dynamic_slice_in_dim(dmod, t * part, part, 3)
-    cond_cols = lax.dynamic_slice_in_dim(conds, d * (cond_width // n_dp), cond_width // n_dp, 2)
-    ada_grad = jnp.sum(cond_cols[:, :, None, :, None] * dmod_cols[:, :, :, None, :], axis=(0, 1))
+    ada_grad = jnp.sum(conds[:, :, None, :, None] * dmod_cols[:, :, :, None, :], axis=(0, 1))
 
     am, av = jnp.transpose(ada_first[0], (1, 0, 2)), jnp.transpose(ada_second[0], (1, 0, 2))
     ada_m, ada_v = adam_parts(ada_grad, am, av)

time: 385 us -> 328 us (0.85)
  Pallas kernels: 327 us -> 285 us
  local copies, waits for them, and re-layouts: 24.9 us -> 15.2 us
  other arithmetic: 30.4 us -> 26.5 us
    pallas_call x7 -> x1, Pallas kernels: 138 us -> 96.6 us  [forward(): pl.pallas_call(functools.partial(forward_kernel, direct, cores, n_tp, nam...]
    unnamed x115 -> x65, local copies, waits for them, and re-layouts: 18.6 us -> 7.26 us
where the time goes in v2:
time: 328 us; the launch traced here: 327 us
  Pallas kernels  285 us (87%)
  other arithmetic  26.5 us (8%)
  local copies, waits for them, and re-layouts  15.2 us (5%)
    pallas_call x1, Pallas kernels, step_exchange(): pl.pallas_call(functools.partial(step_kernel, cores), out_shape=(jax.Shap...  113 us
    pallas_call x1, Pallas kernels, forward(): pl.pallas_call(functools.partial(forward_kernel, direct, cores, n_tp, nam...  96.6 us
    pallas_call x1, Pallas kernels, last(): pl.pallas_call(functools.partial(last_kernel, cores, spans), out_shape=(j...  42.9 us
    pallas_call x1, Pallas kernels, pull_attention(): pl.pallas_call(body, grid=(pairs,), out_shape=(jax.ShapeDtypeStruct((leng...  31.9 us
    unnamed x65, local copies, waits for them, and re-layouts  7.26 us

profile of v2, /device:TPU:0, one launch (start us, length us, event | category | flops | bytes accessed | tf_op | source)
XLA Modules:
  0.0 327.2 jit_solution(8871667080256590596)
XLA Ops:
  0.7 96.6 %forward.1 = (bf16[1024,768]{1,0:T(8,128)(2,1)}, bf16[4,384,768]{2,1,0:T(8,128)(2,1)}, bf16[384,1024]{1,0:T(8,128)(2,1)}, bf16[384,1024]{1,0:T(8,128)(2,1)}, bf1...) custom-call(s32[2]{0:T(128)} %args_0_.4, ...), custom_call_target="tpu_custom_call" | custom-call | tf_op jit(solution)/shard_map/forward/pallas_call | solution.py:555
  97.3 1.9 slice_bitcast_fusion.wo
  99.2 0.8 reduce
  100.0 0.6 reshape.117.inv
  100.7 2.8 slice.31.wq
  103.5 31.9 %attention_pull.1 = (bf16[1024,768]{1,0:T(8,128)(2,1)}, bf16[3,384,768]{2,1,0:T(8,128)(2,1)}, bf16[384,768]{1,0:T(8,128)(2,1)}) custom-call(bf16[1024,768]{1,0:T(8,128)(2,1)} %get-tuple-element.55.ga, bf16[384,768]{1,0:T(8,128)(2,1)} %slice_bitcast_fusion.wo, bf16[384,1024]{1,0:T(8,128)(2,1)} %get-tuple-element.57.o_t, f32[3,2,1024]{2,1,0:T(2,128)} %reshape.117.inv, ...), custom_call_target="tpu_custom_call" | custom-call | tf_op jit(solution)/shard_map/attention_pull/pallas_call | solution.py:626
  135.4 0.0 copy-start
  135.4 1.6 dynamic-slice_bitcast_fusion.tok
  137.0 0.0 copy-done.28
  137.1 0.2 copy-done
  137.3 1.4 copy-done.1
  138.7 1.1 copy-done.2
  139.8 0.8 copy-done.3
  140.6 0.7 copy-done.4
  141.3 42.9 %last_norm.1 = (bf16[2,1024,768]{2,1,0:T(8,128)(2,1)}, bf16[2,1024,768]{2,1,0:T(8,128)(2,1)}, f32[4,2,16,768]{3,2,1,0:T(8,128)S(1)}) custom-call(bf16[1024,768]{1,0:T(8,128)(2,1)S(1)} %copy-done.1, f32[512,768]{1,0:T(8,128)S(1)} %copy-done, bf16[1024,768]{1,0:T(8,128)(2,1)S(1)} %dynamic-slice_bitcast_fusion.tok, bf16[512,768]{1,0:T(8,128)(2,1)S(1)} %copy-done.2, ...), custom_call_target="tpu_custom_call" | custom-call | tf_op jit(solution)/shard_map/last_norm/pallas_call | solution.py:770
  184.2 0.0 copy-start.11
  184.2 0.0 copy-start.15
  184.3 0.0 copy-start.16
  184.3 5.2 %convert_element_type.12 = f32[2,1024,768]{2,1,0:T(8,128)} convert(bf16[2,1024,768]{2,1,0:T(8,128)(2,1)} %get-tuple-element.71) | non-fusion elementwise | flops 1572864 | bytes 9437184 | tf_op jit(solution)/shard_map/convert_element_type | solution.py:1125
  189.5 0.0 copy-start.26
  189.5 0.0 copy-start.27
  189.5 0.1 constant_dynamic-slice_fusion.1
  189.6 0.7 slice_bitcast_fusion.1
  190.3 0.2 multiply_reduce_fusion
  190.5 0.0 copy-done.11
  190.5 0.0 copy-done.15
  190.6 0.0 copy-done.16
  190.6 1.0 fusion.18.ea
  191.6 0.0 copy-done.21
  191.6 0.1 fusion.23
  191.7 0.0 copy-done.19
  191.7 0.0 copy-done.25
  191.7 0.6 fusion.22
  192.4 0.1 reshape.120
  192.5 0.1 constant_dynamic-slice_fusion
  192.6 0.0 copy-done.24
  192.6 0.0 copy-done.26
  192.6 0.0 copy-done.27
  192.6 0.6 add_multiply_fusion.1.eb
  193.2 113.1 %step_exchange.1 = (f32[12,192,384]{2,1,0:T(8,128)}, bf16[12,192,384]{2,1,0:T(8,128)(2,1)}, bf16[6,64,192]{2,1,0:T(8,128)(2,1)}, f32[9,384]{1,0:T(8,128)}, f32[4,96]{1,0:T(4,128)}) custom-call(bf16[3,384,768]{2,1,0:T(8,128)(2,1)} %get-tuple-element.72.gq, bf16[384,768]{1,0:T(8,128)(2,1)} %get-tuple-element.73.go, bf16[4,384,768]{2,1,0:T(8,128)(2,1)} %get-tuple-element.74.gu, ...), custom_call_target="tpu_custom_call" | custom-call | tf_op jit(solution)/shard_map/step_exchange/pallas_call | solution.py:1012
  306.4 0.0 copy-done.7
  306.4 0.0 copy-start.9
  306.4 0.0 copy-start.10
  306.4 4.3 %fusion.1 = (f32[1,384,7,192]{1,3,2,0:T(8,128)}, f32[1,384,7,192]{1,3,2,0:T(8,128)}) fusion(f32[12,192,384]{2,1,0:T(8,128)} %get-tuple-element.78, f32[1,384,7,192]{1,3,2,0:T(8,128)S(1)} %copy-done.8, f32[1,384,7,192]{1,3,2,0:T(8,128)S(1)} %copy-done.7), kind=kLoop, calls=%fused_computation.3 | loop fusion | flops 3612672 | bytes 10321920 | tf_op jit(solution)/shard_map/broadcast_in_dim | solution.py:1193
  310.7 0.0 copy-done.10
  310.7 0.0 copy-start.14
  310.7 3.6 %fusion.5 = (f32[1,5,192,384]{3,2,1,0:T(8,128)}, f32[1,5,192,384]{3,2,1,0:T(8,128)}) fusion(f32[12,192,384]{2,1,0:T(8,128)} %get-tuple-element.78, f32[1,5,192,384]{3,2,1,0:T(8,128)S(1)} %copy-done.10, f32[1,5,192,384]{3,2,1,0:T(8,128)S(1)} %copy-done.9), kind=kLoop, calls=%fused_computation.13 | loop fusion | flops 2580480 | bytes 7372800 | tf_op jit(solution)/shard_map/broadcast_in_dim | solution.py:1193
  314.3 1.0 fusion.13
  315.3 0.6 copy.75
  315.9 0.6 fusion.29
  316.5 0.6 copy.76
  317.1 0.0 copy-done.13
  317.1 0.0 copy-start.17
  317.1 3.3 %fusion.3 = (f32[384,7,192]{0,2,1:T(8,128)}, f32[384,7,192]{0,2,1:T(8,128)}, f32[384,7,192]{0,2,1:T(8,128)}) fusion(f32[384,7,192]{0,2,1:T(8,128)S(1)} %copy-done.13, bf16[12,192,384]{2,1,0:T(8,128)(2,1)S(1)} %copy-done.14, f32[384,7,192]{0,2,1:T(8,128)S(1)} %copy-done.5), kind=kLoop, calls=%fused_computation.9 | loop fusion | flops 4128768 | bytes 11354112 | tf_op jit(solution)/shard_map/transpose | solution.py:1180
  320.5 0.0 copy-done.6
  320.5 2.6 multiply_subtract_fusion
  323.2 0.0 copy-done.18
  323.2 0.0 copy-done.20
  323.2 1.1 fusion.19
  324.3 0.0 copy-done.22
  324.3 0.6 multiply_subtract_fusion.1
  325.0 0.0 copy-done.29
  325.0 0.6 multiply_subtract_fusion.2
  325.6 1.7 copy.95
  (36 shorter events, 0.2 us)
Async XLA Ops:
  135.4 1.7 copy-start.28
  135.4 1.9 copy-start
  137.3 1.4 copy-start.1
  138.7 1.1 copy-start.2
  139.8 0.8 copy-start.3
  140.6 0.7 copy-start.4
  184.2 6.3 %copy-start.11 = (f32[64,6,192]{2,0,1:T(8,128)S(1)}, f32[64,6,192]{2,0,1:T(8,128)}, u32[]{:S(2)}) copy-start(f32[64,6,192]{2,0,1:T(8,128)} %param.34) | copy-start | bytes 884740
  184.2 6.3 %copy-start.15 = (f32[1,64,6,192]{3,1,2,0:T(8,128)S(1)}, f32[1,64,6,192]{3,1,2,0:T(8,128)}, u32[]{:S(2)}) copy-start(f32[1,64,6,192]{3,1,2,0:T(8,128)} %param.44) | copy-start | bytes 884740
  184.3 6.3 %copy-start.16 = (f32[1,64,6,192]{3,1,2,0:T(8,128)S(1)}, f32[1,64,6,192]{3,1,2,0:T(8,128)}, u32[]{:S(2)}) copy-start(f32[1,64,6,192]{3,1,2,0:T(8,128)} %param.39) | copy-start | bytes 884740
  189.4 2.2 copy-start.21
  189.4 2.3 copy-start.19
  189.4 2.3 copy-start.25
  189.4 3.1 copy-start.24
  189.5 3.1 copy-start.26
  189.5 3.1 copy-start.27
  193.2 113.2 %copy-start.7 = (f32[1,384,7,192]{1,3,2,0:T(8,128)S(1)}, f32[1,384,7,192]{1,3,2,0:T(8,128)}, u32[]{:S(2)}) copy-start(f32[1,384,7,192]{1,3,2,0:T(8,128)} %param.37) | copy-start | bytes 6193156
  193.2 113.2 %copy-start.8 = (f32[1,384,7,192]{1,3,2,0:T(8,128)S(1)}, f32[1,384,7,192]{1,3,2,0:T(8,128)}, u32[]{:S(2)}) copy-start(f32[1,384,7,192]{1,3,2,0:T(8,128)} %param.42) | copy-start | bytes 6193156
  306.4 4.3 %copy-start.9 = (f32[1,5,192,384]{3,2,1,0:T(8,128)S(1)}, f32[1,5,192,384]{3,2,1,0:T(8,128)}, u32[]{:S(2)}) copy-start(f32[1,5,192,384]{3,2,1,0:T(8,128)} %param.38) | copy-start | bytes 4423684
  306.4 4.3 %copy-start.10 = (f32[1,5,192,384]{3,2,1,0:T(8,128)S(1)}, f32[1,5,192,384]{3,2,1,0:T(8,128)}, u32[]{:S(2)}) copy-start(f32[1,5,192,384]{3,2,1,0:T(8,128)} %param.43) | copy-start | bytes 4423684
  310.7 6.4 %copy-start.13 = (f32[384,7,192]{0,2,1:T(8,128)S(1)}, f32[384,7,192]{0,2,1:T(8,128)}, u32[]{:S(2)}) copy-start(f32[384,7,192]{0,2,1:T(8,128)} %param.47) | copy-start | bytes 6193156
  310.7 6.4 %copy-start.14 = (bf16[12,192,384]{2,1,0:T(8,128)(2,1)S(1)}, bf16[12,192,384]{2,1,0:T(8,128)(2,1)}, u32[]{:S(2)}) copy-start(bf16[12,192,384]{2,1,0:T(8,128)(2,1)} %get-tuple-element.79) | copy-start | bytes 5308420
  314.3 2.8 copy-start.5
  317.1 3.4 %copy-start.6 = (f32[5,192,384]{2,1,0:T(8,128)S(1)}, f32[5,192,384]{2,1,0:T(8,128)}, u32[]{:S(2)}) copy-start(f32[5,192,384]{2,1,0:T(8,128)} %wb.1) | copy-start | bytes 4423684
  317.1 3.4 %copy-start.17 = (f32[5,192,384]{2,1,0:T(8,128)S(1)}, f32[5,192,384]{2,1,0:T(8,128)}, u32[]{:S(2)}) copy-start(f32[5,192,384]{2,1,0:T(8,128)} %param.48) | copy-start | bytes 4423684
  320.5 2.7 copy-start.18
  320.5 2.7 copy-start.20
  320.5 5.1 %copy-start.12 = (bf16[2,1024,768]{2,1,0:T(8,128)(2,1)S(1)}, bf16[2,1024,768]{2,1,0:T(8,128)(2,1)}, u32[]{:S(2)}) copy-start(bf16[2,1024,768]{2,1,0:T(8,128)(2,1)} %get-tuple-element.247) | copy-start | bytes 9437188
  323.1 1.2 copy-start.22
  323.1 1.2 copy-start.23
  323.1 1.8 copy-start.29
  323.2 1.8 copy-start.30

commit v3 on v2

v3 whole, which is shorter than its diff:
```python
import functools
from types import SimpleNamespace

import jax
import jax.numpy as jnp
import numpy as np
from jax import lax
from jax.experimental import pallas as pl
from jax.experimental.pallas import tpu as pltpu
from jax.sharding import PartitionSpec as P

HEAD_DIM = 64
STEP = 10
MESH = pl.DeviceIdType.MESH
ANY = pl.BlockSpec(memory_space=pl.ANY)
VMEM = pl.BlockSpec(memory_space=pltpu.VMEM)
MIB = 2**20

f32 = jnp.float32
bf16 = jnp.bfloat16
highest = lax.Precision.HIGHEST
norm_eps = 1e-05
beta_one = 0.9
beta_two = 0.999
adam_eps = 1e-08
decay_rate = 0.1
rate_matrix = 0.03
rate_small = 0.3
outer_mu = 0.9
outer_rate = 0.7
gelu_a = 0.7978845608028654
gelu_b = 0.044715


def nn(a, b):
    return lax.dot_general(a, b, (((1,), (0,)), ((), ())), preferred_element_type=f32)


def nt(a, b):
    return lax.dot_general(a, b, (((1,), (1,)), ((), ())), preferred_element_type=f32)


def tn(a, b):
    return lax.dot_general(a, b, (((0,), (0,)), ((), ())), preferred_element_type=f32)


def fold(values):
    return jnp.sum(values.reshape(values.shape[0] // 8, 8, values.shape[1]), axis=0)


def normalize(values):
    mean = jnp.mean(values, axis=-1, keepdims=True)
    centered = values - mean
    variance = jnp.mean(centered * centered, axis=-1, keepdims=True)
    inverse = lax.rsqrt(variance + norm_eps)
    return centered * inverse, inverse


def norm_pull(grad_hat, hat, inverse):
    first = jnp.mean(grad_hat, axis=-1, keepdims=True)
    second = jnp.mean(grad_hat * hat, axis=-1, keepdims=True)
    return inverse * (grad_hat - first - hat * second)


def adam_parts(gradient, first, second):
    first_new = beta_one * first + (1.0 - beta_one) * gradient
    second_new = beta_two * second + (1.0 - beta_two) * gradient * gradient
    return first_new, second_new


def adam_diff(weight, first_new, second_new, rate, decay):
    first_hat = first_new / (1.0 - beta_one**STEP)
    second_hat = second_new / (1.0 - beta_two**STEP)
    return rate * (first_hat / (jnp.sqrt(second_hat) + adam_eps) + decay * weight)


def at(start, size, unit=128):
    return pl.ds(pl.multiple_of(start, unit), size)


def remote(source, target, send, recv, device):
    return pltpu.make_async_remote_copy(
        src_ref=source, dst_ref=target, send_sem=send, recv_sem=recv, device_id=device, device_id_type=MESH)


def turn(values, cosine, sine):
    heads = values.shape[0] // HEAD_DIM
    half = HEAD_DIM // 2
    out = []
    for h in range(heads):
        low = values[h * HEAD_DIM : h * HEAD_DIM + half]
        high = values[h * HEAD_DIM + half : (h + 1) * HEAD_DIM]
        out.append(low * cosine - high * sine)
        out.append(high * cosine + low * sine)
    return jnp.concatenate(out, axis=0)


def only_head(pair, h):
    row = lax.broadcasted_iota(jnp.int32, pair.shape, 0)
    return jnp.where(row // HEAD_DIM == h, pair, jnp.zeros_like(pair))


def greet(devices):
    barrier = pltpu.get_barrier_semaphore()
    for device in devices:
        pl.semaphore_signal(barrier, inc=1, device_id=device, device_id_type=MESH)
    pl.semaphore_wait(barrier, len(devices))


def plane_devices(t, d, n_tp, spans):
    others = []
    for dt in range(n_tp):
        for dd in range(spans):
            if dt or dd:
                dev = {"tp": lax.rem(t + dt, n_tp)}
                if spans > 1:
                    dev["dp"] = lax.rem(d + dd, spans)
                others.append(dev)
    return others


def forward_kernel(direct, cores, n_tp, names, *args):
    R = SimpleNamespace(**dict(zip(names, args)))
    t, d = lax.axis_index("tp"), lax.axis_index("dp")
    s = t // cores
    c = lax.rem(t, cores)
    length, width = R.tok.shape
    half = length // cores
    slot_rows = R.weights.shape[1]
    rows, cols = slot_rows // 2, width // 2
    own, other = at(c * half, half), at((1 - c) * half, half)
    sibling = {"tp": s * cores + (1 - c)}
    xdev = {"dp": 1 - d}
    ydev = {"tp": (1 - s) * cores + c}

    tok_load = pltpu.make_async_copy(R.tok_all.at[s], R.tok, R.load_sem.at[0])
    cot_load = pltpu.make_async_copy(R.cot_all.at[s], R.cot, R.load_sem.at[1])

    if direct:
        stages = (R.attn, R.x1, R.away)

        def staged(a):
            return stages[a // 4].at[pl.ds((a % 4 // 2) * rows, rows), pl.ds((a % 2) * cols, cols)]

        weight_loads = []
        for a in range(12):
            source = R.wi.at[a] if a < 3 else R.wb.at[0] if a == 3 else R.wi.at[a - 1] if a < 8 else R.wb.at[a - 7]
            weight_loads.append(pltpu.make_async_copy(source, staged(a), R.stage_sem.at[a]))
            weight_loads[a].start()
    else:
        weight_load = pltpu.make_async_copy(R.weights_in, R.weights, R.stage_sem.at[0])
        weight_load.start()
    tok_load.start()
    cot_load.start()

    def block(a, ss, dd):
        return R.weights.at[a, at(ss * rows, rows, 16), at(dd * cols, cols)]

    def hop(kind, a):
        if kind == 0:
            ref, dev = block(a, s, d), xdev
        elif kind == 1:
            ref, dev = block(a, s, d), ydev
        elif kind == 2:
            ref, dev = block(a, s, 1 - d), ydev
        else:
            ref, dev = block(a, 1 - s, d), xdev
        k = min(kind, 2)
        return remote(ref, ref, R.wsend.at[k, a], R.wrecv.at[k, a], dev)

    ahead = 2

    def launch(a):
        hop(0, a).start()
        hop(1, a).start()

    def pass_on(a):
        @pl.when(lax.rem(a, 2) == 0)
        def _():
            hop(0, a).wait_recv()
            hop(2, a).start()

        @pl.when(lax.rem(a, 2) == 1)
        def _():
            hop(1, a).wait_recv()
            hop(3, a).start()

        @pl.when(a + ahead < 12)
        def _():
            launch(a + ahead)

    def arrived(a):
        hop(1 - a % 2, a).wait_recv()
        hop(2 + a % 2, a).wait_recv()

    if direct:
        others = plane_devices(t, d, n_tp, 2)
        R.cond[...] = jnp.zeros_like(R.cond)
        for ss in range(2):
            row = R.table[pl.ds(R.sigma[ss], 1), :]
            R.cond[ss : ss + 1, :] = (row / (1.0 + jnp.exp(-row))).astype(bf16).astype(f32)
        turned = pltpu.roll(R.cond[...], R.cond.shape[1] // 2, 1)
        R.cond_near[...] = jnp.where(d == 0, R.cond[...], turned)
        R.cond_far[...] = jnp.where(d == 1, R.cond[...], turned)
        R.ps_low[...] = R.ps[...].astype(bf16).astype(f32)
        R.bu_low[...] = R.bu[...].astype(bf16).astype(f32)
        greet(others)
        cc = remote(R.cond_far, R.cond_got, R.small_sem.at[0, 0], R.small_sem.at[1, 0], xdev)
        cc.start()
        pc = remote(R.ps_low, R.ps_all.at[d], R.small_sem.at[0, 1], R.small_sem.at[1, 1], xdev)
        pc.start()
        bcs = []
        for i, (ds, dd) in enumerate(((0, 1), (1, 0), (1, 1))):
            dev = {"tp": lax.rem(s + ds, 2) * cores + c, "dp": lax.rem(d + dd, 2)}
            bcs.append(remote(R.bu_low, R.bu_all.at[s, d], R.small_sem.at[0, 2 + i], R.small_sem.at[1, 2 + i], dev))
            bcs[i].start()

        def prepare(a):
            weight_loads[a].wait()
            R.weights[a, at(s * rows, rows, 16), at(d * cols, cols)] = staged(a)[...].astype(bf16)

        for a in range(ahead):
            prepare(a)
            launch(a)
        R.ps_all[d] = R.ps_low[...]
        R.bu_all[s, d] = R.bu_low[...]
        span = R.wa.shape[1]
        R.parts[...] = jnp.zeros_like(R.parts)

        def partial_mod(source, dd):
            lhs = source[...][:, :span].astype(bf16)
            for a in range(6):
                product = nn(lhs, R.wa[a].astype(bf16))
                for ss in range(2):
                    R.parts[dd, ss, a : a + 1, :] = product[ss : ss + 1]

        partial_mod(R.cond_near, d)
        cc.wait()
        partial_mod(R.cond_got, 1 - d)
        mods = []
        for i, dev in enumerate(others):
            mods.append(remote(
                R.parts.at[dev["dp"], dev["tp"] // cores], R.mod_got.at[t, d], R.mod_sem.at[0, i], R.mod_sem.at[1, i], dev))
            mods[i].start()
        R.mod_got[t, d] = R.parts[d, s]
        R.cond_out[d] = R.cond_near[...]
        R.cond_out[1 - d] = R.cond_got[...]
        for a in range(ahead, 12):
            prepare(a)
        pc.wait()
        for bc in bcs:
            bc.wait()
        for mc in mods:
            mc.wait()
        small_rows = jnp.concatenate([R.ps_all[0], R.ps_all[1]], axis=1)
        mod_rows = jnp.concatenate([R.mod_got[tt, 0] + R.mod_got[tt, 1] for tt in range(n_tp)], axis=1)
        R.vecs[...] = jnp.zeros_like(R.vecs)
        R.vecs[0:3] = small_rows[0:3]
        R.vecs[3:9] = mod_rows[0:6] + small_rows[3:9]
        R.bias[...] = jnp.concatenate(
            [R.bu_all[ss, dd, j : j + 1, :] for j in range(4) for ss in range(2) for dd in range(2)], axis=1)
    else:
        greet([sibling])
        R.vecs[...] = R.vecs_in[...]
        R.bias[...] = R.bias_in[...]
        R.cond_out[...] = jnp.zeros_like(R.cond_out)

    tok_load.wait()
    step = 256

    @pl.loop(0, length // step)
    def _(i):
        r = at(i * step, step)
        hat, _ = normalize(R.tok[r].astype(f32))
        hidden = hat * (R.vecs[0:1] * (1.0 + R.vecs[4:5])) + R.vecs[3:4]
        R.h1[r] = hidden.astype(bf16)

    outs = []

    def emit(source, target):
        cp = pltpu.make_async_copy(source, target, R.out_sem.at[len(outs)])
        cp.start()
        outs.append(cp)

    emit(R.h1, R.h1_out)

    if direct:
        for a in range(3):
            pass_on(a)
        for a in range(3):
            arrived(a)
    else:
        weight_load.wait()
    @pl.loop(0, length // step)
    def _(i):
        r = at(i * step, step)
        low = R.h1[r]
        cos, sin = R.cosine[:, r], R.sine[:, r]
        R.q_t[:, r] = (turn(nt(R.weights[0], low), cos, sin) * 0.125).astype(bf16)
        keys = turn(nt(R.weights[1], low), cos, sin).astype(bf16)
        R.k_t[:, r] = keys
        R.k_r[r] = keys.T
        values = nt(R.weights[2], low).astype(bf16)
        R.v_t[:, r] = values
        R.v_r[r] = values.T

    emit(R.q_t, R.q_out)
    emit(R.k_t, R.k_out)
    emit(R.v_r, R.v_out)

    if direct:
        pass_on(3)
    heads = R.probs.shape[0]

    @pl.loop(0, heads)
    def _(h):
        pair = at(h // 2 * 2 * HEAD_DIM, 2 * HEAD_DIM)
        one = at(h * HEAD_DIM, HEAD_DIM, HEAD_DIM)
        scores = nn(R.k_r[:, pair], only_head(R.q_t[pair, :], lax.rem(h, 2)))
        top = jnp.max(scores, axis=0, keepdims=True)
        shifted = jnp.exp(scores - top)
        inverse = 1.0 / jnp.sum(shifted, axis=0, keepdims=True)
        low = shifted.astype(bf16)
        R.probs[h] = low
        R.inv_out[h] = inverse
        R.o_t[one, :] = (nn(R.v_t[one, :], low) * inverse).astype(bf16)
        if direct:
            @pl.when(lax.rem(h, 2) == 0)
            def _():
                pass_on(4 + h // 2)

    for h in range(heads):
        emit(R.probs.at[h], R.probs_out.at[h])
    emit(R.o_t, R.o_out)

    if direct:
        arrived(3)
    emit(R.weights.at[pl.ds(0, 4)], R.weights_out.at[pl.ds(0, 4)])
    away = remote(R.away, R.got, R.pair_sem.at[0, 0], R.pair_sem.at[1, 0], sibling)
    R.away[...] = tn(R.o_t[:, other], R.weights[3])
    away.start()
    R.attn[...] = tn(R.o_t[:, own], R.weights[3])
    if direct:
        pass_on(7)
    away.wait()
    small = 128

    @pl.loop(0, half // small)
    def _(i):
        r = at(i * small, small)
        total = R.attn[r] + R.got[r]
        R.attn[r] = total
        after = R.tok[at(c * half + i * small, small)].astype(f32) + R.vecs[5:6] * total
        R.x1[r] = after
        hat, _ = normalize(after)
        hidden = hat * (R.vecs[1:2] * (1.0 + R.vecs[7:8])) + R.vecs[6:7]
        R.h2[at(c * half + i * small, small)] = hidden.astype(bf16)

    share = remote(R.h2.at[own], R.h2.at[own], R.pair_sem.at[0, 1], R.pair_sem.at[1, 1], sibling)
    share.start()
    for cp in outs:
        cp.wait()
    flags = jnp.broadcast_to(R.flags[pl.ds(s, 1), :].astype(f32), (128, length)).T
    R.column[...] = flags
    cot_load.wait()

    chunks = 2
    if direct:
        pass_on(8)
        for a in range(4, 8):
            arrived(a)
    outs.clear()
    emit(R.weights.at[pl.ds(4, 4)], R.weights_out.at[pl.ds(4, 4)])
    emit(R.attn, R.attn_out)
    emit(R.x1, R.x1_out)
    emit(R.vecs, R.vecs_out)

    def up(r):
        low = R.h2[r]
        grad = R.cot[r].astype(f32) * jnp.concatenate([R.column[r]] * (width // 128), axis=1)
        R.cot[r] = grad.astype(bf16)
        R.probs[4, r, 0:width] = (R.vecs[8:9] * grad).astype(bf16)
        for j in range(chunks):
            pair = R.weights[4 + 2 * j : 6 + 2 * j].reshape(2 * slot_rows, width)
            u = nt(low, pair) + R.bias[:, j * width : (j + 1) * width]
            square = u * u
            inner = jnp.tanh(gelu_a * (u + gelu_b * square * u))
            z = 0.5 * u * (1.0 + inner)
            slope = 0.5 * (1.0 + inner) + 0.5 * u * (1.0 - inner * inner) * gelu_a * (1.0 + 3.0 * gelu_b * square)
            R.probs[j, r, 0:width] = z.astype(bf16)
            R.probs[2 + j, r, 0:width] = slope.astype(bf16)

    @pl.loop(0, half // step)
    def _(i):
        up(at(c * half + i * step, step))

    if direct:
        pass_on(9)
    share.wait()
    emit(R.h2, R.h2_out)
    emit(R.cot.at[own], R.gy_out)

    @pl.loop(0, half // step)
    def _(i):
        up(at((1 - c) * half + i * step, step))

    for k in range(4):
        emit(R.probs.at[k, :, pl.ds(0, width)], R.hidden_out.at[k])
    emit(R.probs.at[4, :, pl.ds(0, width)], R.gm_out)
    if direct:
        pass_on(10)

    for k in range(4):
        where = pl.ds((k % 2) * slot_rows, slot_rows)
        R.gd[k] = tn(R.probs[k // 2, :, where], R.probs[4, :, 0:width]).astype(bf16)
        if k == 1 and direct:
            pass_on(11)
    emit(R.gd, R.gd_out)
    if direct:
        for a in range(8, 12):
            arrived(a)
    emit(R.weights.at[pl.ds(8, 4)], R.weights_out.at[pl.ds(8, 4)])
    if direct:
        for a in range(12):
            hop(0, a).wait_send()
            hop(1, a).wait_send()
            hop(2 + a % 2, a).wait_send()
    for cp in outs:
        cp.wait()


def forward(direct, cores, length, width, slot_rows, first, tokens, flags, cotangent, cosine, sine):
    n_tp = lax.axis_size("tp")
    half = length // cores
    heads = slot_rows // HEAD_DIM
    dma = pltpu.SemaphoreType.DMA
    smem = pl.BlockSpec(memory_space=pltpu.SMEM)
    arr = jax.ShapeDtypeStruct
    vm = pltpu.VMEM
    if direct:
        ins = dict(sigma=smem, table=VMEM, wa=VMEM, ps=VMEM, bu=VMEM, wi=ANY, wb=ANY)
    else:
        ins = dict(weights_in=ANY, vecs_in=VMEM, bias_in=VMEM)
    ins |= dict(tok_all=ANY, flags=VMEM, cot_all=ANY, cosine=VMEM, sine=VMEM)
    outs = dict(
        h1_out=(arr((length, width), bf16), ANY),
        weights_out=(arr((12, slot_rows, width), bf16), ANY),
        q_out=(arr((slot_rows, length), bf16), ANY),
        k_out=(arr((slot_rows, length), bf16), ANY),
        v_out=(arr((length, slot_rows), bf16), ANY),
        probs_out=(arr((heads, length, length), bf16), ANY),
        inv_out=(arr((heads, 1, length), f32), VMEM),
        o_out=(arr((slot_rows, length), bf16), ANY),
        attn_out=(arr((half, width), f32), ANY),
        x1_out=(arr((half, width), f32), ANY),
        h2_out=(arr((length, width), bf16), ANY),
        vecs_out=(arr((16, width), f32), ANY),
        hidden_out=(arr((4, length, width), bf16), ANY),
        gm_out=(arr((length, width), bf16), ANY),
        gy_out=(arr((half, width), bf16), ANY),
        gd_out=(arr((4, slot_rows, width), bf16), ANY),
        cond_out=(arr((2, 8, 128), f32), VMEM),
    )
    scratch = dict(
        tok=vm((length, width), bf16),
        cot=vm((length, width), bf16),
        weights=vm((12, slot_rows, width), bf16),
        h1=vm((length, width), bf16),
        q_t=vm((slot_rows, length), bf16),
        k_t=vm((slot_rows, length), bf16),
        v_t=vm((slot_rows, length), bf16),
        k_r=vm((length, slot_rows), bf16),
        v_r=vm((length, slot_rows), bf16),
        probs=vm((heads, length, length), bf16),
        o_t=vm((slot_rows, length), bf16),
        away=vm((half, width), f32),
        got=vm((half, width), f32),
        attn=vm((half, width), f32),
        x1=vm((half, width), f32),
        h2=vm((length, width), bf16),
        column=vm((length, 128), f32),
        bias=vm((1, 4 * slot_rows), f32),
        vecs=vm((16, width), f32),
        gd=vm((4, slot_rows, width), bf16),
        load_sem=dma((2,)),
        stage_sem=dma((12,)),
        out_sem=dma((20,)),
        pair_sem=dma((2, 2)),
    )
    if direct:
        wa, ps, bu = first[2:5]
        scratch |= dict(
            cond=vm((8, 128), f32),
            cond_near=vm((8, 128), f32),
            cond_far=vm((8, 128), f32),
            cond_got=vm((8, 128), f32),
            ps_low=vm(ps.shape, f32),
            bu_low=vm(bu.shape, f32),
            ps_all=vm((2,) + ps.shape, f32),
            bu_all=vm((2, 2) + bu.shape, f32),
            parts=vm((2, 2, 8, wa.shape[2]), f32),
            mod_got=vm((n_tp, 2, 8, wa.shape[2]), f32),
            wsend=dma((3, 12)),
            wrecv=dma((3, 12)),
            small_sem=dma((2, 5)),
            mod_sem=dma((2, 2 * n_tp - 1)),
        )
    names = list(ins) + list(outs) + list(scratch)
    results = pl.pallas_call(
        functools.partial(forward_kernel, direct, cores, n_tp, names),
        out_shape=tuple(o[0] for o in outs.values()),
        in_specs=list(ins.values()),
        out_specs=tuple(o[1] for o in outs.values()),
        scratch_shapes=list(scratch.values()),
        compiler_params=pltpu.CompilerParams(collective_id=0, has_side_effects=True, vmem_limit_bytes=60 * MIB),
        name="forward",
    )(*first, tokens, flags, cotangent, cosine, sine)
    return SimpleNamespace(**dict(zip(outs, results)))


def backward_kernel(direct, cores, n_tp, names, *args):
    R = SimpleNamespace(**dict(zip(names, args)))
    t, g = lax.axis_index("tp"), lax.axis_index("grp")
    spans = 2 if direct else 1
    d = lax.axis_index("dp") if direct else 0
    s = t // cores
    c = lax.rem(t, cores)
    length, width = R.ga.shape
    half = length // cores
    slot_rows = R.weights.shape[1]
    rows, cols = slot_rows // 2, width // 2
    own, other = at(c * half, half), at((1 - c) * half, half)
    sibling = {"tp": s * cores + (1 - c)}
    across = {"tp": (1 - s) * cores + c}
    xdev = {"dp": 1 - d}
    heads = R.inv.shape[0]
    others = plane_devices(t, d, n_tp, spans)

    def load(source, target, i):
        cp = pltpu.make_async_copy(source, target, R.load_sem.at[i])
        cp.start()
        return cp

    def load_probs(h, slot):
        return pltpu.make_async_copy(R.probs_in.at[h], R.spare.at[slot], R.probs_sem.at[slot])

    spare = R.spare
    if direct:
        gd_load = pltpu.make_async_copy(R.gd_in, R.weights.at[pl.ds(12, 4)], R.gd_sem)
        gd_load.start()
        greet(others + [{"grp": lax.rem(g + 1 + i, 4)} for i in range(3)])
    else:
        greet(others)
    loads = [load(R.weights_in.at[pl.ds(8, 4)], R.weights.at[pl.ds(8, 4)], 0), load(R.gm_in, spare.at[4, :, pl.ds(0, width)], 1)]
    for k in (2, 3, 0, 1):
        loads.append(load(R.hidden_in.at[k], spare.at[k, :, pl.ds(0, width)], 2 + k))
    loads.append(load(R.weights_in.at[pl.ds(0, 8)], R.weights.at[pl.ds(0, 8)], 6))
    for i, (source, target) in enumerate((
        (R.x1_in, R.x1), (R.attn_in, R.attn), (R.gy_in, R.gy), (R.h2_in, R.hid), (R.o_in, R.o_t), (R.v_in, R.v_r),
        (R.k_in, R.k_t), (R.q_in, R.q_t))):
        loads.append(load(source, target, 7 + i))

    inner = jnp.logical_or(g == 1, g == 2)
    outer = jnp.logical_not(inner)
    pair = jnp.where(g == 0, 1, jnp.where(g == 1, 0, jnp.where(g == 2, 3, 2)))
    pdev = {"grp": pair}
    mdev = {"grp": 3 - g}
    mine = jnp.where(g == 1, 0, 1)
    hrows = rows // 2
    n_slots = 12
    window = 3

    pieces = 4
    size = half // pieces

    def piece(k):
        return at(c * half + k * size, size)

    def spread(kind, target):
        copies = (
            remote(R.half_out, target.at[s, own], R.spread_sem.at[0, kind, 0], R.spread_sem.at[1, kind, 0], sibling),
            pltpu.make_async_copy(R.half_out, target.at[s, own], R.spread_sem.at[0, kind, 1]),
        )
        for cp in copies:
            cp.start()
        return copies

    def cross(kind, target, k):
        source = R.half_out.at[at(k * size, size)]
        return remote(source, target.at[s, piece(k)], R.cross_sem.at[0, kind, k], R.cross_sem.at[1, kind, k], across)

    def relay(kind, target, k):
        ref = target.at[1 - s, piece(k)]
        return remote(ref, ref, R.relay_sem.at[0, kind, k], R.relay_sem.at[1, kind, k], sibling)

    def pass_piece(kind, target, k):
        cross(kind, target, k).wait_recv()
        relay(kind, target, k).start()

    def place(a):
        return jnp.where(a < 4, a + 12, jnp.where(a < 8, a + 4, a - 4))

    def order(a):
        return jnp.where(a < 4, a + 8, jnp.where(a < 8, a - 1, jnp.where(a == 8, 7, a - 9)))

    def first_hop(a):
        return remote(R.weights.at[place(a), :, at((1 - d) * cols, cols)], R.got_a.at[a], R.asem.at[0, a], R.asem.at[1, a], xdev)

    def second_hop(a):
        return remote(R.send_b.at[a], R.got_b.at[a], R.bsem.at[0, a], R.bsem.at[1, a], across)

    def state_load(a, run):
        slot = lax.rem(a, 3)
        for low, high, refs, base in (
            (0, 4, (R.wb, R.mb, R.vb), 1), (4, 8, (R.wi, R.mi, R.vi), 3), (8, 9, (R.wb, R.mb, R.vb), 0), (9, 12, (R.wi, R.mi, R.vi), 0)):
            @pl.when(jnp.logical_and(a >= low, a < high))
            def _():
                for k in range(3):
                    run(pltpu.make_async_copy(refs[k].at[a - low + base], R.state.at[slot, k], R.state_sem.at[slot, k]))

    def pair_send(a):
        return remote(R.diff.at[a], R.got_p.at[a], R.psem.at[0, a], R.psem.at[1, a], pdev)

    def h_at(k):
        return at(k * hrows, hrows, 16)

    def half_send(a):
        return remote(R.got_p.at[a, h_at(1 - mine)], R.got_h.at[a], R.hsem.at[0, a], R.hsem.at[1, a], mdev)

    def final(a, kind, dev):
        ref = R.total.at[order(a), h_at(1 - mine if kind == 2 else mine)]
        return remote(ref, ref, R.fsem.at[0, a, kind], R.fsem.at[1, a, kind], dev)

    def sum_copy(a):
        return pltpu.make_async_copy(R.sum_ring.at[lax.rem(a, 3)], R.gsum.at[order(a)], R.sum_sem.at[lax.rem(a, 3)])

    def stage_b(a):
        first_hop(a).wait_recv()

        @pl.when(a + window < n_slots)
        def _():
            first_hop(a + window).start()

        there = at((1 - s) * rows, rows, 16)
        R.send_b[a] = (R.weights[place(a), there, at(d * cols, cols)].astype(f32) + R.got_a[a, there].astype(f32)).astype(bf16)
        second_hop(a).start()
        state_load(a, lambda cp: cp.start())

    def stage_c(a):
        second_hop(a).wait_recv()
        here = at(s * rows, rows, 16)
        gradient = R.weights[place(a), here, at(d * cols, cols)].astype(f32) + R.got_a[a, here].astype(f32) + R.got_b[a].astype(f32)
        ring = lax.rem(a, 3)

        @pl.when(a >= 3)
        def _():
            sum_copy(a - 3).wait()

        R.sum_ring[ring] = gradient
        sum_copy(a).start()
        state_load(a, lambda cp: cp.wait())
        slot = lax.rem(a, 3)
        first_new, second_new = adam_parts(gradient, R.state[slot, 1], R.state[slot, 2])
        R.diff[a] = adam_diff(R.state[slot, 0], first_new, second_new, rate_matrix, decay_rate).astype(bf16)

        @pl.when(outer)
        def _():
            pair_send(a).start()

    def stage_d(a):
        pair_send(a).wait_recv()
        R.got_p[a] = (R.diff[a].astype(f32) + R.got_p[a].astype(f32)).astype(bf16)
        half_send(a).start()

    def stage_e(a):
        half_send(a).wait_recv()
        R.total[order(a), h_at(mine)] = (R.got_p[a, h_at(mine)].astype(f32) + R.got_h[a].astype(f32)).astype(bf16)
        final(a, 0, mdev).start()
        final(a, 1, pdev).start()

    def stage_f(a):
        remote(R.got_h.at[a], R.got_h.at[a], R.fsem.at[0, a, 0], R.fsem.at[1, a, 0], mdev).wait_recv()
        final(a, 2, pdev).start()

    def advance(j):
        for stage, lag, only in (
            (stage_b, 0, None), (stage_c, 2, None), (stage_d, 4, inner), (stage_e, 5, inner), (stage_f, 6, inner)):
            a = j - lag
            ok = jnp.logical_and(a >= 0, a < n_slots)

            @pl.when(ok if only is None else jnp.logical_and(ok, only))
            def _():
                stage(a)

    if direct:
        gd_load.wait()
        for a in range(window):
            first_hop(a).start()

    chunks = 2
    step = 256
    R.bias_sum[...] = jnp.zeros_like(R.bias_sum)
    for i in range(7):
        loads[i].wait()

    def down(r, target, where):
        gm = spare[4, r, 0:width]
        forward = jnp.zeros((step, width), f32)
        backward = jnp.zeros((step, width), f32)
        for j in range(chunks):
            lower = R.weights[8 + 2 * j : 10 + 2 * j].reshape(2 * slot_rows, width)
            upper = R.weights[4 + 2 * j : 6 + 2 * j].reshape(2 * slot_rows, width)
            du = (nt(gm, lower) * spare[2 + j, r, 0:width].astype(f32)).astype(bf16)
            spare[2 + j, r, 0:width] = du
            R.bias_sum[:, j * width : (j + 1) * width] += fold(du.astype(f32))
            forward += nn(spare[j, r, 0:width], lower)
            backward += nn(du, upper)
        spare[5, r, 0:width] = forward.astype(bf16)
        target[where] = backward.astype(bf16)

    @pl.loop(0, half // step)
    def _(i):
        down(at((1 - c) * half + i * step, step), R.tok, at(i * step, step))

    trades = [
        remote(spare.at[5, other, pl.ds(0, width)], R.trade.at[0], R.pair_sem.at[0, 0], R.pair_sem.at[1, 0], sibling),
        remote(R.tok, R.trade.at[1], R.pair_sem.at[0, 1], R.pair_sem.at[1, 1], sibling),
    ]
    for cp in trades:
        cp.start()

    @pl.loop(0, half // step)
    def _(i):
        down(at(c * half + i * step, step), R.half_out, at(i * step, step))

    small = 128
    R.acc[...] = jnp.zeros_like(R.acc)
    for i in range(7, 11):
        loads[i].wait()
    for cp in trades:
        cp.wait()
    loads.append(load(R.tok_all.at[s, own], R.tok, 15))

    @pl.loop(0, half // small)
    def _(i):
        r = at(i * small, small)
        g = at(c * half + i * small, small)
        after = R.x1[r]
        branch = spare[5, g, 0:width].astype(f32) + R.trade[0, r].astype(f32) + R.vecs[2:3]
        grad = R.gy[r].astype(f32)
        dh = R.half_out[r].astype(f32) + R.trade[1, r].astype(f32)
        R.half_out[r] = (after + R.vecs[8:9] * branch).astype(bf16)
        hat, inverse = normalize(after)
        total = grad + norm_pull(dh * (R.vecs[1:2] * (1.0 + R.vecs[7:8])), hat, inverse)
        R.x1[r] = total
        R.ga[g] = (R.vecs[5:6] * total).astype(bf16)
        R.acc[0] += fold(dh)
        R.acc[1] += fold(dh * hat)
        R.acc[2] += fold(total * R.attn[r])
        R.acc[3] += fold(grad * branch)
        R.acc[4] += fold(spare[4, g, 0:width].astype(f32))

    give = remote(R.ga.at[own], R.ga.at[own], R.pair_sem.at[0, 2], R.pair_sem.at[1, 2], sibling)
    give.start()
    block_copies = spread(0, R.block_out)
    cross(0, R.block_out, 0).start()
    for i in range(5):
        R.stats[i : i + 1] = jnp.sum(R.acc[i], axis=0, keepdims=True)

    for k in range(4):
        where = pl.ds((k % 2) * slot_rows, slot_rows)
        R.weights[8 + k] = tn(spare[2 + k // 2, :, where], R.hid[...]).astype(bf16)
    for h in range(4):
        load_probs(h, h).start()
    h1_load = pltpu.make_async_copy(R.h1_in, R.hid, R.load_sem.at[16])
    h1_load.start()
    if direct:
        advance(0)
        advance(1)

    for i in range(11, 16):
        loads[i].wait()
    give.wait()
    R.weights[4] = nn(R.o_t[...], R.ga[...]).astype(bf16)
    do_t = nt(R.weights[3], R.ga[...])
    for h in range(heads):
        one = pl.ds(h * HEAD_DIM, HEAD_DIM)
        R.do_t[one] = (do_t[h * HEAD_DIM : (h + 1) * HEAD_DIM] * R.inv[h]).astype(bf16)
    wide = 256

    @pl.loop(0, heads)
    def _(h):
        two = at(h // 2 * 2 * HEAD_DIM, 2 * HEAD_DIM)
        one = at(h * HEAD_DIM, HEAD_DIM, HEAD_DIM)
        slot = lax.rem(h, 4)
        load_probs(h, slot).wait()
        delta = jnp.sum(R.do_t[one].astype(f32) * R.o_t[one].astype(f32), axis=0, keepdims=True)
        for i in range(length // wide):
            q = slice(i * wide, (i + 1) * wide)
            dp = nn(R.v_r[:, two], only_head(R.do_t[two, q], lax.rem(h, 2)))
            spare[4, :, q] = (spare[slot, :, q].astype(f32) * (dp - delta[:, q])).astype(bf16)
        cos, sin = R.cosine[...], R.sine[...]
        dq = nn(R.k_t[one], spare[4]) * 0.125
        dk = nt(R.q_t[one], spare[4])
        spare[5, one] = turn(dq, cos, -sin).astype(bf16)
        spare[5, at(slot_rows + h * HEAD_DIM, HEAD_DIM, HEAD_DIM)] = turn(dk, cos, -sin).astype(bf16)
        R.dv_t[one] = nt(R.do_t[one], spare[slot]).astype(bf16)

        @pl.when(h + 4 < heads)
        def _():
            load_probs(h + 4, slot).start()

        @pl.when(h < pieces - 1)
        def _():
            cross(0, R.block_out, h + 1).start()

        if direct:
            @pl.when(jnp.logical_or(h == 2, h == 3))
            def _():
                advance(h)

    h1_load.wait()
    turned = (spare.at[5, pl.ds(0, slot_rows)], spare.at[5, pl.ds(slot_rows, slot_rows)], R.dv_t)
    for k in range(3):
        R.weights[5 + k] = nn(turned[k][...], R.hid[...]).astype(bf16)
    if direct:
        advance(4)
    for k in range(pieces):
        pass_piece(0, R.block_out, k)

    def dh1_part(r):
        total = tn(turned[0][:, r], R.weights[0])
        for k in range(1, 3):
            total += tn(turned[k][:, r], R.weights[k])
        return total

    R.trade[0] = dh1_part(other).astype(bf16)
    trade = remote(R.trade.at[0], R.trade.at[1], R.pair_sem.at[0, 3], R.pair_sem.at[1, 3], sibling)
    trade.start()
    R.attn[...] = dh1_part(own)

    R.acc[...] = jnp.zeros_like(R.acc)
    trade.wait()
    block_copies[0].wait_send()
    block_copies[1].wait()
    for k in range(pieces):
        cross(0, R.block_out, k).wait_send()

    @pl.loop(0, half // small)
    def _(i):
        r = at(i * small, small)
        dh = R.attn[r] + R.trade[1, r].astype(f32)
        hat, inverse = normalize(R.tok[r].astype(f32))
        R.acc[0] += fold(dh)
        R.acc[1] += fold(dh * hat)
        total = R.x1[r] + norm_pull(dh * (R.vecs[0:1] * (1.0 + R.vecs[4:5])), hat, inverse)
        R.half_out[r] = total.astype(bf16)

    grad_copies = spread(1, R.grad_out)
    cross(1, R.grad_out, 0).start()
    if direct:
        advance(5)
    shift1 = jnp.sum(R.acc[0], axis=0, keepdims=True)
    turn1 = jnp.sum(R.acc[1], axis=0, keepdims=True)
    R.sums[...] = jnp.zeros_like(R.sums)
    R.sums[0:1] = shift1
    R.sums[1:2] = turn1 * R.vecs[0:1]
    R.sums[2:3] = R.stats[2:3]
    R.sums[3:4] = R.stats[0:1]
    R.sums[4:5] = R.stats[1:2] * R.vecs[1:2]
    R.sums[5:6] = R.stats[3:4]
    R.sums[6:7] = turn1 * (1.0 + R.vecs[4:5])
    R.sums[7:8] = R.stats[1:2] * (1.0 + R.vecs[7:8])
    R.sums[8:9] = R.stats[4:5]
    bias_total = jnp.sum(R.bias_sum[...], axis=0, keepdims=True)
    R.sums[9:10] = bias_total[:, 0:width]
    R.sums[10:11] = bias_total[:, width : 2 * width]
    R.shared[t, d] = R.sums[...]
    casts = [
        remote(R.sums, R.shared.at[t, d], R.cast_sem.at[0, i], R.cast_sem.at[1, i], dev) for i, dev in enumerate(others)
    ]
    for cp in casts:
        cp.start()
    if direct:
        advance(6)
        advance(7)
    for cp in casts:
        cp.wait()
    if direct:
        step_small(R, t, d, g, s, c, n_tp, width)
        a_rows = R.ada_low.shape[0] // 2

        def ada_at(ref, k):
            return ref.at[pl.ds(k * a_rows, a_rows)]

        tiny = []
        for i in range(3):
            dev = {"grp": lax.rem(g + 1 + i, 4)}
            tiny.append(remote(R.small_low, R.small_all.at[g], R.tiny_sem.at[0, 0, i], R.tiny_sem.at[1, 0, i], dev))
            tiny.append(remote(R.bias_low, R.bias_all.at[g], R.tiny_sem.at[0, 1, i], R.tiny_sem.at[1, 1, i], dev))
        for cp in tiny:
            cp.start()
        R.small_all[g] = R.small_low[...]
        R.bias_all[g] = R.bias_low[...]
        ada_sem = R.ada_sem
        a_pair = remote(R.ada_low, R.ada_p, ada_sem.at[0, 0], ada_sem.at[1, 0], pdev)
        a_half = remote(ada_at(R.ada_p, 1 - mine), R.ada_h, ada_sem.at[0, 1], ada_sem.at[1, 1], mdev)
        a_mid = remote(ada_at(R.ada_total, mine), ada_at(R.ada_total, mine), ada_sem.at[0, 2], ada_sem.at[1, 2], mdev)
        a_out = remote(ada_at(R.ada_total, mine), ada_at(R.ada_total, mine), ada_sem.at[0, 3], ada_sem.at[1, 3], pdev)
        a_pass = remote(ada_at(R.ada_total, 1 - mine), ada_at(R.ada_total, 1 - mine), ada_sem.at[0, 4], ada_sem.at[1, 4], pdev)

        @pl.when(outer)
        def _():
            a_pair.start()

        @pl.loop(8, n_slots + 6)
        def _(j):
            advance(j)

            @pl.when(j < 7 + pieces)
            def _():
                cross(1, R.grad_out, j - 7).start()

            @pl.when(jnp.logical_and(j >= 10, j < 10 + pieces))
            def _():
                pass_piece(1, R.grad_out, j - 10)

            @pl.when(jnp.logical_and(inner, j == 8))
            def _():
                a_pair.wait_recv()
                R.ada_p[...] = (R.ada_p[...].astype(f32) + R.ada_low[...].astype(f32)).astype(bf16)
                a_half.start()

            @pl.when(jnp.logical_and(inner, j == 9))
            def _():
                a_half.wait()
                mine_rows = pl.ds(mine * a_rows, a_rows)
                R.ada_total[mine_rows] = (R.ada_p[mine_rows].astype(f32) + R.ada_h[...].astype(f32)).astype(bf16)
                a_mid.start()
                a_out.start()

            @pl.when(jnp.logical_and(inner, j == 10))
            def _():
                a_mid.wait()
                a_pass.start()

    else:
        for k in range(1, pieces):
            cross(1, R.grad_out, k).start()
        for k in range(pieces):
            pass_piece(1, R.grad_out, k)
    if direct:
        @pl.when(outer)
        def _():
            a_pair.wait_send()
            remote(R.ada_h, R.ada_h, ada_sem.at[0, 3], ada_sem.at[1, 3], pdev).wait_recv()
            remote(R.ada_h, R.ada_h, ada_sem.at[0, 4], ada_sem.at[1, 4], pdev).wait_recv()

            @pl.loop(0, n_slots)
            def _(a):
                pair_send(a).wait_send()
                remote(R.got_h.at[a], R.got_h.at[a], R.fsem.at[0, a, 1], R.fsem.at[1, a, 1], pdev).wait_recv()
                remote(R.got_h.at[a], R.got_h.at[a], R.fsem.at[0, a, 2], R.fsem.at[1, a, 2], pdev).wait_recv()

        @pl.when(inner)
        def _():
            a_out.wait_send()
            a_pass.wait_send()

            @pl.loop(0, n_slots)
            def _(a):
                half_send(a).wait_send()
                final(a, 0, mdev).wait_send()
                final(a, 1, pdev).wait_send()
                final(a, 2, pdev).wait_send()

        for a in range(n_slots):
            first_hop(a).wait_send()
            second_hop(a).wait_send()
        for cp in tiny:
            cp.wait()
        R.small_total[...] = (R.small_all[0] + R.small_all[1]) + (R.small_all[2] + R.small_all[3])
        R.bias_total[...] = (R.bias_all[0] + R.bias_all[1]) + (R.bias_all[2] + R.bias_all[3])
        for a in range(n_slots - 3, n_slots):
            sum_copy(a).wait()
    else:
        R.grads[...] = R.weights[4:8]
        R.grads_up[...] = R.weights[8:12]
    block_copies[0].wait_recv()
    for cp in grad_copies:
        cp.wait()
    for k in range(pieces):
        cross(1, R.grad_out, k).wait_send()
        relay(0, R.block_out, k).wait()
        relay(1, R.grad_out, k).wait()


def step_small(R, t, d, g, s, c, n_tp, width):
    part = R.wa.shape[2]
    everything = R.shared[0, 0]
    for tt in range(n_tp):
        for dd in range(2):
            if tt or dd:
                everything = everything + R.shared[tt, dd]
    R.summed[...] = everything
    near = at(d * (width // 2), width // 2)
    R.small_grad[0:3] = R.summed[6:9, near]
    R.small_grad[3:9] = R.summed[0:6, near]
    first_new, second_new = adam_parts(R.small_grad[...], R.ms[...], R.vs[...])
    R.small_low[...] = adam_diff(R.ps[...], first_new, second_new, rate_small, 0.0).astype(bf16).astype(f32)

    mine = R.shared[c, 0, 8:16]
    for ss in range(2):
        for dd in range(2):
            if ss or dd:
                mine = mine + R.shared[ss * (n_tp // 2) + c, dd, 8:16]
    size = R.bu.shape[1]
    turned = pltpu.roll(mine, lax.rem(width - (s * 2 + d) * size, width), 1)
    R.bias_grad[0:1] = turned[1:2, 0:size]
    R.bias_grad[1:2] = turned[1:2, width // 2 : width // 2 + size]
    R.bias_grad[2:3] = turned[2:3, 0:size]
    R.bias_grad[3:4] = turned[2:3, width // 2 : width // 2 + size]
    first_new, second_new = adam_parts(R.bias_grad[...], R.mu[...], R.vu[...])
    R.bias_low[...] = adam_diff(R.bu[...], first_new, second_new, rate_small, 0.0).astype(bf16).astype(f32)

    R.ada_rows[...] = jnp.zeros_like(R.ada_rows)
    R.cond_rows[...] = jnp.zeros_like(R.cond_rows)
    for ss in range(2):
        for dd in range(2):
            total = R.shared[2 * ss, dd, 0:8] + R.shared[2 * ss + 1, dd, 0:8]
            turned = pltpu.roll(total, lax.rem(width - t * part, width), 1)
            k = ss * 2 + dd
            R.cond_rows[k : k + 1] = R.cond[dd, ss : ss + 1]
            for a in range(6):
                R.ada_rows[a, k : k + 1] = turned[a : a + 1, 0:part]
    lhs = R.cond_rows[...][:, : R.wa.shape[1]]
    for a in range(6):
        gradient = lax.dot_general(
            lhs, R.ada_rows[a], (((0,), (0,)), ((), ())), precision=highest, preferred_element_type=f32)
        R.ada_grad[a] = gradient
        first_new, second_new = adam_parts(gradient, R.ma[a], R.va[a])
        R.ada_low[a] = adam_diff(R.wa[a], first_new, second_new, rate_matrix, decay_rate).astype(bf16)


def backward(direct, cores, seqs, fw, tokens, cosine, sine, states, smalls):
    n_tp = lax.axis_size("tp")
    length, width = fw.h1_out.shape
    heads = fw.inv_out.shape[0]
    slot_rows = fw.weights_out.shape[1]
    half = length // cores
    dma = pltpu.SemaphoreType.DMA
    arr = jax.ShapeDtypeStruct
    vm = pltpu.VMEM
    spans = 2 if direct else 1
    ins = dict(
        weights_in=(fw.weights_out, ANY), o_in=(fw.o_out, ANY), v_in=(fw.v_out, ANY),
        k_in=(fw.k_out, ANY), q_in=(fw.q_out, ANY), probs_in=(fw.probs_out, ANY), h1_in=(fw.h1_out, ANY),
        x1_in=(fw.x1_out, ANY), attn_in=(fw.attn_out, ANY), h2_in=(fw.h2_out, ANY), hidden_in=(fw.hidden_out, ANY),
        gm_in=(fw.gm_out, ANY), gy_in=(fw.gy_out, ANY), tok_all=(tokens, ANY),
        inv=(fw.inv_out, VMEM), vecs=(fw.vecs_out, VMEM), cosine=(cosine, VMEM), sine=(sine, VMEM),
    )
    outs = dict(
        block_out=(arr((seqs, length, width), bf16), ANY),
        grad_out=(arr((seqs, length, width), bf16), ANY),
    )
    scratch = dict(
        weights=vm((16 if direct else 12, slot_rows, width), bf16),
        spare=vm((heads, length, length), bf16),
        ga=vm((length, width), bf16),
        hid=vm((length, width), bf16),
        trade=vm((2, half, width), bf16),
        x1=vm((half, width), f32),
        attn=vm((half, width), f32),
        gy=vm((half, width), bf16),
        tok=vm((half, width), bf16),
        half_out=vm((half, width), bf16),
        o_t=vm((slot_rows, length), bf16),
        v_r=vm((length, slot_rows), bf16),
        k_t=vm((slot_rows, length), bf16),
        q_t=vm((slot_rows, length), bf16),
        do_t=vm((slot_rows, length), bf16),
        dv_t=vm((slot_rows, length), bf16),
        bias_sum=vm((8, 4 * slot_rows), f32),
        acc=vm((5, 8, width), f32),
        stats=vm((8, width), f32),
        sums=vm((16, width), f32),
        load_sem=dma((17,)),
        probs_sem=dma((4,)),
        spread_sem=dma((2, 2, 2)),
        cross_sem=dma((2, 2, 4)),
        relay_sem=dma((2, 2, 4)),
        pair_sem=dma((2, 4)),
        cast_sem=dma((2, spans * n_tp - 1)),
    )
    if direct:
        wa, ma, va, ps, ms, vs, bu, mu, vu = smalls
        rows, cols = slot_rows // 2, width // 2
        slot = (12, rows, cols)
        wi, wb, mi, mb, vi, vb = states
        ins |= dict(
            gd_in=(fw.gd_out, ANY), cond=(fw.cond_out, VMEM), wi=(wi, ANY), wb=(wb, ANY),
            mi=(mi, ANY), mb=(mb, ANY), vi=(vi, ANY), vb=(vb, ANY), wa=(wa, VMEM), ma=(ma, VMEM), va=(va, VMEM),
            ps=(ps, VMEM), ms=(ms, VMEM), vs=(vs, VMEM), bu=(bu, VMEM), mu=(mu, VMEM), vu=(vu, VMEM),
        )
        outs |= dict(
            gsum=(arr(slot, f32), ANY),
            total=(arr(slot, bf16), VMEM),
            ada_grad=(arr(wa.shape, f32), VMEM),
            small_grad=(arr(ps.shape, f32), VMEM),
            bias_grad=(arr(bu.shape, f32), VMEM),
            ada_total=(arr(wa.shape, bf16), VMEM),
            small_total=(arr(ps.shape, f32), VMEM),
            bias_total=(arr(bu.shape, f32), VMEM),
        )
        scratch |= dict(
            shared=vm((n_tp, spans, 16, width), f32),
            sum_ring=vm((3, rows, cols), f32),
            got_a=vm((12, slot_rows, cols), bf16),
            send_b=vm(slot, bf16),
            got_b=vm(slot, bf16),
            state=vm((3, 3, rows, cols), f32),
            diff=vm(slot, bf16),
            got_p=vm(slot, bf16),
            got_h=vm((12, rows // 2, cols), bf16),
            summed=vm((16, width), f32),
            ada_rows=vm((6, 8, wa.shape[2]), f32),
            cond_rows=vm((8, 128), f32),
            ada_low=vm(wa.shape, bf16),
            ada_p=vm(wa.shape, bf16),
            ada_h=vm((wa.shape[0] // 2,) + wa.shape[1:], bf16),
            small_low=vm(ps.shape, f32),
            bias_low=vm(bu.shape, f32),
            small_all=vm((4,) + ps.shape, f32),
            bias_all=vm((4,) + bu.shape, f32),
            gd_sem=dma,
            sum_sem=dma((3,)),
            state_sem=dma((3, 3)),
            asem=dma((2, 12)),
            bsem=dma((2, 12)),
            psem=dma((2, 12)),
            hsem=dma((2, 12)),
            fsem=dma((2, 12, 3)),
            tiny_sem=dma((2, 2, 3)),
            ada_sem=dma((2, 5)),
        )
    else:
        outs |= dict(
            grads=(arr((4, slot_rows, width), bf16), VMEM),
            grads_up=(arr((4, slot_rows, width), bf16), VMEM),
            shared=(arr((n_tp, spans, 16, width), f32), VMEM),
        )
    names = list(ins) + list(outs) + list(scratch)
    results = pl.pallas_call(
        functools.partial(backward_kernel, direct, cores, n_tp, names),
        out_shape=tuple(o[0] for o in outs.values()),
        in_specs=[i[1] for i in ins.values()],
        out_specs=tuple(o[1] for o in outs.values()),
        scratch_shapes=list(scratch.values()),
        compiler_params=pltpu.CompilerParams(collective_id=1, has_side_effects=True, vmem_limit_bytes=60 * MIB),
        name="backward",
    )(*[i[0] for i in ins.values()])
    return SimpleNamespace(**dict(zip(outs, results)))


def angle_tables(length):
    half = HEAD_DIM // 2
    frequency = np.float32(10000.0) ** (np.float32(-2.0) * np.arange(half, dtype=np.float32) / np.float32(HEAD_DIM))
    angles = frequency[:, None] * np.arange(length, dtype=np.float32)[None, :]
    return jnp.asarray(np.cos(angles)), jnp.asarray(np.sin(angles))


def on_device(
    tokens, sigma_index, absorbed, cotangent, time_table,
    in_weight, back_weight, ada_weight, small_params, up_bias,
    in_first, back_first, ada_first, small_first, bias_first,
    in_second, back_second, ada_second, small_second, bias_second,
    in_moment, back_moment, ada_moment, small_moment, bias_moment,
):
    n_tp, n_dp, n_grp = lax.axis_size("tp"), lax.axis_size("dp"), lax.axis_size("grp")
    seqs, length, width = tokens.shape
    cores = n_tp // seqs
    part = in_weight.shape[2]
    heads_width = seqs * part
    direct = n_dp == 2 and n_grp == 4 and seqs == 2 and cores == 2
    t, d = lax.axis_index("tp"), lax.axis_index("dp")
    s = t // cores
    c = lax.rem(t, cores)
    groups = [[a * cores + b for a in range(seqs)] for b in range(cores)]

    wi_t = jnp.transpose(in_weight, (1, 2, 0))
    wa_t = jnp.transpose(ada_weight, (1, 0, 2))
    cosine, sine = angle_tables(length)
    if direct:
        first = (sigma_index, time_table, wa_t, small_params, up_bias, wi_t, back_weight)
    else:
        def over_tp(x, axis):
            return lax.all_gather(x, "tp", axis=axis, tiled=True, axis_index_groups=groups)

        table_ids = jnp.arange(time_table.shape[0], dtype=jnp.int32)
        onehot = (sigma_index[:, None] == table_ids[None, :]).astype(f32)
        condition = jax.nn.silu(jnp.dot(onehot, time_table, precision=highest))
        cond_low = condition.astype(bf16).astype(f32)
        wi_all = over_tp(lax.all_gather(wi_t.astype(bf16), "dp", axis=2, tiled=True), 1)
        wb_all = over_tp(lax.all_gather(back_weight.astype(bf16), "dp", axis=2, tiled=True), 1)
        weights = jnp.concatenate([wi_all[:3], wb_all[:1], wi_all[3:], wb_all[1:]], axis=0)
        bu_all = over_tp(lax.all_gather(up_bias.astype(bf16), "dp", axis=1, tiled=True)[None], 0)
        bias_row = jnp.transpose(bu_all, (1, 0, 2)).reshape(1, 4 * heads_width).astype(f32)
        small_rows = lax.all_gather(small_params.astype(bf16), "dp", axis=1, tiled=True).astype(f32)
        wa_all = lax.all_gather(ada_weight.astype(bf16), "dp", axis=0, tiled=True)
        mod_part = jnp.einsum("sc,cad->sad", cond_low.astype(bf16), wa_all, preferred_element_type=f32)
        mod_all = lax.all_gather(mod_part, "tp", axis=2, tiled=True)
        mod_rows = lax.dynamic_index_in_dim(mod_all, s, 0, keepdims=False) + small_rows[3:9]
        vecs = jnp.concatenate([small_rows[0:3], mod_rows, jnp.zeros((7, width), f32)], axis=0)
        first = (weights, vecs, bias_row)

    fw = forward(direct, cores, length, width, heads_width, first, tokens, absorbed, cotangent, cosine, sine)
    mi, vi = jnp.transpose(in_first[0], (1, 2, 0)), jnp.transpose(in_second[0], (1, 2, 0))
    mb, vb = back_first[0], back_second[0]
    am, av = jnp.transpose(ada_first[0], (1, 0, 2)), jnp.transpose(ada_second[0], (1, 0, 2))
    states = (wi_t, back_weight, mi, mb, vi, vb)
    smalls = (
        wa_t, am, av, small_params, small_first[0], small_second[0], up_bias, bias_first[0], bias_second[0])
    bw = backward(direct, cores, seqs, fw, tokens, cosine, sine, states, smalls)
    block_out = bw.block_out
    input_grad = bw.grad_out.astype(f32)
    if direct:
        gi, gbk = bw.gsum[:7], bw.gsum[7:]
        di, db = bw.total[:7].astype(f32), bw.total[7:].astype(f32)
        ada_grad, small_shard, bias_grad = bw.ada_grad, bw.small_grad, bw.bias_grad
        ada_t, small_t, bias_t = bw.ada_total.astype(f32), bw.small_total, bw.bias_total
    else:
        shared = lax.all_gather(bw.shared[:, 0], "dp", axis=1).reshape(seqs, cores, n_dp, 16, width)
        by_seq = shared.sum(axis=1)
        dmod = by_seq[:, :, 0:6]
        small_grad = jnp.concatenate([by_seq[:, :, 6:9].sum(axis=(0, 1)), dmod.sum(axis=(0, 1))], axis=0)
        bias_sum = shared[:, :, :, 9:11].sum(axis=(0, 2)).reshape(cores, 4, seqs, part)
        mine = lax.dynamic_index_in_dim(lax.dynamic_index_in_dim(bias_sum, c, 0, keepdims=False), s, 1, keepdims=False)
        bias_grad = lax.dynamic_slice_in_dim(mine, d * (part // n_dp), part // n_dp, 1)
        small_shard = lax.dynamic_slice_in_dim(small_grad, d * (width // n_dp), width // n_dp, 1)
        dmod_cols = lax.dynamic_slice_in_dim(dmod, t * part, part, 3)
        conds = jnp.transpose(lax.all_gather(cond_low, "dp", axis=0), (1, 0, 2))
        conds = lax.dynamic_slice_in_dim(conds, d * wa_t.shape[1], wa_t.shape[1], 2)
        ada_grad = jnp.sum(conds[:, :, None, :, None] * dmod_cols[:, :, :, None, :], axis=(0, 1))

        def scatter(x):
            x = lax.psum_scatter(x, "tp", scatter_dimension=1, tiled=True, axis_index_groups=groups)
            return lax.psum_scatter(x, "dp", scatter_dimension=2, tiled=True).astype(f32)

        gi = scatter(jnp.concatenate([bw.grads[1:4], bw.grads_up], axis=0))
        gbk = scatter(jnp.concatenate([bw.grads[0:1], fw.gd_out], axis=0))
    ada_m, ada_v = adam_parts(ada_grad, am, av)
    small_m, small_v = adam_parts(small_shard, small_first[0], small_second[0])
    bias_m, bias_v = adam_parts(bias_grad, bias_first[0], bias_second[0])
    in_m, in_v = adam_parts(gi, mi, vi)
    back_m, back_v = adam_parts(gbk, mb, vb)
    if not direct:
        def over_groups(weight, first_new, second_new, rate, decay):
            return lax.psum(adam_diff(weight, first_new, second_new, rate, decay).astype(bf16), "grp").astype(f32)

        di = over_groups(wi_t, in_m, in_v, rate_matrix, decay_rate)
        db = over_groups(back_weight, back_m, back_v, rate_matrix, decay_rate)
        ada_t = over_groups(wa_t, ada_m, ada_v, rate_matrix, decay_rate)
        small_t = over_groups(small_params, small_m, small_v, rate_small, 0.0)
        bias_t = over_groups(up_bias, bias_m, bias_v, rate_small, 0.0)

    def outer(weight, moment, summed):
        diff = summed / n_grp
        moment_new = outer_mu * moment + diff
        return weight - outer_rate * (diff + outer_mu * moment_new), diff, moment_new

    def back_in(x):
        return jnp.transpose(x, (2, 0, 1))

    def back_ada(x):
        return jnp.transpose(x, (1, 0, 2))

    in_w, in_diff, in_mom = (back_in(x) for x in outer(wi_t, jnp.transpose(in_moment, (1, 2, 0)), di))
    back_w, back_diff, back_mom = outer(back_weight, back_moment, db)
    ada_w, ada_diff, ada_mom = (back_ada(x) for x in outer(wa_t, jnp.transpose(ada_moment, (1, 0, 2)), ada_t))
    small_w, small_diff, small_mom = outer(small_params, small_moment, small_t)
    bias_w, bias_diff, bias_mom = outer(up_bias, bias_moment, bias_t)
    return (
        block_out, input_grad,
        back_in(in_m)[None], back_m[None], back_ada(ada_m)[None], small_m[None], bias_m[None],
        back_in(in_v)[None], back_v[None], back_ada(ada_v)[None], small_v[None], bias_v[None],
        in_w, back_w, ada_w, small_w, bias_w,
        in_diff, back_diff, ada_diff, small_diff, bias_diff,
        in_mom, back_mom, ada_mom, small_mom, bias_mom,
    )


def solution(mesh):
    rows = P(("dp", "grp"), None, None)
    shared = (
        P("dp", None, "tp"), P(None, "tp", "dp"), P("dp", None, "tp"), P(None, "dp"), P(None, ("tp", "dp")),
    )
    grouped = (
        P("grp", "dp", None, "tp"), P("grp", None, "tp", "dp"), P("grp", "dp", None, "tp"),
        P("grp", None, "dp"), P("grp", None, ("tp", "dp")),
    )
    in_specs = (rows, P(("dp", "grp")), P(("dp", "grp"), None), rows, P()) + shared + grouped + grouped + shared
    out_specs = (rows, rows) + grouped + grouped + shared + shared + shared
    return jax.shard_map(on_device, mesh=mesh, in_specs=in_specs, out_specs=out_specs, check_vma=False)
```

time: 328 us -> 230 us (0.70)
  Pallas kernels: 285 us -> 199 us
  local copies, waits for them, and re-layouts: 15.2 us -> 6.63 us
    pallas_call x3 -> x1, Pallas kernels: 188 us -> 122 us  [backward(): pl.pallas_call(functools.partial(backward_kernel, direct, cores, n_tp, na...]
    pallas_call x1, Pallas kernels: 96.6 us -> 76.7 us  [forward(): pl.pallas_call(functools.partial(forward_kernel, direct, cores, n_tp, nam...]
    squeeze x2 -> x0, local copies, waits for them, and re-layouts: 3.55 us -> none  [the longest x1 1.92 us: on_device(): wq, wo = (fw.wq_out[:3], fw.wq_out[3])]
    unnamed x65 -> x54, local copies, waits for them, and re-layouts: 7.26 us -> 6.63 us
where the time goes in v3:
time: 230 us
  Pallas kernels  199 us (87%)
  other arithmetic  23.6 us (10%)
  local copies, waits for them, and re-layouts  6.63 us (3%)
    pallas_call x1, Pallas kernels, backward(): pl.pallas_call(functools.partial(backward_kernel, direct, cores, n_tp, na...  122 us
    pallas_call x1, Pallas kernels, forward(): pl.pallas_call(functools.partial(forward_kernel, direct, cores, n_tp, nam...  76.7 us
    unnamed x54, local copies, waits for them, and re-layouts  6.63 us
    sub x3, other arithmetic, outer(): weight - outer_rate * (diff + outer_mu * moment_new)  5.26 us

profile of v3, /device:TPU:0, one launch (start us, length us, event | category | flops | bytes accessed | tf_op | source)
XLA Modules:
  0.0 229.8 jit_solution(9181633677980925462)
XLA Ops:
  0.7 1.3 copy_bitcast_fusion
  2.0 76.7 %forward.1 = (bf16[1024,768]{1,0:T(8,128)(2,1)}, bf16[12,384,768]{2,1,0:T(8,128)(2,1)}, bf16[384,1024]{1,0:T(8,128)(2,1)}, bf16[384,1024]{1,0:T(8,128)(2,1)}, bf...) custom-call(s32[2]{0:T(128)} %args_0_.4, ...), custom_call_target="tpu_custom_call" | custom-call | tf_op jit(solution)/shard_map/forward/pallas_call | solution.py:509
  78.7 0.0 copy-start.22
  78.7 0.0 copy-start.23
  78.8 0.0 copy-start.21
  78.8 0.0 copy-start.24
  78.8 0.0 copy-start.18
  78.8 0.0 copy-start.19
  78.8 0.0 copy-start.16
  78.8 0.0 copy-start.20
  78.8 0.0 copy-start.12
  78.8 0.0 copy-start.13
  78.9 122.0 %backward.1 = (bf16[2,1024,768]{2,1,0:T(8,128)(2,1)}, bf16[2,1024,768]{2,1,0:T(8,128)(2,1)}, f32[12,192,384]{2,1,0:T(8,128)}, bf16[12,192,384]{2,1,0:T(8,128)(2,...) custom-call(bf16[12,384,768]{2,1,0:T(8,128)(2,1)} %get-tuple-element, ...), custom_call_target="tpu_custom_call" | custom-call | tf_op jit(solution)/shard_map/backward/pallas_call | solution.py:1153
  200.8 0.0 copy-start.6
  200.9 0.0 copy-start.15
  200.9 0.0 copy-start.17
  200.9 0.0 copy-done.22
  200.9 0.0 copy-done.23
  200.9 1.3 fusion.13
  202.2 0.0 copy-done.21
  202.2 0.0 copy-done.24
  202.2 1.3 multiply_subtract_fusion.2
  203.5 0.0 copy-done.18
  203.5 0.0 copy-done.19
  203.5 0.7 fusion.11
  204.2 0.6 copy.55
  204.8 0.6 copy.54
  205.4 0.0 copy-done.16
  205.4 0.0 copy-done.20
  205.4 1.4 multiply_subtract_fusion.1
  206.8 0.0 copy-done.12
  206.8 0.0 copy-done.13
  206.8 0.0 copy-start.4
  206.8 0.0 copy-start.5
  206.8 2.1 fusion.7
  209.0 0.0 copy-done.6
  209.0 0.0 copy-done.15
  209.0 0.0 copy-done.17
  209.0 0.0 copy-start.7
  209.0 1.1 fusion.9
  210.1 0.0 copy-done.4
  210.1 0.0 copy-done.5
  210.1 0.0 copy-start.2
  210.1 0.0 copy-start.3
  210.2 3.8 %fusion.5 = (f32[1,5,192,384]{3,2,1,0:T(8,128)}, f32[1,5,192,384]{3,2,1,0:T(8,128)}) fusion(f32[12,192,384]{2,1,0:T(8,128)} %get-tuple-element.73, f32[1,5,192,384]{3,2,1,0:T(8,128)S(1)} %copy-done.5, f32[1,5,192,384]{3,2,1,0:T(8,128)S(1)} %copy-done.4), kind=kLoop, calls=%fused_computation.11 | loop fusion | flops 2580480 | bytes 7372800 | tf_op jit(solution)/shard_map/broadcast_in_dim | solution.py:1285
  213.9 0.0 copy-done.7
  213.9 0.0 copy-done.2
  213.9 0.0 copy-done.3
  213.9 0.0 copy-start.1
  213.9 0.0 copy-start.11
  214.0 0.0 copy-start.14
  214.0 2.7 %fusion.1 = (f32[1,384,7,192]{1,3,2,0:T(8,128)}, f32[1,384,7,192]{1,3,2,0:T(8,128)}) fusion(f32[12,192,384]{2,1,0:T(8,128)S(1)} %copy-done.7, f32[1,384,7,192]{1,3,2,0:T(8,128)S(1)} %copy-done.3, f32[1,384,7,192]{1,3,2,0:T(8,128)S(1)} %copy-done.2), kind=kLoop, calls=%fused_computation.3 | loop fusion | flops 3612672 | bytes 10321920 | tf_op jit(solution)/shard_map/broadcast_in_dim | solution.py:1285
  216.7 0.0 copy-done.1
  216.7 0.0 copy-done.11
  216.7 1.1 copy-done.14
  217.8 0.0 copy-start
  217.8 2.6 %multiply_subtract_fusion = (f32[5,192,384]{2,1,0:T(8,128)}, f32[5,192,384]{2,1,0:T(8,128)}, f32[5,192,384]{2,1,0:T(8,128)}) fusion(f32[5,192,384]{2,1,0:T(8,128)S(1)} %copy-done.1, f32[5,192,384]{2,1,0:T(8,128)S(1)} %copy-done.14, bf16[12,192,384]{2,1,0:T(8,128)(2,1)S(1)} %copy-done.11), kind=kLoop, calls=%fused_computation.12 | loop fusion | flops 2949120 | bytes 8110080 | tf_op jit(solution)/shard_map/sub | solution.py:1269
  220.4 0.0 copy-done
  220.4 1.2 copy-done.10
  221.6 3.4 %fusion.3 = (f32[384,7,192]{0,2,1:T(8,128)}, f32[384,7,192]{0,2,1:T(8,128)}, f32[384,7,192]{0,2,1:T(8,128)}) fusion(f32[384,7,192]{0,2,1:T(8,128)S(1)} %copy-done.10, bf16[12,192,384]{2,1,0:T(8,128)(2,1)S(1)} %copy-done.11, f32[384,7,192]{0,2,1:T(8,128)S(1)} %copy-done), kind=kLoop, calls=%fused_computation.9 | loop fusion | flops 4128768 | bytes 11354112 | tf_op jit(solution)/shard_map/transpose | solution.py:1272
  224.9 0.0 copy-done.9
  224.9 3.2 %convert_element_type.12 = f32[2,1024,768]{2,1,0:T(8,128)} convert(bf16[2,1024,768]{2,1,0:T(8,128)(2,1)S(1)} %copy-done.9) | non-fusion elementwise | flops 1572864 | bytes 9437184 | tf_op jit(solution)/shard_map/convert_element_type | solution.py:1225
  228.1 0.0 copy-done.8
  228.1 1.7 copy.65
  (3 shorter events, 0.0 us)
Async XLA Ops:
  78.7 122.2 %copy-start.22 = (f32[1,4,96]{2,1,0:T(4,128)S(1)}, f32[1,4,96]{2,1,0:T(4,128)}, u32[]{:S(2)}) copy-start(f32[1,4,96]{2,1,0:T(4,128)} %param.41) | copy-start | bytes 4612
  78.7 122.1 %copy-start.23 = (f32[1,4,96]{2,1,0:T(4,128)S(1)}, f32[1,4,96]{2,1,0:T(4,128)}, u32[]{:S(2)}) copy-start(f32[1,4,96]{2,1,0:T(4,128)} %param.46) | copy-start | bytes 4612
  78.8 123.4 %copy-start.21 = (f32[4,96]{1,0:T(4,128)S(1)}, f32[4,96]{1,0:T(4,128)}, u32[]{:S(2)}) copy-start(f32[4,96]{1,0:T(4,128)} %args_32_.1) | copy-start | bytes 4612
  78.8 123.4 %copy-start.24 = (f32[4,96]{1,0:T(4,128)S(1)}, f32[4,96]{1,0:T(4,128)}, u32[]{:S(2)}) copy-start(f32[4,96]{1,0:T(4,128)} %param.51) | copy-start | bytes 4612
  78.8 124.7 %copy-start.18 = (f32[1,9,384]{2,0,1:T(1,128)S(1)}, f32[1,9,384]{2,0,1:T(1,128)}, u32[]{:S(2)}) copy-start(f32[1,9,384]{2,0,1:T(1,128)} %param.45) | copy-start | bytes 41476
  78.8 124.7 %copy-start.19 = (f32[1,9,384]{2,0,1:T(1,128)S(1)}, f32[1,9,384]{2,0,1:T(1,128)}, u32[]{:S(2)}) copy-start(f32[1,9,384]{2,0,1:T(1,128)} %param.40) | copy-start | bytes 41476
  78.8 126.6 %copy-start.16 = (f32[9,384]{1,0:T(8,128)S(1)}, f32[9,384]{1,0:T(8,128)}, u32[]{:S(2)}) copy-start(f32[9,384]{1,0:T(8,128)} %args_29_.1) | copy-start | bytes 41476
  78.8 126.6 %copy-start.20 = (f32[9,384]{1,0:T(8,128)S(1)}, f32[9,384]{1,0:T(8,128)}, u32[]{:S(2)}) copy-start(f32[9,384]{1,0:T(8,128)} %param.50) | copy-start | bytes 41476
  78.8 128.0 %copy-start.12 = (f32[1,64,6,192]{3,1,2,0:T(8,128)S(1)}, f32[1,64,6,192]{3,1,2,0:T(8,128)}, u32[]{:S(2)}) copy-start(f32[1,64,6,192]{3,1,2,0:T(8,128)} %param.39) | copy-start | bytes 884740
  78.8 128.0 %copy-start.13 = (f32[1,64,6,192]{3,1,2,0:T(8,128)S(1)}, f32[1,64,6,192]{3,1,2,0:T(8,128)}, u32[]{:S(2)}) copy-start(f32[1,64,6,192]{3,1,2,0:T(8,128)} %param.44) | copy-start | bytes 884740
  200.8 8.1 %copy-start.6 = (f32[64,6,192]{2,0,1:T(8,128)S(1)}, f32[64,6,192]{2,0,1:T(8,128)}, u32[]{:S(2)}) copy-start(f32[64,6,192]{2,0,1:T(8,128)} %param.34) | copy-start | bytes 884740
  200.9 8.1 %copy-start.15 = (f32[64,6,192]{2,0,1:T(8,128)S(1)}, f32[64,6,192]{2,0,1:T(8,128)}, u32[]{:S(2)}) copy-start(f32[64,6,192]{2,0,1:T(8,128)} %param.49) | copy-start | bytes 884740
  200.9 8.1 %copy-start.17 = (bf16[6,64,192]{2,1,0:T(8,128)(2,1)S(1)}, bf16[6,64,192]{2,1,0:T(8,128)(2,1)}, u32[]{:S(2)}) copy-start(bf16[6,64,192]{2,1,0:T(8,128)(2,1)} %get-tuple-element.78) | copy-start | bytes 442372
  206.8 3.3 %copy-start.4 = (f32[1,5,192,384]{3,2,1,0:T(8,128)S(1)}, f32[1,5,192,384]{3,2,1,0:T(8,128)}, u32[]{:S(2)}) copy-start(f32[1,5,192,384]{3,2,1,0:T(8,128)} %param.38) | copy-start | bytes 4423684
  206.8 3.3 %copy-start.5 = (f32[1,5,192,384]{3,2,1,0:T(8,128)S(1)}, f32[1,5,192,384]{3,2,1,0:T(8,128)}, u32[]{:S(2)}) copy-start(f32[1,5,192,384]{3,2,1,0:T(8,128)} %param.43) | copy-start | bytes 4423684
  209.0 4.9 %copy-start.7 = (f32[12,192,384]{2,1,0:T(8,128)S(1)}, f32[12,192,384]{2,1,0:T(8,128)}, u32[]{:S(2)}) copy-start(f32[12,192,384]{2,1,0:T(8,128)} %get-tuple-element.73) | copy-start | bytes 10616836
  210.1 3.8 %copy-start.2 = (f32[1,384,7,192]{1,3,2,0:T(8,128)S(1)}, f32[1,384,7,192]{1,3,2,0:T(8,128)}, u32[]{:S(2)}) copy-start(f32[1,384,7,192]{1,3,2,0:T(8,128)} %param.37) | copy-start | bytes 6193156
  210.1 3.8 %copy-start.3 = (f32[1,384,7,192]{1,3,2,0:T(8,128)S(1)}, f32[1,384,7,192]{1,3,2,0:T(8,128)}, u32[]{:S(2)}) copy-start(f32[1,384,7,192]{1,3,2,0:T(8,128)} %param.42) | copy-start | bytes 6193156
  213.9 2.7 %copy-start.1 = (f32[5,192,384]{2,1,0:T(8,128)S(1)}, f32[5,192,384]{2,1,0:T(8,128)}, u32[]{:S(2)}) copy-start(f32[5,192,384]{2,1,0:T(8,128)} %args_21_.4) | copy-start | bytes 4423684
  213.9 2.7 %copy-start.11 = (bf16[12,192,384]{2,1,0:T(8,128)(2,1)S(1)}, bf16[12,192,384]{2,1,0:T(8,128)(2,1)}, u32[]{:S(2)}) copy-start(bf16[12,192,384]{2,1,0:T(8,128)(2,1)} %get-tuple-element.77) | copy-start | bytes 5308420
  214.0 3.8 %copy-start.14 = (f32[5,192,384]{2,1,0:T(8,128)S(1)}, f32[5,192,384]{2,1,0:T(8,128)}, u32[]{:S(2)}) copy-start(f32[5,192,384]{2,1,0:T(8,128)} %param.48) | copy-start | bytes 4423684
  217.8 2.6 %copy-start = (f32[384,7,192]{0,2,1:T(8,128)S(1)}, f32[384,7,192]{0,2,1:T(8,128)}, u32[]{:S(2)}) copy-start(f32[384,7,192]{0,2,1:T(8,128)} %param.32) | copy-start | bytes 6193156
  217.8 3.8 %copy-start.10 = (f32[384,7,192]{0,2,1:T(8,128)S(1)}, f32[384,7,192]{0,2,1:T(8,128)}, u32[]{:S(2)}) copy-start(f32[384,7,192]{0,2,1:T(8,128)} %param.47) | copy-start | bytes 6193156
  221.6 3.4 %copy-start.9 = (bf16[2,1024,768]{2,1,0:T(8,128)(2,1)S(1)}, bf16[2,1024,768]{2,1,0:T(8,128)(2,1)}, u32[]{:S(2)}) copy-start(bf16[2,1024,768]{2,1,0:T(8,128)(2,1)} %get-tuple-element.72) | copy-start | bytes 9437188
  224.9 3.2 %copy-start.8 = (bf16[2,1024,768]{2,1,0:T(8,128)(2,1)S(1)}, bf16[2,1024,768]{2,1,0:T(8,128)(2,1)}, u32[]{:S(2)}) copy-start(bf16[2,1024,768]{2,1,0:T(8,128)(2,1)} %get-tuple-element.162) | copy-start | bytes 9437188

commit v4 on v3

--- a/solution.py
+++ b/solution.py
@@ -168,7 +168,7 @@
         k = min(kind, 2)
         return remote(ref, ref, R.wsend.at[k, a], R.wrecv.at[k, a], dev)
 
-    ahead = 2
+    ahead = 3
 
     def launch(a):
         hop(0, a).start()
@@ -303,13 +303,15 @@
         values = nt(R.weights[2], low).astype(bf16)
         R.v_t[:, r] = values
         R.v_r[r] = values.T
+        if direct:
+            @pl.when(lax.rem(i, 2) == 1)
+            def _():
+                pass_on(3 + i // 2)
 
     emit(R.q_t, R.q_out)
     emit(R.k_t, R.k_out)
     emit(R.v_r, R.v_out)
 
-    if direct:
-        pass_on(3)
     heads = R.probs.shape[0]
 
     @pl.loop(0, heads)
@@ -325,9 +327,9 @@
         R.inv_out[h] = inverse
         R.o_t[one, :] = (nn(R.v_t[one, :], low) * inverse).astype(bf16)
         if direct:
-            @pl.when(lax.rem(h, 2) == 0)
+            @pl.when(lax.rem(h, 2) == 1)
             def _():
-                pass_on(4 + h // 2)
+                pass_on(5 + h // 2)
 
     for h in range(heads):
         emit(R.probs.at[h], R.probs_out.at[h])
@@ -341,7 +343,7 @@
     away.start()
     R.attn[...] = tn(R.o_t[:, own], R.weights[3])
     if direct:
-        pass_on(7)
+        pass_on(8)
     away.wait()
     small = 128
 
@@ -366,7 +368,7 @@
 
     chunks = 2
     if direct:
-        pass_on(8)
+        pass_on(9)
         for a in range(4, 8):
             arrived(a)
     outs.clear()
@@ -395,7 +397,7 @@
         up(at(c * half + i * step, step))
 
     if direct:
-        pass_on(9)
+        pass_on(10)
     share.wait()
     emit(R.h2, R.h2_out)
     emit(R.cot.at[own], R.gy_out)
@@ -408,13 +410,13 @@
         emit(R.probs.at[k, :, pl.ds(0, width)], R.hidden_out.at[k])
     emit(R.probs.at[4, :, pl.ds(0, width)], R.gm_out)
     if direct:
-        pass_on(10)
+        pass_on(11)
 
     for k in range(4):
         where = pl.ds((k % 2) * slot_rows, slot_rows)
         R.gd[k] = tn(R.probs[k // 2, :, where], R.probs[4, :, 0:width]).astype(bf16)
         if k == 1 and direct:
-            pass_on(11)
+            pass
     emit(R.gd, R.gd_out)
     if direct:
         for a in range(8, 12):
@@ -512,7 +514,7 @@
         in_specs=list(ins.values()),
         out_specs=tuple(o[1] for o in outs.values()),
         scratch_shapes=list(scratch.values()),
-        compiler_params=pltpu.CompilerParams(collective_id=0, has_side_effects=True, vmem_limit_bytes=60 * MIB),
+        compiler_params=pltpu.CompilerParams(collective_id=0, has_side_effects=True, vmem_limit_bytes=61 * MIB),
         name="forward",
     )(*first, tokens, flags, cotangent, cosine, sine)
     return SimpleNamespace(**dict(zip(outs, results)))
@@ -610,7 +612,7 @@
         return remote(R.send_b.at[a], R.got_b.at[a], R.bsem.at[0, a], R.bsem.at[1, a], across)
 
     def state_load(a, run):
-        slot = lax.rem(a, 3)
+        slot = lax.rem(a, 4)
         for low, high, refs, base in (
             (0, 4, (R.wb, R.mb, R.vb), 1), (4, 8, (R.wi, R.mi, R.vi), 3), (8, 9, (R.wb, R.mb, R.vb), 0), (9, 12, (R.wi, R.mi, R.vi), 0)):
             @pl.when(jnp.logical_and(a >= low, a < high))
@@ -632,7 +634,7 @@
         return remote(ref, ref, R.fsem.at[0, a, kind], R.fsem.at[1, a, kind], dev)
 
     def sum_copy(a):
-        return pltpu.make_async_copy(R.sum_ring.at[lax.rem(a, 3)], R.gsum.at[order(a)], R.sum_sem.at[lax.rem(a, 3)])
+        return pltpu.make_async_copy(R.sum_ring.at[lax.rem(a, 2)], R.gsum.at[order(a)], R.sum_sem.at[lax.rem(a, 2)])
 
     def stage_b(a):
         first_hop(a).wait_recv()
@@ -650,16 +652,16 @@
         second_hop(a).wait_recv()
         here = at(s * rows, rows, 16)
         gradient = R.weights[place(a), here, at(d * cols, cols)].astype(f32) + R.got_a[a, here].astype(f32) + R.got_b[a].astype(f32)
-        ring = lax.rem(a, 3)
-
-        @pl.when(a >= 3)
+        ring = lax.rem(a, 2)
+
+        @pl.when(a >= 2)
         def _():
-            sum_copy(a - 3).wait()
+            sum_copy(a - 2).wait()
 
         R.sum_ring[ring] = gradient
         sum_copy(a).start()
         state_load(a, lambda cp: cp.wait())
-        slot = lax.rem(a, 3)
+        slot = lax.rem(a, 4)
         first_new, second_new = adam_parts(gradient, R.state[slot, 1], R.state[slot, 2])
         R.diff[a] = adam_diff(R.state[slot, 0], first_new, second_new, rate_matrix, decay_rate).astype(bf16)
 
@@ -684,7 +686,7 @@
 
     def advance(j):
         for stage, lag, only in (
-            (stage_b, 0, None), (stage_c, 2, None), (stage_d, 4, inner), (stage_e, 5, inner), (stage_f, 6, inner)):
+            (stage_b, 0, None), (stage_c, 3, None), (stage_d, 5, inner), (stage_e, 6, inner), (stage_f, 7, inner)):
             a = j - lag
             ok = jnp.logical_and(a >= 0, a < n_slots)
 
@@ -884,6 +886,7 @@
     if direct:
         advance(6)
         advance(7)
+        advance(8)
     for cp in casts:
         cp.wait()
     if direct:
@@ -913,25 +916,25 @@
         def _():
             a_pair.start()
 
-        @pl.loop(8, n_slots + 6)
+        @pl.loop(9, n_slots + 7)
         def _(j):
             advance(j)
 
-            @pl.when(j < 7 + pieces)
+            @pl.when(j < 8 + pieces)
             def _():
-                cross(1, R.grad_out, j - 7).start()
-
-            @pl.when(jnp.logical_and(j >= 10, j < 10 + pieces))
+                cross(1, R.grad_out, j - 8).start()
+
+            @pl.when(jnp.logical_and(j >= 11, j < 11 + pieces))
             def _():
-                pass_piece(1, R.grad_out, j - 10)
-
-            @pl.when(jnp.logical_and(inner, j == 8))
+                pass_piece(1, R.grad_out, j - 11)
+
+            @pl.when(jnp.logical_and(inner, j == 9))
             def _():
                 a_pair.wait_recv()
                 R.ada_p[...] = (R.ada_p[...].astype(f32) + R.ada_low[...].astype(f32)).astype(bf16)
                 a_half.start()
 
-            @pl.when(jnp.logical_and(inner, j == 9))
+            @pl.when(jnp.logical_and(inner, j == 10))
             def _():
                 a_half.wait()
                 mine_rows = pl.ds(mine * a_rows, a_rows)
@@ -939,7 +942,7 @@
                 a_mid.start()
                 a_out.start()
 
-            @pl.when(jnp.logical_and(inner, j == 10))
+            @pl.when(jnp.logical_and(inner, j == 11))
             def _():
                 a_mid.wait()
                 a_pass.start()
@@ -981,7 +984,7 @@
             cp.wait()
         R.small_total[...] = (R.small_all[0] + R.small_all[1]) + (R.small_all[2] + R.small_all[3])
         R.bias_total[...] = (R.bias_all[0] + R.bias_all[1]) + (R.bias_all[2] + R.bias_all[3])
-        for a in range(n_slots - 3, n_slots):
+        for a in range(n_slots - 2, n_slots):
             sum_copy(a).wait()
     else:
         R.grads[...] = R.weights[4:8]
@@ -1114,11 +1117,11 @@
         )
         scratch |= dict(
             shared=vm((n_tp, spans, 16, width), f32),
-            sum_ring=vm((3, rows, cols), f32),
+            sum_ring=vm((2, rows, cols), f32),
             got_a=vm((12, slot_rows, cols), bf16),
             send_b=vm(slot, bf16),
             got_b=vm(slot, bf16),
-            state=vm((3, 3, rows, cols), f32),
+            state=vm((4, 3, rows, cols), f32),
             diff=vm(slot, bf16),
             got_p=vm(slot, bf16),
             got_h=vm((12, rows // 2, cols), bf16),
@@ -1133,8 +1136,8 @@
             small_all=vm((4,) + ps.shape, f32),
             bias_all=vm((4,) + bu.shape, f32),
             gd_sem=dma,
-            sum_sem=dma((3,)),
-            state_sem=dma((3, 3)),
+            sum_sem=dma((2,)),
+            state_sem=dma((4, 3)),
             asem=dma((2, 12)),
             bsem=dma((2, 12)),
             psem=dma((2, 12)),
@@ -1156,7 +1159,7 @@
         in_specs=[i[1] for i in ins.values()],
         out_specs=tuple(o[1] for o in outs.values()),
         scratch_shapes=list(scratch.values()),
-        compiler_params=pltpu.CompilerParams(collective_id=1, has_side_effects=True, vmem_limit_bytes=60 * MIB),
+        compiler_params=pltpu.CompilerParams(collective_id=1, has_side_effects=True, vmem_limit_bytes=61 * MIB),
         name="backward",
     )(*[i[0] for i in ins.values()])
     return SimpleNamespace(**dict(zip(outs, results)))

time: 230 us -> 223 us (0.970)
  Pallas kernels: 199 us -> 192 us
    pallas_call x1, Pallas kernels: 122 us -> 117 us  [backward(): pl.pallas_call(functools.partial(backward_kernel, direct, cores, n_tp, na...]
where the time goes in v4:
time: 223 us
  Pallas kernels  192 us (86%)
  other arithmetic  23.6 us (11%)
  local copies, waits for them, and re-layouts  6.63 us (3%)
    pallas_call x1, Pallas kernels, backward(): pl.pallas_call(functools.partial(backward_kernel, direct, cores, n_tp, na...  117 us
    pallas_call x1, Pallas kernels, forward(): pl.pallas_call(functools.partial(forward_kernel, direct, cores, n_tp, nam...  75.3 us
    unnamed x54, local copies, waits for them, and re-layouts  6.63 us
    sub x3, other arithmetic, outer(): weight - outer_rate * (diff + outer_mu * moment_new)  5.26 us

profile of v4, /device:TPU:0, one launch (start us, length us, event | category | flops | bytes accessed | tf_op | source)
XLA Modules:
  0.0 223.0 jit_solution(6505157938710103059)
XLA Ops:
  0.7 1.3 copy_bitcast_fusion
  2.0 75.3 %forward.1 = (bf16[1024,768]{1,0:T(8,128)(2,1)}, bf16[12,384,768]{2,1,0:T(8,128)(2,1)}, bf16[384,1024]{1,0:T(8,128)(2,1)}, bf16[384,1024]{1,0:T(8,128)(2,1)}, bf...) custom-call(s32[2]{0:T(128)} %args_0_.4, ...), custom_call_target="tpu_custom_call" | custom-call | tf_op jit(solution)/shard_map/forward/pallas_call | solution.py:511
  77.3 0.0 copy-start.22
  77.3 0.0 copy-start.23
  77.3 0.0 copy-start.21
  77.3 0.0 copy-start.24
  77.3 0.0 copy-start.18
  77.3 0.0 copy-start.19
  77.3 0.0 copy-start.16
  77.4 0.0 copy-start.20
  77.4 0.0 copy-start.12
  77.4 0.0 copy-start.13
  77.4 116.6 %backward.1 = (bf16[2,1024,768]{2,1,0:T(8,128)(2,1)}, bf16[2,1024,768]{2,1,0:T(8,128)(2,1)}, f32[12,192,384]{2,1,0:T(8,128)}, bf16[12,192,384]{2,1,0:T(8,128)(2,...) custom-call(bf16[12,384,768]{2,1,0:T(8,128)(2,1)} %get-tuple-element, ...), custom_call_target="tpu_custom_call" | custom-call | tf_op jit(solution)/shard_map/backward/pallas_call | solution.py:1156
  194.1 0.0 copy-start.6
  194.1 0.0 copy-start.15
  194.1 0.0 copy-start.17
  194.1 0.0 copy-done.22
  194.1 0.0 copy-done.23
  194.1 1.3 fusion.13
  195.4 0.0 copy-done.21
  195.4 0.0 copy-done.24
  195.4 1.3 multiply_subtract_fusion.2
  196.7 0.0 copy-done.18
  196.7 0.0 copy-done.19
  196.7 0.7 fusion.11
  197.4 0.6 copy.55
  198.0 0.6 copy.54
  198.6 0.0 copy-done.16
  198.6 0.0 copy-done.20
  198.7 1.4 multiply_subtract_fusion.1
  200.0 0.0 copy-done.12
  200.0 0.0 copy-done.13
  200.0 0.0 copy-start.4
  200.0 0.0 copy-start.5
  200.0 2.1 fusion.7
  202.2 0.0 copy-done.6
  202.2 0.0 copy-done.15
  202.2 0.0 copy-done.17
  202.2 0.0 copy-start.7
  202.2 1.1 fusion.9
  203.3 0.0 copy-done.4
  203.3 0.0 copy-done.5
  203.3 0.0 copy-start.3
  203.4 3.8 %fusion.5 = (f32[1,5,192,384]{3,2,1,0:T(8,128)}, f32[1,5,192,384]{3,2,1,0:T(8,128)}) fusion(f32[12,192,384]{2,1,0:T(8,128)} %get-tuple-element.73, f32[1,5,192,384]{3,2,1,0:T(8,128)S(1)} %copy-done.5, f32[1,5,192,384]{3,2,1,0:T(8,128)S(1)} %copy-done.4), kind=kLoop, calls=%fused_computation.11 | loop fusion | flops 2580480 | bytes 7372800 | tf_op jit(solution)/shard_map/broadcast_in_dim | solution.py:1288
  207.1 0.0 copy-done.7
  207.1 0.0 copy-done.2
  207.1 0.0 copy-done.3
  207.1 0.0 copy-start.1
  207.1 0.0 copy-start.11
  207.2 0.0 copy-start.14
  207.2 2.7 %fusion.1 = (f32[1,384,7,192]{1,3,2,0:T(8,128)}, f32[1,384,7,192]{1,3,2,0:T(8,128)}) fusion(f32[12,192,384]{2,1,0:T(8,128)S(1)} %copy-done.7, f32[1,384,7,192]{1,3,2,0:T(8,128)S(1)} %copy-done.3, f32[1,384,7,192]{1,3,2,0:T(8,128)S(1)} %copy-done.2), kind=kLoop, calls=%fused_computation.3 | loop fusion | flops 3612672 | bytes 10321920 | tf_op jit(solution)/shard_map/broadcast_in_dim | solution.py:1288
  209.9 0.0 copy-done.1
  209.9 0.0 copy-done.11
  209.9 1.1 copy-done.14
  211.0 0.0 copy-start
  211.0 0.0 copy-start.10
  211.0 2.6 %multiply_subtract_fusion = (f32[5,192,384]{2,1,0:T(8,128)}, f32[5,192,384]{2,1,0:T(8,128)}, f32[5,192,384]{2,1,0:T(8,128)}) fusion(f32[5,192,384]{2,1,0:T(8,128)S(1)} %copy-done.1, f32[5,192,384]{2,1,0:T(8,128)S(1)} %copy-done.14, bf16[12,192,384]{2,1,0:T(8,128)(2,1)S(1)} %copy-done.11), kind=kLoop, calls=%fused_computation.12 | loop fusion | flops 2949120 | bytes 8110080 | tf_op jit(solution)/shard_map/sub | solution.py:1272
  213.6 0.0 copy-done
  213.6 1.2 copy-done.10
  214.8 3.4 %fusion.3 = (f32[384,7,192]{0,2,1:T(8,128)}, f32[384,7,192]{0,2,1:T(8,128)}, f32[384,7,192]{0,2,1:T(8,128)}) fusion(f32[384,7,192]{0,2,1:T(8,128)S(1)} %copy-done.10, bf16[12,192,384]{2,1,0:T(8,128)(2,1)S(1)} %copy-done.11, f32[384,7,192]{0,2,1:T(8,128)S(1)} %copy-done), kind=kLoop, calls=%fused_computation.9 | loop fusion | flops 4128768 | bytes 11354112 | tf_op jit(solution)/shard_map/transpose | solution.py:1275
  218.1 0.0 copy-done.9
  218.1 3.2 %convert_element_type.12 = f32[2,1024,768]{2,1,0:T(8,128)} convert(bf16[2,1024,768]{2,1,0:T(8,128)(2,1)S(1)} %copy-done.9) | non-fusion elementwise | flops 1572864 | bytes 9437184 | tf_op jit(solution)/shard_map/convert_element_type | solution.py:1228
  221.3 0.0 copy-done.8
  221.3 1.7 copy.65
  (3 shorter events, 0.0 us)
Async XLA Ops:
  77.3 116.8 %copy-start.22 = (f32[1,4,96]{2,1,0:T(4,128)S(1)}, f32[1,4,96]{2,1,0:T(4,128)}, u32[]{:S(2)}) copy-start(f32[1,4,96]{2,1,0:T(4,128)} %param.41) | copy-start | bytes 4612
  77.3 116.8 %copy-start.23 = (f32[1,4,96]{2,1,0:T(4,128)S(1)}, f32[1,4,96]{2,1,0:T(4,128)}, u32[]{:S(2)}) copy-start(f32[1,4,96]{2,1,0:T(4,128)} %param.46) | copy-start | bytes 4612
  77.3 118.1 %copy-start.21 = (f32[4,96]{1,0:T(4,128)S(1)}, f32[4,96]{1,0:T(4,128)}, u32[]{:S(2)}) copy-start(f32[4,96]{1,0:T(4,128)} %args_32_.1) | copy-start | bytes 4612
  77.3 118.1 %copy-start.24 = (f32[4,96]{1,0:T(4,128)S(1)}, f32[4,96]{1,0:T(4,128)}, u32[]{:S(2)}) copy-start(f32[4,96]{1,0:T(4,128)} %param.51) | copy-start | bytes 4612
  77.3 119.3 %copy-start.18 = (f32[1,9,384]{2,0,1:T(1,128)S(1)}, f32[1,9,384]{2,0,1:T(1,128)}, u32[]{:S(2)}) copy-start(f32[1,9,384]{2,0,1:T(1,128)} %param.45) | copy-start | bytes 41476
  77.3 119.3 %copy-start.19 = (f32[1,9,384]{2,0,1:T(1,128)S(1)}, f32[1,9,384]{2,0,1:T(1,128)}, u32[]{:S(2)}) copy-start(f32[1,9,384]{2,0,1:T(1,128)} %param.40) | copy-start | bytes 41476
  77.3 121.3 %copy-start.16 = (f32[9,384]{1,0:T(8,128)S(1)}, f32[9,384]{1,0:T(8,128)}, u32[]{:S(2)}) copy-start(f32[9,384]{1,0:T(8,128)} %args_29_.1) | copy-start | bytes 41476
  77.4 121.3 %copy-start.20 = (f32[9,384]{1,0:T(8,128)S(1)}, f32[9,384]{1,0:T(8,128)}, u32[]{:S(2)}) copy-start(f32[9,384]{1,0:T(8,128)} %param.50) | copy-start | bytes 41476
  77.4 122.6 %copy-start.12 = (f32[1,64,6,192]{3,1,2,0:T(8,128)S(1)}, f32[1,64,6,192]{3,1,2,0:T(8,128)}, u32[]{:S(2)}) copy-start(f32[1,64,6,192]{3,1,2,0:T(8,128)} %param.39) | copy-start | bytes 884740
  77.4 122.6 %copy-start.13 = (f32[1,64,6,192]{3,1,2,0:T(8,128)S(1)}, f32[1,64,6,192]{3,1,2,0:T(8,128)}, u32[]{:S(2)}) copy-start(f32[1,64,6,192]{3,1,2,0:T(8,128)} %param.44) | copy-start | bytes 884740
  194.1 8.1 %copy-start.6 = (f32[64,6,192]{2,0,1:T(8,128)S(1)}, f32[64,6,192]{2,0,1:T(8,128)}, u32[]{:S(2)}) copy-start(f32[64,6,192]{2,0,1:T(8,128)} %param.34) | copy-start | bytes 884740
  194.1 8.1 %copy-start.15 = (f32[64,6,192]{2,0,1:T(8,128)S(1)}, f32[64,6,192]{2,0,1:T(8,128)}, u32[]{:S(2)}) copy-start(f32[64,6,192]{2,0,1:T(8,128)} %param.49) | copy-start | bytes 884740
  194.1 8.1 %copy-start.17 = (bf16[6,64,192]{2,1,0:T(8,128)(2,1)S(1)}, bf16[6,64,192]{2,1,0:T(8,128)(2,1)}, u32[]{:S(2)}) copy-start(bf16[6,64,192]{2,1,0:T(8,128)(2,1)} %get-tuple-element.78) | copy-start | bytes 442372
  200.0 3.3 %copy-start.4 = (f32[1,5,192,384]{3,2,1,0:T(8,128)S(1)}, f32[1,5,192,384]{3,2,1,0:T(8,128)}, u32[]{:S(2)}) copy-start(f32[1,5,192,384]{3,2,1,0:T(8,128)} %param.38) | copy-start | bytes 4423684
  200.0 3.3 %copy-start.5 = (f32[1,5,192,384]{3,2,1,0:T(8,128)S(1)}, f32[1,5,192,384]{3,2,1,0:T(8,128)}, u32[]{:S(2)}) copy-start(f32[1,5,192,384]{3,2,1,0:T(8,128)} %param.43) | copy-start | bytes 4423684
  202.2 4.9 %copy-start.7 = (f32[12,192,384]{2,1,0:T(8,128)S(1)}, f32[12,192,384]{2,1,0:T(8,128)}, u32[]{:S(2)}) copy-start(f32[12,192,384]{2,1,0:T(8,128)} %get-tuple-element.73) | copy-start | bytes 10616836
  203.3 3.8 %copy-start.2 = (f32[1,384,7,192]{1,3,2,0:T(8,128)S(1)}, f32[1,384,7,192]{1,3,2,0:T(8,128)}, u32[]{:S(2)}) copy-start(f32[1,384,7,192]{1,3,2,0:T(8,128)} %param.37) | copy-start | bytes 6193156
  203.3 3.8 %copy-start.3 = (f32[1,384,7,192]{1,3,2,0:T(8,128)S(1)}, f32[1,384,7,192]{1,3,2,0:T(8,128)}, u32[]{:S(2)}) copy-start(f32[1,384,7,192]{1,3,2,0:T(8,128)} %param.42) | copy-start | bytes 6193156
  207.1 2.7 %copy-start.1 = (f32[5,192,384]{2,1,0:T(8,128)S(1)}, f32[5,192,384]{2,1,0:T(8,128)}, u32[]{:S(2)}) copy-start(f32[5,192,384]{2,1,0:T(8,128)} %args_21_.4) | copy-start | bytes 4423684
  207.1 2.7 %copy-start.11 = (bf16[12,192,384]{2,1,0:T(8,128)(2,1)S(1)}, bf16[12,192,384]{2,1,0:T(8,128)(2,1)}, u32[]{:S(2)}) copy-start(bf16[12,192,384]{2,1,0:T(8,128)(2,1)} %get-tuple-element.77) | copy-start | bytes 5308420
  207.2 3.8 %copy-start.14 = (f32[5,192,384]{2,1,0:T(8,128)S(1)}, f32[5,192,384]{2,1,0:T(8,128)}, u32[]{:S(2)}) copy-start(f32[5,192,384]{2,1,0:T(8,128)} %param.48) | copy-start | bytes 4423684
  211.0 2.6 %copy-start = (f32[384,7,192]{0,2,1:T(8,128)S(1)}, f32[384,7,192]{0,2,1:T(8,128)}, u32[]{:S(2)}) copy-start(f32[384,7,192]{0,2,1:T(8,128)} %param.32) | copy-start | bytes 6193156
  211.0 3.8 %copy-start.10 = (f32[384,7,192]{0,2,1:T(8,128)S(1)}, f32[384,7,192]{0,2,1:T(8,128)}, u32[]{:S(2)}) copy-start(f32[384,7,192]{0,2,1:T(8,128)} %param.47) | copy-start | bytes 6193156
  214.8 3.4 %copy-start.9 = (bf16[2,1024,768]{2,1,0:T(8,128)(2,1)S(1)}, bf16[2,1024,768]{2,1,0:T(8,128)(2,1)}, u32[]{:S(2)}) copy-start(bf16[2,1024,768]{2,1,0:T(8,128)(2,1)} %get-tuple-element.72) | copy-start | bytes 9437188
  218.1 3.2 %copy-start.8 = (bf16[2,1024,768]{2,1,0:T(8,128)(2,1)S(1)}, bf16[2,1024,768]{2,1,0:T(8,128)(2,1)}, u32[]{:S(2)}) copy-start(bf16[2,1024,768]{2,1,0:T(8,128)(2,1)} %get-tuple-element.162) | copy-start | bytes 9437188

commit v5 on v4

--- a/solution.py
+++ b/solution.py
@@ -686,7 +686,7 @@
 
     def advance(j):
         for stage, lag, only in (
-            (stage_b, 0, None), (stage_c, 3, None), (stage_d, 5, inner), (stage_e, 6, inner), (stage_f, 7, inner)):
+            (stage_b, 0, None), (stage_c, 3, None), (stage_d, 4, inner), (stage_e, 5, inner), (stage_f, 6, inner)):
             a = j - lag
             ok = jnp.logical_and(a >= 0, a < n_slots)
 
@@ -916,7 +916,7 @@
         def _():
             a_pair.start()
 
-        @pl.loop(9, n_slots + 7)
+        @pl.loop(9, n_slots + 6)
         def _(j):
             advance(j)
 

time: 223 us -> 222 us (level)
  no operation moved by 1% of the time
where the time goes in v5:
time: 222 us
  Pallas kernels  191 us (86%)
  other arithmetic  23.6 us (11%)
  local copies, waits for them, and re-layouts  6.63 us (3%)
    pallas_call x1, Pallas kernels, backward(): pl.pallas_call(functools.partial(backward_kernel, direct, cores, n_tp, na...  115 us
    pallas_call x1, Pallas kernels, forward(): pl.pallas_call(functools.partial(forward_kernel, direct, cores, n_tp, nam...  75.3 us
    unnamed x54, local copies, waits for them, and re-layouts  6.63 us
    sub x3, other arithmetic, outer(): weight - outer_rate * (diff + outer_mu * moment_new)  5.26 us

profile of v5, /device:TPU:0, one launch (start us, length us, event | category | flops | bytes accessed | tf_op | source)
XLA Modules:
  0.0 221.8 jit_solution(1944796328336527460)
XLA Ops:
  0.7 1.3 copy_bitcast_fusion
  2.0 75.3 %forward.1 = (bf16[1024,768]{1,0:T(8,128)(2,1)}, bf16[12,384,768]{2,1,0:T(8,128)(2,1)}, bf16[384,1024]{1,0:T(8,128)(2,1)}, bf16[384,1024]{1,0:T(8,128)(2,1)}, bf...) custom-call(s32[2]{0:T(128)} %args_0_.4, ...), custom_call_target="tpu_custom_call" | custom-call | tf_op jit(solution)/shard_map/forward/pallas_call | solution.py:511
  77.3 0.0 copy-start.22
  77.3 0.0 copy-start.23
  77.3 0.0 copy-start.21
  77.3 0.0 copy-start.24
  77.3 0.0 copy-start.18
  77.3 0.0 copy-start.19
  77.3 0.0 copy-start.16
  77.4 0.0 copy-start.20
  77.4 0.0 copy-start.12
  77.4 0.0 copy-start.13
  77.4 115.4 %backward.1 = (bf16[2,1024,768]{2,1,0:T(8,128)(2,1)}, bf16[2,1024,768]{2,1,0:T(8,128)(2,1)}, f32[12,192,384]{2,1,0:T(8,128)}, bf16[12,192,384]{2,1,0:T(8,128)(2,...) custom-call(bf16[12,384,768]{2,1,0:T(8,128)(2,1)} %get-tuple-element, ...), custom_call_target="tpu_custom_call" | custom-call | tf_op jit(solution)/shard_map/backward/pallas_call | solution.py:1156
  192.8 0.0 copy-start.6
  192.9 0.0 copy-start.15
  192.9 0.0 copy-start.17
  192.9 0.0 copy-done.22
  192.9 0.0 copy-done.23
  192.9 1.3 fusion.13
  194.2 0.0 copy-done.21
  194.2 0.0 copy-done.24
  194.2 1.3 multiply_subtract_fusion.2
  195.5 0.0 copy-done.18
  195.5 0.0 copy-done.19
  195.5 0.7 fusion.11
  196.2 0.6 copy.55
  196.8 0.6 copy.54
  197.4 0.0 copy-done.16
  197.4 0.0 copy-done.20
  197.5 1.4 multiply_subtract_fusion.1
  198.8 0.0 copy-done.12
  198.8 0.0 copy-done.13
  198.8 0.0 copy-start.4
  198.8 0.0 copy-start.5
  198.8 2.1 fusion.7
  201.0 0.0 copy-done.6
  201.0 0.0 copy-done.15
  201.0 0.0 copy-done.17
  201.0 0.0 copy-start.7
  201.0 1.1 fusion.9
  202.1 0.0 copy-done.4
  202.1 0.0 copy-done.5
  202.1 0.0 copy-start.2
  202.1 0.0 copy-start.3
  202.2 3.8 %fusion.5 = (f32[1,5,192,384]{3,2,1,0:T(8,128)}, f32[1,5,192,384]{3,2,1,0:T(8,128)}) fusion(f32[12,192,384]{2,1,0:T(8,128)} %get-tuple-element.73, f32[1,5,192,384]{3,2,1,0:T(8,128)S(1)} %copy-done.5, f32[1,5,192,384]{3,2,1,0:T(8,128)S(1)} %copy-done.4), kind=kLoop, calls=%fused_computation.11 | loop fusion | flops 2580480 | bytes 7372800 | tf_op jit(solution)/shard_map/broadcast_in_dim | solution.py:1288
  205.9 0.0 copy-done.7
  205.9 0.0 copy-done.2
  205.9 0.0 copy-done.3
  205.9 0.0 copy-start.1
  205.9 0.0 copy-start.11
  206.0 0.0 copy-start.14
  206.0 2.7 %fusion.1 = (f32[1,384,7,192]{1,3,2,0:T(8,128)}, f32[1,384,7,192]{1,3,2,0:T(8,128)}) fusion(f32[12,192,384]{2,1,0:T(8,128)S(1)} %copy-done.7, f32[1,384,7,192]{1,3,2,0:T(8,128)S(1)} %copy-done.3, f32[1,384,7,192]{1,3,2,0:T(8,128)S(1)} %copy-done.2), kind=kLoop, calls=%fused_computation.3 | loop fusion | flops 3612672 | bytes 10321920 | tf_op jit(solution)/shard_map/broadcast_in_dim | solution.py:1288
  208.7 0.0 copy-done.1
  208.7 0.0 copy-done.11
  208.7 1.1 copy-done.14
  209.8 0.0 copy-start
  209.8 2.6 %multiply_subtract_fusion = (f32[5,192,384]{2,1,0:T(8,128)}, f32[5,192,384]{2,1,0:T(8,128)}, f32[5,192,384]{2,1,0:T(8,128)}) fusion(f32[5,192,384]{2,1,0:T(8,128)S(1)} %copy-done.1, f32[5,192,384]{2,1,0:T(8,128)S(1)} %copy-done.14, bf16[12,192,384]{2,1,0:T(8,128)(2,1)S(1)} %copy-done.11), kind=kLoop, calls=%fused_computation.12 | loop fusion | flops 2949120 | bytes 8110080 | tf_op jit(solution)/shard_map/sub | solution.py:1272
  212.4 0.0 copy-done
  212.4 1.2 copy-done.10
  213.6 3.4 %fusion.3 = (f32[384,7,192]{0,2,1:T(8,128)}, f32[384,7,192]{0,2,1:T(8,128)}, f32[384,7,192]{0,2,1:T(8,128)}) fusion(f32[384,7,192]{0,2,1:T(8,128)S(1)} %copy-done.10, bf16[12,192,384]{2,1,0:T(8,128)(2,1)S(1)} %copy-done.11, f32[384,7,192]{0,2,1:T(8,128)S(1)} %copy-done), kind=kLoop, calls=%fused_computation.9 | loop fusion | flops 4128768 | bytes 11354112 | tf_op jit(solution)/shard_map/transpose | solution.py:1275
  216.9 0.0 copy-done.9
  216.9 3.2 %convert_element_type.12 = f32[2,1024,768]{2,1,0:T(8,128)} convert(bf16[2,1024,768]{2,1,0:T(8,128)(2,1)S(1)} %copy-done.9) | non-fusion elementwise | flops 1572864 | bytes 9437184 | tf_op jit(solution)/shard_map/convert_element_type | solution.py:1228
  220.1 0.0 copy-done.8
  220.1 1.7 copy.65
  (3 shorter events, 0.0 us)
Async XLA Ops:
  77.3 115.6 %copy-start.22 = (f32[1,4,96]{2,1,0:T(4,128)S(1)}, f32[1,4,96]{2,1,0:T(4,128)}, u32[]{:S(2)}) copy-start(f32[1,4,96]{2,1,0:T(4,128)} %param.41) | copy-start | bytes 4612
  77.3 115.6 %copy-start.23 = (f32[1,4,96]{2,1,0:T(4,128)S(1)}, f32[1,4,96]{2,1,0:T(4,128)}, u32[]{:S(2)}) copy-start(f32[1,4,96]{2,1,0:T(4,128)} %param.46) | copy-start | bytes 4612
  77.3 116.9 %copy-start.21 = (f32[4,96]{1,0:T(4,128)S(1)}, f32[4,96]{1,0:T(4,128)}, u32[]{:S(2)}) copy-start(f32[4,96]{1,0:T(4,128)} %args_32_.1) | copy-start | bytes 4612
  77.3 116.9 %copy-start.24 = (f32[4,96]{1,0:T(4,128)S(1)}, f32[4,96]{1,0:T(4,128)}, u32[]{:S(2)}) copy-start(f32[4,96]{1,0:T(4,128)} %param.51) | copy-start | bytes 4612
  77.3 118.1 %copy-start.18 = (f32[1,9,384]{2,0,1:T(1,128)S(1)}, f32[1,9,384]{2,0,1:T(1,128)}, u32[]{:S(2)}) copy-start(f32[1,9,384]{2,0,1:T(1,128)} %param.45) | copy-start | bytes 41476
  77.3 118.1 %copy-start.19 = (f32[1,9,384]{2,0,1:T(1,128)S(1)}, f32[1,9,384]{2,0,1:T(1,128)}, u32[]{:S(2)}) copy-start(f32[1,9,384]{2,0,1:T(1,128)} %param.40) | copy-start | bytes 41476
  77.3 120.1 %copy-start.16 = (f32[9,384]{1,0:T(8,128)S(1)}, f32[9,384]{1,0:T(8,128)}, u32[]{:S(2)}) copy-start(f32[9,384]{1,0:T(8,128)} %args_29_.1) | copy-start | bytes 41476
  77.4 120.1 %copy-start.20 = (f32[9,384]{1,0:T(8,128)S(1)}, f32[9,384]{1,0:T(8,128)}, u32[]{:S(2)}) copy-start(f32[9,384]{1,0:T(8,128)} %param.50) | copy-start | bytes 41476
  77.4 121.4 %copy-start.12 = (f32[1,64,6,192]{3,1,2,0:T(8,128)S(1)}, f32[1,64,6,192]{3,1,2,0:T(8,128)}, u32[]{:S(2)}) copy-start(f32[1,64,6,192]{3,1,2,0:T(8,128)} %param.39) | copy-start | bytes 884740
  77.4 121.4 %copy-start.13 = (f32[1,64,6,192]{3,1,2,0:T(8,128)S(1)}, f32[1,64,6,192]{3,1,2,0:T(8,128)}, u32[]{:S(2)}) copy-start(f32[1,64,6,192]{3,1,2,0:T(8,128)} %param.44) | copy-start | bytes 884740
  192.8 8.1 %copy-start.6 = (f32[64,6,192]{2,0,1:T(8,128)S(1)}, f32[64,6,192]{2,0,1:T(8,128)}, u32[]{:S(2)}) copy-start(f32[64,6,192]{2,0,1:T(8,128)} %param.34) | copy-start | bytes 884740
  192.9 8.1 %copy-start.15 = (f32[64,6,192]{2,0,1:T(8,128)S(1)}, f32[64,6,192]{2,0,1:T(8,128)}, u32[]{:S(2)}) copy-start(f32[64,6,192]{2,0,1:T(8,128)} %param.49) | copy-start | bytes 884740
  192.9 8.1 %copy-start.17 = (bf16[6,64,192]{2,1,0:T(8,128)(2,1)S(1)}, bf16[6,64,192]{2,1,0:T(8,128)(2,1)}, u32[]{:S(2)}) copy-start(bf16[6,64,192]{2,1,0:T(8,128)(2,1)} %get-tuple-element.78) | copy-start | bytes 442372
  198.8 3.3 %copy-start.4 = (f32[1,5,192,384]{3,2,1,0:T(8,128)S(1)}, f32[1,5,192,384]{3,2,1,0:T(8,128)}, u32[]{:S(2)}) copy-start(f32[1,5,192,384]{3,2,1,0:T(8,128)} %param.38) | copy-start | bytes 4423684
  198.8 3.3 %copy-start.5 = (f32[1,5,192,384]{3,2,1,0:T(8,128)S(1)}, f32[1,5,192,384]{3,2,1,0:T(8,128)}, u32[]{:S(2)}) copy-start(f32[1,5,192,384]{3,2,1,0:T(8,128)} %param.43) | copy-start | bytes 4423684
  201.0 4.9 %copy-start.7 = (f32[12,192,384]{2,1,0:T(8,128)S(1)}, f32[12,192,384]{2,1,0:T(8,128)}, u32[]{:S(2)}) copy-start(f32[12,192,384]{2,1,0:T(8,128)} %get-tuple-element.73) | copy-start | bytes 10616836
  202.1 3.8 %copy-start.2 = (f32[1,384,7,192]{1,3,2,0:T(8,128)S(1)}, f32[1,384,7,192]{1,3,2,0:T(8,128)}, u32[]{:S(2)}) copy-start(f32[1,384,7,192]{1,3,2,0:T(8,128)} %param.37) | copy-start | bytes 6193156
  202.1 3.8 %copy-start.3 = (f32[1,384,7,192]{1,3,2,0:T(8,128)S(1)}, f32[1,384,7,192]{1,3,2,0:T(8,128)}, u32[]{:S(2)}) copy-start(f32[1,384,7,192]{1,3,2,0:T(8,128)} %param.42) | copy-start | bytes 6193156
  205.9 2.7 %copy-start.1 = (f32[5,192,384]{2,1,0:T(8,128)S(1)}, f32[5,192,384]{2,1,0:T(8,128)}, u32[]{:S(2)}) copy-start(f32[5,192,384]{2,1,0:T(8,128)} %args_21_.4) | copy-start | bytes 4423684
  205.9 2.7 %copy-start.11 = (bf16[12,192,384]{2,1,0:T(8,128)(2,1)S(1)}, bf16[12,192,384]{2,1,0:T(8,128)(2,1)}, u32[]{:S(2)}) copy-start(bf16[12,192,384]{2,1,0:T(8,128)(2,1)} %get-tuple-element.77) | copy-start | bytes 5308420
  206.0 3.8 %copy-start.14 = (f32[5,192,384]{2,1,0:T(8,128)S(1)}, f32[5,192,384]{2,1,0:T(8,128)}, u32[]{:S(2)}) copy-start(f32[5,192,384]{2,1,0:T(8,128)} %param.48) | copy-start | bytes 4423684
  209.8 2.6 %copy-start = (f32[384,7,192]{0,2,1:T(8,128)S(1)}, f32[384,7,192]{0,2,1:T(8,128)}, u32[]{:S(2)}) copy-start(f32[384,7,192]{0,2,1:T(8,128)} %param.32) | copy-start | bytes 6193156
  209.8 3.8 %copy-start.10 = (f32[384,7,192]{0,2,1:T(8,128)S(1)}, f32[384,7,192]{0,2,1:T(8,128)}, u32[]{:S(2)}) copy-start(f32[384,7,192]{0,2,1:T(8,128)} %param.47) | copy-start | bytes 6193156
  213.6 3.4 %copy-start.9 = (bf16[2,1024,768]{2,1,0:T(8,128)(2,1)S(1)}, bf16[2,1024,768]{2,1,0:T(8,128)(2,1)}, u32[]{:S(2)}) copy-start(bf16[2,1024,768]{2,1,0:T(8,128)(2,1)} %get-tuple-element.72) | copy-start | bytes 9437188
  216.9 3.2 %copy-start.8 = (bf16[2,1024,768]{2,1,0:T(8,128)(2,1)S(1)}, bf16[2,1024,768]{2,1,0:T(8,128)(2,1)}, u32[]{:S(2)}) copy-start(bf16[2,1024,768]{2,1,0:T(8,128)(2,1)} %get-tuple-element.162) | copy-start | bytes 9437188
